TPU v7x, 256 devices: a whole 4x4x8 slice. The times are simulated.
256 devices in a mesh: sec: 4 (over x), feat: 16 (over z, core), row: 4 (over y).
Axes of the slice: x: 4, y: 4, z: 8, core: 2. Of those that a mesh axis runs over, the one named last changes fastest.
Arguments:
- inputs: bfloat16 [4, 1024, 2304], P('sec', 'row', 'feat'), may hold values from -6 to 6
- enc_weight: bfloat16 [4, 2304, 16384], P('sec', None, 'feat'), may hold values from -0.125 to 0.125
- enc_bias: float32 [4, 16384], P('sec', 'feat'), may hold values from -0.5 to 0.5
- dec_weight: bfloat16 [4, 4, 16384, 2304], P('sec', None, 'feat', 'row'), may hold values from -0.046875 to 0.046875
- dec_bias: float32 [4, 2304], P('sec', 'row'), may hold values from -3 to 3
Outputs:
- recon: bfloat16 [4, 1024, 2304], P('sec', 'feat', 'row')
All inputs are finite; a program needn't handle non-finite values.
Results may differ from a plain program's by a relative error of at most 0.0047.
Values may be sent and summed in bfloat16 or wider, within the bound.
No kernel may reach another device: no remote copies, remote signals or barrier semaphores. Data moves between devices by JAX's collectives and lax.ppermute only.
A program may use at most 64 MiB of HBM per device.

v0:
```python
import jax
import jax.numpy as jnp
from jax import lax
from jax.experimental import pallas as pl
from jax.experimental.pallas import tpu as pltpu
from jax.sharding import PartitionSpec as P


CHIPS = 8
ROWS = 4
PIECE = 64
VMEM = pl.BlockSpec(memory_space=pltpu.VMEM)
SMEM = pl.BlockSpec(memory_space=pltpu.SMEM)


def ring(shift):
    return [(i, (i + shift) % ROWS) for i in range(ROWS)]


def hop(shift):
    return [(i, ((i // 2 + shift) % CHIPS) * 2 + i % 2) for i in range(2 * CHIPS)]


SWAP = [(i, i ^ 1) for i in range(2 * CHIPS)]
BOTH = [(i, ((i // 2 + (1 if i % 2 == 0 else -1)) % CHIPS) * 2 + i % 2) for i in range(2 * CHIPS)]


def gather_inputs(own, core, chip):
    other = lax.ppermute(own, "feat", SWAP)
    block = jnp.where(core == 0, jnp.concatenate([own, other]), jnp.concatenate([other, own]))
    b1 = lax.ppermute(block, "feat", BOTH)
    b2 = lax.ppermute(b1, "feat", BOTH)
    b3 = lax.ppermute(b2, "feat", BOTH)
    b4 = lax.ppermute(b3, "feat", BOTH)
    s1, s2, s3 = jnp.split(lax.ppermute(jnp.concatenate([b1, b2, b3]), "feat", SWAP), 3)
    sign = 1 - 2 * core
    size = block.shape[0]
    whole = jnp.zeros((CHIPS * size, own.shape[1]), own.dtype)
    for piece, shift in ((block, 0), (b1, -1), (b2, -2), (b3, -3), (b4, -4), (s1, 1), (s2, 2), (s3, 3)):
        at = (chip + sign * shift) & (CHIPS - 1)
        whole = lax.dynamic_update_slice(whole, piece, (at * size, 0))
    return whole


def encode(x, weight, bias):
    hidden = lax.dot_general(x, weight, (((0,), (0,)), ((), ())), preferred_element_type=jnp.float32)
    return jnp.maximum(hidden + bias, 0.0).astype(jnp.bfloat16)


def gather_rows(own):
    half = own.shape[0] // 2
    before = lax.ppermute(own, "row", ring(1))
    after = lax.ppermute(own, "row", ring(-1))
    first = lax.ppermute(before[:half], "row", ring(1))
    second = lax.ppermute(after[half:], "row", ring(-1))
    return own, before, after, first, second


def decode(where, rows, weight, start, split):
    tokens, count = rows[0].shape
    width = weight.shape[0]
    has_start = start is not None

    def kernel(where_ref, own, before, after, first, second, weight_ref, *rest):
        core, chip, row = where_ref[0], where_ref[1], where_ref[2]
        if has_start:
            start_ref, *rest = rest
        if split:
            mine_ref, theirs_ref, turned = rest
        else:
            out_ref, turned = rest
        turned[...] = weight_ref[...].T
        for j, parts in enumerate(((own,), (after,), (first, second), (before,))):
            block = parts[0][...] if len(parts) == 1 else jnp.concatenate([p[...] for p in parts])
            value = jnp.dot(block, turned[...], preferred_element_type=jnp.float32)
            if has_start:
                value = value + start_ref[j]
            if not split:
                out_ref[j] = value
                continue
            for h in range(2):
                at = (2 * ((row + j) & (ROWS - 1)) + h - (chip if split == "relative" else 0)) & (CHIPS - 1)
                low = value[2 * h * PIECE : (2 * h + 1) * PIECE]
                high = value[(2 * h + 1) * PIECE : (2 * h + 2) * PIECE]
                mine_ref[at] = jnp.where(core == 0, low, high)
                theirs_ref[at] = jnp.where(core == 0, high, low).astype(jnp.bfloat16)

    if split:
        shape = (CHIPS, PIECE, width)
        out_shape = (jax.ShapeDtypeStruct(shape, jnp.float32), jax.ShapeDtypeStruct(shape, jnp.bfloat16))
        out_specs = (VMEM, VMEM); out_shape = tuple(pltpu.VMEM(o.shape, o.dtype) for o in out_shape)
    else:
        out_shape = jax.ShapeDtypeStruct((ROWS, tokens, width), jnp.float32)
        out_specs = VMEM; out_shape = pltpu.VMEM(out_shape.shape, out_shape.dtype)
    operands = list(rows) + [weight] + ([start] if has_start else [])
    return pl.pallas_call(
        kernel,
        in_specs=[SMEM] + [VMEM] * len(operands),
        out_specs=out_specs,
        out_shape=out_shape,
        scratch_shapes=[pltpu.VMEM((count, width), jnp.bfloat16)],
        compiler_params=pltpu.CompilerParams(vmem_limit_bytes=12 << 20),
    )(where, *[pltpu.with_memory_space_constraint(o, pltpu.VMEM) for o in operands])


def per_device(inputs, enc_weight, enc_bias, dec_weight, dec_bias):
    decoders = jnp.swapaxes(dec_weight[0], 1, 2)
    sec = lax.axis_index("sec")
    feat = lax.axis_index("feat")
    row = lax.axis_index("row")
    core, chip = feat & 1, feat >> 1

    where = jnp.stack([core, chip, row]).astype(jnp.int32)

    lent = jnp.where(sec == 3, 1, 0)
    lent_a = lax.ppermute(lax.dynamic_index_in_dim(decoders, lent, 0, keepdims=False), "sec", [(2, 0), (3, 1)])
    lent_b = lax.ppermute(decoders[2], "sec", [(3, 2)])

    whole = gather_inputs(inputs[0].T, core, chip)
    features = encode(whole, enc_weight[0], enc_bias)

    every_own = gather_rows(features)
    brought_a = lax.ppermute(features, "sec", [(0, 1), (1, 2)])
    brought_b = lax.ppermute(features, "sec", [(0, 3)])
    every_brought = gather_rows(brought_a + brought_b)

    mine, theirs = decode(where, every_own, lent_a + lent_b, None, "absolute")
    pair = mine + lax.ppermute(theirs, "feat", SWAP).astype(jnp.float32)
    same_core = [[2 * i + c for i in range(CHIPS)] for c in range(2)]
    spread = lax.all_to_all(pair.astype(jnp.bfloat16), "feat", 0, 0, tiled=True, axis_index_groups=same_core)
    lent_sum = jnp.sum(spread.astype(jnp.float32), axis=0)
    back_a = lax.ppermute(lent_sum, "sec", [(0, 2), (1, 3)])
    back_b = lax.ppermute(lent_sum, "sec", [(2, 3)])

    own_weight = lax.dynamic_index_in_dim(decoders, sec, 0, keepdims=False)
    brought_weight = lax.dynamic_index_in_dim(decoders, jnp.where(sec == 2, 1, 0), 0, keepdims=False)
    start = decode(where, every_own, own_weight, None, "")
    mine, theirs = decode(where, every_brought, brought_weight, start, "relative")
    pair = mine + lax.ppermute(theirs, "feat", SWAP).astype(jnp.float32)
    send = pair.astype(jnp.bfloat16)
    got = [lax.ppermute(send[d], "feat", hop(d)) for d in (4, 3, 5, 2, 6, 1, 7)]
    total = pair[0]
    for g in got:
        total = total + g.astype(jnp.float32)
    return (total + back_a + back_b + dec_bias[0]).astype(jnp.bfloat16)[None]


def solution(mesh):
    in_specs = (
        P("sec", "row", "feat"),
        P("sec", None, "feat"),
        P("sec", "feat"),
        P("sec", None, "feat", "row"),
        P("sec", "row"),
    )
    out_specs = P("sec", "feat", "row")

    return jax.shard_map(per_device, mesh=mesh, in_specs=in_specs, out_specs=out_specs, check_vma=False)
```

profile of v0, /device:TPU:24, one launch (start us, length us, event | category | flops | bytes accessed | tf_op | source)
XLA Modules:
  0.0 150.6 jit_solution(17870435224780648198)
XLA Ops:
  0.0 0.0 collective-permute-start
  0.0 1.5 collective-permute-done
  1.5 0.1 broadcast_in_dim.6
  1.6 2.0 %collective-permute-start.1 = (bf16[288,256]{1,0:T(8,128)(2,1)S(1)}, bf16[288,256]{1,0:T(8,128)(2,1)}, u32[]{:S(2)}, u32[]{:S(2)}) collective-permute-start(bf16[288,256]{1,0:T(8,128)(2,1)S(1)} %get-tuple-element.16), channel_id=1, source_target_pairs={{0,8},{4,60},{8,16},{12,4},{16,24},{20,12},{24,32},{28,20},{32,40}... | collective-permute-start | bytes 442376 | tf_op jit(solution)/shard_map/ppermute | solution.py:31
  3.6 7.2 %collective-permute-done.1 = bf16[288,256]{1,0:T(8,128)(2,1)} collective-permute-done((bf16[288,256]{1,0:T(8,128)(2,1)S(1)}, bf16[288,256]{1,0:T(8,128)(2,1)}, u32[]{:S(2)}, u32[]{:S(2)}) %collective-permute-start.1) | collective-permute-done | bytes 147488 | tf_op jit(solution)/shard_map/ppermute | solution.py:31
  10.8 6.7 %collective-permute-done.2 = bf16[288,256]{1,0:T(8,128)(2,1)} collective-permute-done((bf16[288,256]{1,0:T(8,128)(2,1)}, bf16[288,256]{1,0:T(8,128)(2,1)}, u32[]{:S(2)}, u32[]{:S(2)}) %collective-permute-start.2) | collective-permute-done | bytes 147488 | tf_op jit(solution)/shard_map/ppermute | solution.py:32
  17.5 3.7 %dynamic-slice_bitcast_fusion.1 = (bf16[576,1024]{1,0:T(8,128)(2,1)S(1)}, bf16[576,1024]{1,0:T(8,128)(2,1)S(1)}, bf16[576,1024]{1,0:T(8,128)(2,1)}) fusion(bf16[1,4,1024,576]{2,3,1,0:T(8,128)(2,1)} %param.8, s32[]{:T(128)S(6)} %select_n.57, s32[]{:T(128)S(6)} %select_n.56, s32[]{:T(128)S(6)} %select_n.58), kind=kLoop, calls=%fused_computation.10 | loop fusion | bytes 7077900 | tf_op jit(solution)/shard_map/jit(dynamic_index_in_dim)/squeeze | solution.py:135
  21.1 1.3 collective-permute-start.24
  22.5 1.7 %collective-permute-done.3 = bf16[288,256]{1,0:T(8,128)(2,1)} collective-permute-done((bf16[288,256]{1,0:T(8,128)(2,1)}, bf16[288,256]{1,0:T(8,128)(2,1)}, u32[]{:S(2)}, u32[]{:S(2)}) %collective-permute-start.3) | collective-permute-done | bytes 147488 | tf_op jit(solution)/shard_map/ppermute | solution.py:33
  24.1 1.1 pad_maximum_fusion
  25.2 0.0 copy-start.4
  25.2 0.1 collective-permute-start.5
  25.3 0.9 constant_dynamic-update-slice_fusion.3
  26.3 0.1 collective-permute-start.4
  26.3 0.9 constant_dynamic-update-slice_fusion.2
  27.3 0.9 constant_dynamic-update-slice_fusion.1
  28.2 4.7 %collective-permute-done.4 = bf16[288,256]{1,0:T(8,128)(2,1)S(1)} collective-permute-done((bf16[288,256]{1,0:T(8,128)(2,1)}, bf16[288,256]{1,0:T(8,128)(2,1)S(1)}, u32[]{:S(2)}, u32[]{:S(2)}) %collective-permute-start.4) | collective-permute-done | bytes 147488 | tf_op jit(solution)/shard_map/ppermute | solution.py:34
  33.0 3.8 %fusion.8.own = bf16[256,1024]{1,0:T(8,128)(2,1)S(1)} fusion(bf16[2304,256]{1,0:T(8,128)(2,1)S(1)} %slice_dynamic-update-slice_fusion, bf16[1,2304,1024]{2,1,0:T(8,128)(2,1)} %param.6, f32[1024]{0:T(1024)S(1)} %bitcast.85), kind=kOutput, calls=%fused_computation.7 | convolution fusion | flops 1208745984 | bytes 6426624 | tf_op jit(solution)/shard_map/dot_general | solution.py:46
  36.8 0.3 collective-permute-start.12
  37.1 2.4 %slice_bitcast_fusion = bf16[576,1024]{1,0:T(8,128)(2,1)} fusion(bf16[4,576,1024]{2,1,0:T(8,128)(2,1)} %bitcast.82), kind=kLoop, calls=%fused_computation.8 | loop fusion | bytes 2359296 | tf_op jit(solution)/shard_map/squeeze | solution.py:117
  39.5 1.7 %collective-permute-start.25 = (bf16[576,1024]{1,0:T(8,128)(2,1)}, bf16[576,1024]{1,0:T(8,128)(2,1)}, u32[]{:S(2)}, u32[]{:S(2)}) collective-permute-start(bf16[576,1024]{1,0:T(8,128)(2,1)} %slice_bitcast_fusion), channel_id=1, source_target_pairs={{192,128},{193,129},{194,130},{195,131},{196,132},{197,133},{198,1... | collective-permute-start | bytes 3538952 | tf_op jit(solution)/shard_map/ppermute | solution.py:117
  41.1 1.8 %collective-permute-start.13 = (bf16[256,1024]{1,0:T(8,128)(2,1)S(1)}, bf16[256,1024]{1,0:T(8,128)(2,1)S(1)}, u32[]{:S(2)}, u32[]{:S(2)}) collective-permute-start(bf16[256,1024]{1,0:T(8,128)(2,1)S(1)} %fusion.8.own), channel_id=1, source_target_pairs={{0,3},{1,0},{2,1},{3,2},{4,7},{5,4},{6,5},{7,6},{8,11},{9,8},{10,9... | collective-permute-start | bytes 1572872 | tf_op jit(solution)/shard_map/ppermute | solution.py:53
  42.9 3.4 %collective-permute-start.6 = (bf16[256,1024]{1,0:T(8,128)(2,1)S(1)}, bf16[256,1024]{1,0:T(8,128)(2,1)S(1)}, u32[]{:S(2)}, u32[]{:S(2)}) collective-permute-start(bf16[256,1024]{1,0:T(8,128)(2,1)S(1)} %fusion.8.own), channel_id=1, source_target_pairs={{0,64},{64,128},{1,65},{65,129},{2,66},{66,130},{3,67},{67,131},{4... | collective-permute-start | bytes 1572872 | tf_op jit(solution)/shard_map/ppermute | solution.py:123
  46.4 2.9 %collective-permute-done.12.before = bf16[256,1024]{1,0:T(8,128)(2,1)S(1)} collective-permute-done((bf16[256,1024]{1,0:T(8,128)(2,1)S(1)}, bf16[256,1024]{1,0:T(8,128)(2,1)S(1)}, u32[]{:S(2)}, u32[]{:S(2)}) %collective-permute-start.12) | collective-permute-done | bytes 524320 | tf_op jit(solution)/shard_map/ppermute | solution.py:52
  49.2 6.6 %collective-permute-start.7 = (bf16[256,1024]{1,0:T(8,128)(2,1)S(1)}, bf16[256,1024]{1,0:T(8,128)(2,1)S(1)}, u32[]{:S(2)}, u32[]{:S(2)}) collective-permute-start(bf16[256,1024]{1,0:T(8,128)(2,1)S(1)} %fusion.8.own), channel_id=1, source_target_pairs={{0,192},{1,193},{2,194},{3,195},{4,196},{5,197},{6,198},{7,199},{8... | collective-permute-start | bytes 1572872 | tf_op jit(solution)/shard_map/ppermute | solution.py:124
  55.8 0.7 slice.54
  56.5 1.5 collective-permute-start.14
  58.0 0.7 slice.55
  58.8 0.5 collective-permute-start.15
  59.3 5.8 %collective-permute-done.7 = bf16[256,1024]{1,0:T(8,128)(2,1)S(1)} collective-permute-done((bf16[256,1024]{1,0:T(8,128)(2,1)S(1)}, bf16[256,1024]{1,0:T(8,128)(2,1)S(1)}, u32[]{:S(2)}, u32[]{:S(2)}) %collective-permute-start.7) | collective-permute-done | bytes 524320 | tf_op jit(solution)/shard_map/ppermute | solution.py:124
  65.0 1.0 add.129.own
  66.0 1.6 %collective-permute-start.8 = (bf16[256,1024]{1,0:T(8,128)(2,1)}, bf16[256,1024]{1,0:T(8,128)(2,1)}, u32[]{:S(2)}, u32[]{:S(2)}) collective-permute-start(bf16[256,1024]{1,0:T(8,128)(2,1)} %add.129.own), channel_id=1, source_target_pairs={{0,1},{1,2},{2,3},{3,0},{4,5},{5,6},{6,7},{7,4},{8,9},{9,10},{10,1... | collective-permute-start | bytes 1572872 | tf_op jit(solution)/shard_map/ppermute | solution.py:52
  67.6 0.5 collective-permute-start.9
  68.1 0.1 pad_add_fusion.where_ref
  68.2 2.1 %add.139.weight_ref = bf16[576,1024]{1,0:T(8,128)(2,1)S(1)} add(bf16[576,1024]{1,0:T(8,128)(2,1)} %collective-permute-done.24, bf16[576,1024]{1,0:T(8,128)(2,1)} %collective-permute-done.25) | non-fusion elementwise | flops 589824 | bytes 3538944 | tf_op jit(solution)/shard_map/add | solution.py:127
  70.3 3.0 %shard_map.57 = (f32[8,64,576]{2,1,0:T(8,128)S(1)}, bf16[8,64,576]{2,1,0:T(8,128)(2,1)S(1)}) custom-call(s32[3]{0:T(128)S(1)} %pad_add_fusion.where_ref, bf16[256,1024]{1,0:T(8,128)(2,1)S(1)} %copy-done.1, bf16[256,1024]{1,0:T(8,128)(2,1)S(1)} %collective-permute-done.12.before, bf16[256,1024]{1,0:T(8,128)(2,1)S(1)} %collective-permute-done.13.after, ...), custom_call_target="tpu_custom_call" | custom-call | tf_op jit(solution)/shard_map/pallas_call | solution.py:96
  73.3 0.1 collective-permute-start.26
  73.4 3.8 %collective-permute-done.8.before = bf16[256,1024]{1,0:T(8,128)(2,1)} collective-permute-done((bf16[256,1024]{1,0:T(8,128)(2,1)}, bf16[256,1024]{1,0:T(8,128)(2,1)}, u32[]{:S(2)}, u32[]{:S(2)}) %collective-permute-start.8) | collective-permute-done | bytes 524320 | tf_op jit(solution)/shard_map/ppermute | solution.py:52
  77.3 1.0 slice.52
  78.2 2.9 %collective-permute-start.10 = (bf16[128,1024]{1,0:T(8,128)(2,1)S(1)}, bf16[128,1024]{1,0:T(8,128)(2,1)S(1)}, u32[]{:S(2)}, u32[]{:S(2)}) collective-permute-start(bf16[128,1024]{1,0:T(8,128)(2,1)S(1)} %slice.52), channel_id=1, source_target_pairs={{0,1},{1,2},{2,3},{3,0},{4,5},{5,6},{6,7},{7,4},{8,9},{9,10},{10,1... | collective-permute-start | bytes 786440 | tf_op jit(solution)/shard_map/ppermute | solution.py:54
  81.2 1.0 slice.53
  82.1 0.1 collective-permute-start.11
  82.2 2.9 %shard_map.55.rest_0_ = f32[4,256,576]{2,1,0:T(8,128)S(1)} custom-call(s32[3]{0:T(128)S(1)} %pad_add_fusion.where_ref, bf16[256,1024]{1,0:T(8,128)(2,1)S(1)} %copy-done.1, bf16[256,1024]{1,0:T(8,128)(2,1)S(1)} %collective-permute-done.12.before, bf16[256,1024]{1,0:T(8,128)(2,1)S(1)} %collective-permute-done.13.after, ...), custom_call_target="tpu_custom_call" | custom-call | tf_op jit(solution)/shard_map/pallas_call | solution.py:96
  85.2 4.6 %collective-permute-done.11.second = bf16[128,1024]{1,0:T(8,128)(2,1)S(1)} collective-permute-done((bf16[128,1024]{1,0:T(8,128)(2,1)S(1)}, bf16[128,1024]{1,0:T(8,128)(2,1)S(1)}, u32[]{:S(2)}, u32[]{:S(2)}) %collective-permute-start.11) | collective-permute-done | bytes 262176 | tf_op jit(solution)/shard_map/ppermute | solution.py:55
  89.8 3.4 %shard_map.56 = (f32[8,64,576]{2,1,0:T(8,128)S(1)}, bf16[8,64,576]{2,1,0:T(8,128)(2,1)S(1)}) custom-call(s32[3]{0:T(128)S(1)} %pad_add_fusion.where_ref, bf16[256,1024]{1,0:T(8,128)(2,1)} %add.129.own, bf16[256,1024]{1,0:T(8,128)(2,1)} %collective-permute-done.8.before, bf16[256,1024]{1,0:T(8,128)(2,1)} %collective-permute-done.9.after, ...), custom_call_target="tpu_custom_call" | custom-call | tf_op jit(solution)/shard_map/pallas_call | solution.py:96
  93.2 0.1 collective-permute-start.16
  93.3 1.0 add_convert_fusion
  94.3 9.9 %all-to-all-start = ((bf16[8,64,576]{2,1,0:T(8,128)(2,1)}), bf16[8,64,576]{2,1,0:T(8,128)(2,1)S(1)}, u32[]{:S(2)}, u32[]{:S(2)}) async-start(bf16[8,64,576]{2,1,0:T(8,128)(2,1)} %add_convert_fusion), calls=%async_computation | async-start | bytes 1310720 | tf_op jit(solution)/shard_map/all_to_all | solution.py:130
  104.2 2.4 %fusion.23 = (bf16[8,64,576]{2,1,0:T(8,128)(2,1)S(1)}, f32[8,64,576]{2,1,0:T(8,128)}) fusion(f32[8,64,576]{2,1,0:T(8,128)S(1)} %get-tuple-element.9, bf16[8,64,576]{2,1,0:T(8,128)(2,1)} %collective-permute-done.16), kind=kLoop, calls=%fused_computation.43 | loop fusion | flops 884736 | bytes 3538944 | tf_op jit(solution)/shard_map/convert_element_type | solution.py:140
  106.6 0.1 slice_bitcast_fusion.8
  106.6 3.3 %collective-permute-start.23 = (bf16[64,576]{1,0:T(8,128)(2,1)S(1)}, bf16[64,576]{1,0:T(8,128)(2,1)S(1)}, u32[]{:S(2)}, u32[]{:S(2)}) collective-permute-start(bf16[64,576]{1,0:T(8,128)(2,1)S(1)} %get-tuple-element.21), channel_id=1, source_target_pairs={{0,56},{4,60},{8,0},{12,4},{16,8},{20,12},{24,16},{28,20},{32,24},... | collective-permute-start | bytes 221192 | tf_op jit(solution)/shard_map/ppermute | solution.py:141
  110.0 2.9 %collective-permute-start.21 = (bf16[64,576]{1,0:T(8,128)(2,1)S(1)}, bf16[64,576]{1,0:T(8,128)(2,1)S(1)}, u32[]{:S(2)}, u32[]{:S(2)}) collective-permute-start(bf16[64,576]{1,0:T(8,128)(2,1)S(1)} %get-tuple-element.23), channel_id=1, source_target_pairs={{0,48},{4,52},{8,56},{12,60},{16,0},{20,4},{24,8},{28,12},{32,16},... | collective-permute-start | bytes 221192 | tf_op jit(solution)/shard_map/ppermute | solution.py:141
  112.9 0.0 collective-permute-start.20
  112.9 12.5 %all-to-all-done = bf16[8,64,576]{2,1,0:T(8,128)(2,1)S(1)} async-done(((bf16[8,64,576]{2,1,0:T(8,128)(2,1)}), bf16[8,64,576]{2,1,0:T(8,128)(2,1)S(1)}, u32[]{:S(2)}, u32[]{:S(2)}) %all-to-all-start) | async-done | bytes 589856 | tf_op jit(solution)/shard_map/all_to_all | solution.py:130
  125.4 0.1 convert_reduce_fusion
  125.5 0.7 collective-permute-start.28
  126.2 8.3 %collective-permute-start.27 = (f32[64,576]{1,0:T(8,128)S(1)}, f32[64,576]{1,0:T(8,128)S(1)}, u32[]{:S(2)}, u32[]{:S(2)}) collective-permute-start(f32[64,576]{1,0:T(8,128)S(1)} %convert_reduce_fusion), channel_id=1, source_target_pairs={{0,128},{64,192},{1,129},{65,193},{2,130},{66,194},{3,131},{67,195... | collective-permute-start | bytes 442376 | tf_op jit(solution)/shard_map/ppermute | solution.py:132
  134.5 1.6 %collective-permute-start.19 = (bf16[64,576]{1,0:T(8,128)(2,1)S(1)}, bf16[64,576]{1,0:T(8,128)(2,1)S(1)}, u32[]{:S(2)}, u32[]{:S(2)}) collective-permute-start(bf16[64,576]{1,0:T(8,128)(2,1)S(1)} %get-tuple-element.25), channel_id=1, source_target_pairs={{0,40},{4,44},{8,48},{12,52},{16,56},{20,60},{24,0},{28,4},{32,8},... | collective-permute-start | bytes 221192 | tf_op jit(solution)/shard_map/ppermute | solution.py:141
  136.1 2.3 %collective-permute-start.18 = (bf16[64,576]{1,0:T(8,128)(2,1)S(1)}, bf16[64,576]{1,0:T(8,128)(2,1)S(1)}, u32[]{:S(2)}, u32[]{:S(2)}) collective-permute-start(bf16[64,576]{1,0:T(8,128)(2,1)S(1)} %get-tuple-element.26), channel_id=1, source_target_pairs={{0,24},{4,28},{8,32},{12,36},{16,40},{20,44},{24,48},{28,52},{32,5... | collective-permute-start | bytes 221192 | tf_op jit(solution)/shard_map/ppermute | solution.py:141
  138.4 1.9 %collective-permute-start.17 = (bf16[64,576]{1,0:T(8,128)(2,1)S(1)}, bf16[64,576]{1,0:T(8,128)(2,1)S(1)}, u32[]{:S(2)}, u32[]{:S(2)}) collective-permute-start(bf16[64,576]{1,0:T(8,128)(2,1)S(1)} %get-tuple-element.20), channel_id=1, source_target_pairs={{0,32},{4,36},{8,40},{12,44},{16,48},{20,52},{24,56},{28,60},{32,0... | collective-permute-start | bytes 221192 | tf_op jit(solution)/shard_map/ppermute | solution.py:141
  140.4 1.3 collective-permute-done.19
  141.7 3.5 %collective-permute-done.18 = bf16[64,576]{1,0:T(8,128)(2,1)S(1)} collective-permute-done((bf16[64,576]{1,0:T(8,128)(2,1)S(1)}, bf16[64,576]{1,0:T(8,128)(2,1)S(1)}, u32[]{:S(2)}, u32[]{:S(2)}) %collective-permute-start.18) | collective-permute-done | bytes 73760 | tf_op jit(solution)/shard_map/ppermute | solution.py:141
  145.2 3.8 %collective-permute-done.17 = bf16[64,576]{1,0:T(8,128)(2,1)S(1)} collective-permute-done((bf16[64,576]{1,0:T(8,128)(2,1)S(1)}, bf16[64,576]{1,0:T(8,128)(2,1)S(1)}, u32[]{:S(2)}, u32[]{:S(2)}) %collective-permute-start.17) | collective-permute-done | bytes 73760 | tf_op jit(solution)/shard_map/ppermute | solution.py:141
  149.0 1.7 %fusion.22 = bf16[1,64,576]{2,1,0:T(8,128)(2,1)} fusion(f32[576]{0:T(1024)S(1)} %reduce, f32[64,576]{1,0:T(8,128)S(1)} %collective-permute-done.28, f32[64,576]{1,0:T(8,128)S(1)} %collective-permute-done.27, bf16[64,576]{1,0:T(8,128)(2,1)S(1)} %collective-permute-done.23, bf16[64,576]{1,0:T(8,128)(2,1)S(1)} %collective-permute-done.22, ...), kind=kLoop, calls=%fused_computation.36 | loop fusion | flops 663552 | bytes 1034496 | tf_op jit(solution)/shard_map/broadcast_in_dim | solution.py:145
  (35 shorter events, 0.2 us)
Async XLA Ops:
  0.0 1.6 %copy-start.2 = (bf16[1,256,144]{1,2,0:T(8,128)(2,1)S(1)}, bf16[1,256,144]{1,2,0:T(8,128)(2,1)}, u32[]{:S(2)}) copy-start(bf16[1,256,144]{1,2,0:T(8,128)(2,1)} %param.5) | copy-start | bytes 221188
  0.0 1.5 collective-permute-start
  1.6 9.2 %collective-permute-start.1 = (bf16[288,256]{1,0:T(8,128)(2,1)S(1)}, bf16[288,256]{1,0:T(8,128)(2,1)}, u32[]{:S(2)}, u32[]{:S(2)}) collective-permute-start(bf16[288,256]{1,0:T(8,128)(2,1)S(1)} %get-tuple-element.16), channel_id=1, source_target_pairs={{0,8},{4,60},{8,16},{12,4},{16,24},{20,12},{24,32},{28,20},{32,40}... | collective-permute-start | bytes 442376 | tf_op jit(solution)/shard_map/ppermute | solution.py:31
  10.8 6.7 %collective-permute-start.2 = (bf16[288,256]{1,0:T(8,128)(2,1)}, bf16[288,256]{1,0:T(8,128)(2,1)}, u32[]{:S(2)}, u32[]{:S(2)}) collective-permute-start(bf16[288,256]{1,0:T(8,128)(2,1)} %collective-permute-done.1), channel_id=1, source_target_pairs={{0,8},{4,60},{8,16},{12,4},{16,24},{20,12},{24,32},{28,20},{32,40}... | collective-permute-start | bytes 442376 | tf_op jit(solution)/shard_map/ppermute | solution.py:32
  17.5 6.7 %collective-permute-start.3 = (bf16[288,256]{1,0:T(8,128)(2,1)}, bf16[288,256]{1,0:T(8,128)(2,1)}, u32[]{:S(2)}, u32[]{:S(2)}) collective-permute-start(bf16[288,256]{1,0:T(8,128)(2,1)} %collective-permute-done.2), channel_id=1, source_target_pairs={{0,8},{4,60},{8,16},{12,4},{16,24},{20,12},{24,32},{28,20},{32,40}... | collective-permute-start | bytes 442376 | tf_op jit(solution)/shard_map/ppermute | solution.py:33
  21.1 46.5 %collective-permute-start.24 = (bf16[576,1024]{1,0:T(8,128)(2,1)}, bf16[576,1024]{1,0:T(8,128)(2,1)}, u32[]{:S(2)}, u32[]{:S(2)}) collective-permute-start(bf16[576,1024]{1,0:T(8,128)(2,1)} %get-tuple-element.19), channel_id=1, source_target_pairs={{128,0},{192,64},{129,1},{193,65},{130,2},{194,66},{131,3},{195,67... | collective-permute-start | bytes 3538952 | tf_op jit(solution)/shard_map/ppermute | solution.py:116
  25.2 7.8 %copy-start.4 = (f32[1,1024]{1,0:T(1,128)S(1)}, f32[1,1024]{1,0:T(1,128)}, u32[]{:S(2)}) copy-start(f32[1,1024]{1,0:T(1,128)} %param.7) | copy-start | bytes 12292
  25.2 7.7 %collective-permute-start.5 = (bf16[864,256]{1,0:T(8,128)(2,1)S(1)}, bf16[864,256]{1,0:T(8,128)(2,1)S(1)}, u32[]{:S(2)}, u32[]{:S(2)}) collective-permute-start(bf16[864,256]{1,0:T(8,128)(2,1)S(1)} %pad_maximum_fusion), channel_id=1, source_target_pairs={{0,4},{4,0},{8,12},{12,8},{16,20},{20,16},{24,28},{28,24},{32,36},... | collective-permute-start | bytes 1327112 | tf_op jit(solution)/shard_map/ppermute | solution.py:35
  26.3 6.6 %collective-permute-start.4 = (bf16[288,256]{1,0:T(8,128)(2,1)}, bf16[288,256]{1,0:T(8,128)(2,1)S(1)}, u32[]{:S(2)}, u32[]{:S(2)}) collective-permute-start(bf16[288,256]{1,0:T(8,128)(2,1)} %collective-permute-done.3), channel_id=1, source_target_pairs={{0,8},{4,60},{8,16},{12,4},{16,24},{20,12},{24,32},{28,20},{32,40}... | collective-permute-start | bytes 442376 | tf_op jit(solution)/shard_map/ppermute | solution.py:34
  36.8 12.5 %copy-start = (bf16[256,1024]{1,0:T(8,128)(2,1)}, bf16[256,1024]{1,0:T(8,128)(2,1)S(1)}, u32[]{:S(2)}) copy-start(bf16[256,1024]{1,0:T(8,128)(2,1)S(1)} %fusion.8.own) | copy-start | bytes 1572868
  36.8 12.4 %collective-permute-start.12 = (bf16[256,1024]{1,0:T(8,128)(2,1)S(1)}, bf16[256,1024]{1,0:T(8,128)(2,1)S(1)}, u32[]{:S(2)}, u32[]{:S(2)}) collective-permute-start(bf16[256,1024]{1,0:T(8,128)(2,1)S(1)} %fusion.8.own), channel_id=1, source_target_pairs={{0,1},{1,2},{2,3},{3,0},{4,5},{5,6},{6,7},{7,4},{8,9},{9,10},{10,1... | collective-permute-start | bytes 1572872 | tf_op jit(solution)/shard_map/ppermute | solution.py:52
  39.5 28.7 %collective-permute-start.25 = (bf16[576,1024]{1,0:T(8,128)(2,1)}, bf16[576,1024]{1,0:T(8,128)(2,1)}, u32[]{:S(2)}, u32[]{:S(2)}) collective-permute-start(bf16[576,1024]{1,0:T(8,128)(2,1)} %slice_bitcast_fusion), channel_id=1, source_target_pairs={{192,128},{193,129},{194,130},{195,131},{196,132},{197,133},{198,1... | collective-permute-start | bytes 3538952 | tf_op jit(solution)/shard_map/ppermute | solution.py:117
  41.1 15.4 %collective-permute-start.13 = (bf16[256,1024]{1,0:T(8,128)(2,1)S(1)}, bf16[256,1024]{1,0:T(8,128)(2,1)S(1)}, u32[]{:S(2)}, u32[]{:S(2)}) collective-permute-start(bf16[256,1024]{1,0:T(8,128)(2,1)S(1)} %fusion.8.own), channel_id=1, source_target_pairs={{0,3},{1,0},{2,1},{3,2},{4,7},{5,4},{6,5},{7,6},{8,11},{9,8},{10,9... | collective-permute-start | bytes 1572872 | tf_op jit(solution)/shard_map/ppermute | solution.py:53
  42.9 15.8 %collective-permute-start.6 = (bf16[256,1024]{1,0:T(8,128)(2,1)S(1)}, bf16[256,1024]{1,0:T(8,128)(2,1)S(1)}, u32[]{:S(2)}, u32[]{:S(2)}) collective-permute-start(bf16[256,1024]{1,0:T(8,128)(2,1)S(1)} %fusion.8.own), channel_id=1, source_target_pairs={{0,64},{64,128},{1,65},{65,129},{2,66},{66,130},{3,67},{67,131},{4... | collective-permute-start | bytes 1572872 | tf_op jit(solution)/shard_map/ppermute | solution.py:123
  49.2 15.8 %collective-permute-start.7 = (bf16[256,1024]{1,0:T(8,128)(2,1)S(1)}, bf16[256,1024]{1,0:T(8,128)(2,1)S(1)}, u32[]{:S(2)}, u32[]{:S(2)}) collective-permute-start(bf16[256,1024]{1,0:T(8,128)(2,1)S(1)} %fusion.8.own), channel_id=1, source_target_pairs={{0,192},{1,193},{2,194},{3,195},{4,196},{5,197},{6,198},{7,199},{8... | collective-permute-start | bytes 1572872 | tf_op jit(solution)/shard_map/ppermute | solution.py:124
  56.5 13.7 %collective-permute-start.14 = (bf16[128,1024]{1,0:T(8,128)(2,1)}, bf16[128,1024]{1,0:T(8,128)(2,1)}, u32[]{:S(2)}, u32[]{:S(2)}) collective-permute-start(bf16[128,1024]{1,0:T(8,128)(2,1)} %slice.54), channel_id=1, source_target_pairs={{0,1},{1,2},{2,3},{3,0},{4,5},{5,6},{6,7},{7,4},{8,9},{9,10},{10,1... | collective-permute-start | bytes 786440 | tf_op jit(solution)/shard_map/ppermute | solution.py:54
  58.8 11.5 %collective-permute-start.15 = (bf16[128,1024]{1,0:T(8,128)(2,1)}, bf16[128,1024]{1,0:T(8,128)(2,1)}, u32[]{:S(2)}, u32[]{:S(2)}) collective-permute-start(bf16[128,1024]{1,0:T(8,128)(2,1)} %slice.55), channel_id=1, source_target_pairs={{0,3},{1,0},{2,1},{3,2},{4,7},{5,4},{6,5},{7,6},{8,11},{9,8},{10,9... | collective-permute-start | bytes 786440 | tf_op jit(solution)/shard_map/ppermute | solution.py:55
  66.0 11.2 %collective-permute-start.8 = (bf16[256,1024]{1,0:T(8,128)(2,1)}, bf16[256,1024]{1,0:T(8,128)(2,1)}, u32[]{:S(2)}, u32[]{:S(2)}) collective-permute-start(bf16[256,1024]{1,0:T(8,128)(2,1)} %add.129.own), channel_id=1, source_target_pairs={{0,1},{1,2},{2,3},{3,0},{4,5},{5,6},{6,7},{7,4},{8,9},{9,10},{10,1... | collective-permute-start | bytes 1572872 | tf_op jit(solution)/shard_map/ppermute | solution.py:52
  67.6 13.6 %collective-permute-start.9 = (bf16[256,1024]{1,0:T(8,128)(2,1)}, bf16[256,1024]{1,0:T(8,128)(2,1)}, u32[]{:S(2)}, u32[]{:S(2)}) collective-permute-start(bf16[256,1024]{1,0:T(8,128)(2,1)} %add.129.own), channel_id=1, source_target_pairs={{0,3},{1,0},{2,1},{3,2},{4,7},{5,4},{6,5},{7,6},{8,11},{9,8},{10,9... | collective-permute-start | bytes 1572872 | tf_op jit(solution)/shard_map/ppermute | solution.py:53
  68.1 2.2 %copy-start.1 = (bf16[256,1024]{1,0:T(8,128)(2,1)S(1)}, bf16[256,1024]{1,0:T(8,128)(2,1)}, u32[]{:S(2)}) copy-start(bf16[256,1024]{1,0:T(8,128)(2,1)} %copy-done) | copy-start | bytes 1572868
  73.3 19.9 %collective-permute-start.26 = (bf16[8,64,576]{2,1,0:T(8,128)(2,1)S(1)}, bf16[8,64,576]{2,1,0:T(8,128)(2,1)S(1)}, u32[]{:S(2)}, u32[]{:S(2)}) collective-permute-start(bf16[8,64,576]{2,1,0:T(8,128)(2,1)S(1)} %get-tuple-element.12), channel_id=1, source_target_pairs={{0,4},{4,0},{8,12},{12,8},{16,20},{20,16},{24,28},{28,24},{32,36},... | collective-permute-start | bytes 1769480 | tf_op jit(solution)/shard_map/ppermute | solution.py:128
  78.2 6.9 %collective-permute-start.10 = (bf16[128,1024]{1,0:T(8,128)(2,1)S(1)}, bf16[128,1024]{1,0:T(8,128)(2,1)S(1)}, u32[]{:S(2)}, u32[]{:S(2)}) collective-permute-start(bf16[128,1024]{1,0:T(8,128)(2,1)S(1)} %slice.52), channel_id=1, source_target_pairs={{0,1},{1,2},{2,3},{3,0},{4,5},{5,6},{6,7},{7,4},{8,9},{9,10},{10,1... | collective-permute-start | bytes 786440 | tf_op jit(solution)/shard_map/ppermute | solution.py:54
  82.1 7.7 %collective-permute-start.11 = (bf16[128,1024]{1,0:T(8,128)(2,1)S(1)}, bf16[128,1024]{1,0:T(8,128)(2,1)S(1)}, u32[]{:S(2)}, u32[]{:S(2)}) collective-permute-start(bf16[128,1024]{1,0:T(8,128)(2,1)S(1)} %slice.53), channel_id=1, source_target_pairs={{0,3},{1,0},{2,1},{3,2},{4,7},{5,4},{6,5},{7,6},{8,11},{9,8},{10,9... | collective-permute-start | bytes 786440 | tf_op jit(solution)/shard_map/ppermute | solution.py:55
  93.2 11.1 %collective-permute-start.16 = (bf16[8,64,576]{2,1,0:T(8,128)(2,1)S(1)}, bf16[8,64,576]{2,1,0:T(8,128)(2,1)}, u32[]{:S(2)}, u32[]{:S(2)}) collective-permute-start(bf16[8,64,576]{2,1,0:T(8,128)(2,1)S(1)} %get-tuple-element.10), channel_id=1, source_target_pairs={{0,4},{4,0},{8,12},{12,8},{16,20},{20,16},{24,28},{28,24},{32,36},... | collective-permute-start | bytes 1769480 | tf_op jit(solution)/shard_map/ppermute | solution.py:139
  94.3 31.1 %all-to-all-start = ((bf16[8,64,576]{2,1,0:T(8,128)(2,1)}), bf16[8,64,576]{2,1,0:T(8,128)(2,1)S(1)}, u32[]{:S(2)}, u32[]{:S(2)}) async-start(bf16[8,64,576]{2,1,0:T(8,128)(2,1)} %add_convert_fusion), calls=%async_computation | async-start | bytes 1310720 | tf_op jit(solution)/shard_map/all_to_all | solution.py:130
  106.6 33.8 %copy-start.3 = (f32[1,576]{1,0:T(1,128)S(1)}, f32[1,576]{1,0:T(1,128)}, u32[]{:S(2)}) copy-start(f32[1,576]{1,0:T(1,128)} %param.9) | copy-start | bytes 6916
  106.6 19.5 %collective-permute-start.23 = (bf16[64,576]{1,0:T(8,128)(2,1)S(1)}, bf16[64,576]{1,0:T(8,128)(2,1)S(1)}, u32[]{:S(2)}, u32[]{:S(2)}) collective-permute-start(bf16[64,576]{1,0:T(8,128)(2,1)S(1)} %get-tuple-element.21), channel_id=1, source_target_pairs={{0,56},{4,60},{8,0},{12,4},{16,8},{20,12},{24,16},{28,20},{32,24},... | collective-permute-start | bytes 221192 | tf_op jit(solution)/shard_map/ppermute | solution.py:141
  109.9 24.5 %collective-permute-start.22 = (bf16[64,576]{1,0:T(8,128)(2,1)S(1)}, bf16[64,576]{1,0:T(8,128)(2,1)S(1)}, u32[]{:S(2)}, u32[]{:S(2)}) collective-permute-start(bf16[64,576]{1,0:T(8,128)(2,1)S(1)} %get-tuple-element.22), channel_id=1, source_target_pairs={{0,8},{4,12},{8,16},{12,20},{16,24},{20,28},{24,32},{28,36},{32,40... | collective-permute-start | bytes 221192 | tf_op jit(solution)/shard_map/ppermute | solution.py:141
  110.0 26.1 %collective-permute-start.21 = (bf16[64,576]{1,0:T(8,128)(2,1)S(1)}, bf16[64,576]{1,0:T(8,128)(2,1)S(1)}, u32[]{:S(2)}, u32[]{:S(2)}) collective-permute-start(bf16[64,576]{1,0:T(8,128)(2,1)S(1)} %get-tuple-element.23), channel_id=1, source_target_pairs={{0,48},{4,52},{8,56},{12,60},{16,0},{20,4},{24,8},{28,12},{32,16},... | collective-permute-start | bytes 221192 | tf_op jit(solution)/shard_map/ppermute | solution.py:141
  112.9 25.5 %collective-permute-start.20 = (bf16[64,576]{1,0:T(8,128)(2,1)S(1)}, bf16[64,576]{1,0:T(8,128)(2,1)S(1)}, u32[]{:S(2)}, u32[]{:S(2)}) collective-permute-start(bf16[64,576]{1,0:T(8,128)(2,1)S(1)} %get-tuple-element.24), channel_id=1, source_target_pairs={{0,16},{4,20},{8,24},{12,28},{16,32},{20,36},{24,40},{28,44},{32,4... | collective-permute-start | bytes 221192 | tf_op jit(solution)/shard_map/ppermute | solution.py:141
  125.5 23.5 %collective-permute-start.28 = (f32[64,576]{1,0:T(8,128)S(1)}, f32[64,576]{1,0:T(8,128)S(1)}, u32[]{:S(2)}, u32[]{:S(2)}) collective-permute-start(f32[64,576]{1,0:T(8,128)S(1)} %convert_reduce_fusion), channel_id=1, source_target_pairs={{128,192},{129,193},{130,194},{131,195},{132,196},{133,197},{134,1... | collective-permute-start | bytes 442376 | tf_op jit(solution)/shard_map/ppermute | solution.py:133
  126.2 22.8 %collective-permute-start.27 = (f32[64,576]{1,0:T(8,128)S(1)}, f32[64,576]{1,0:T(8,128)S(1)}, u32[]{:S(2)}, u32[]{:S(2)}) collective-permute-start(f32[64,576]{1,0:T(8,128)S(1)} %convert_reduce_fusion), channel_id=1, source_target_pairs={{0,128},{64,192},{1,129},{65,193},{2,130},{66,194},{3,131},{67,195... | collective-permute-start | bytes 442376 | tf_op jit(solution)/shard_map/ppermute | solution.py:132
  134.5 7.2 %collective-permute-start.19 = (bf16[64,576]{1,0:T(8,128)(2,1)S(1)}, bf16[64,576]{1,0:T(8,128)(2,1)S(1)}, u32[]{:S(2)}, u32[]{:S(2)}) collective-permute-start(bf16[64,576]{1,0:T(8,128)(2,1)S(1)} %get-tuple-element.25), channel_id=1, source_target_pairs={{0,40},{4,44},{8,48},{12,52},{16,56},{20,60},{24,0},{28,4},{32,8},... | collective-permute-start | bytes 221192 | tf_op jit(solution)/shard_map/ppermute | solution.py:141
  136.1 9.1 %collective-permute-start.18 = (bf16[64,576]{1,0:T(8,128)(2,1)S(1)}, bf16[64,576]{1,0:T(8,128)(2,1)S(1)}, u32[]{:S(2)}, u32[]{:S(2)}) collective-permute-start(bf16[64,576]{1,0:T(8,128)(2,1)S(1)} %get-tuple-element.26), channel_id=1, source_target_pairs={{0,24},{4,28},{8,32},{12,36},{16,40},{20,44},{24,48},{28,52},{32,5... | collective-permute-start | bytes 221192 | tf_op jit(solution)/shard_map/ppermute | solution.py:141
  138.4 10.6 %collective-permute-start.17 = (bf16[64,576]{1,0:T(8,128)(2,1)S(1)}, bf16[64,576]{1,0:T(8,128)(2,1)S(1)}, u32[]{:S(2)}, u32[]{:S(2)}) collective-permute-start(bf16[64,576]{1,0:T(8,128)(2,1)S(1)} %get-tuple-element.20), channel_id=1, source_target_pairs={{0,32},{4,36},{8,40},{12,44},{16,48},{20,52},{24,56},{28,60},{32,0... | collective-permute-start | bytes 221192 | tf_op jit(solution)/shard_map/ppermute | solution.py:141
where the time goes:
time: 151 us
  waiting for transfers between devices  59.9 us (40%)
  starting transfers between devices  55.5 us (37%)
  local copies, waits for them, and re-layouts  12.4 us (8%)
  other arithmetic  9.46 us (6%)
  Pallas kernels  9.28 us (6%)
  matrix products  3.75 us (2%)
    all_to_all x1, waiting for transfers between devices, per_device(): lax.all_to_all(pair.astype(jnp.bfloat16), 'feat', 0, 0, tiled=True, axis_...  12.5 us
    ppermute x7, starting transfers between devices, per_device(): got = [lax.ppermute(send[d], 'feat', hop(d)) for d in (4, 3, 5, 2, 6, 1, 7)]  12.1 us
    all_to_all x1, starting transfers between devices, per_device(): lax.all_to_all(pair.astype(jnp.bfloat16), 'feat', 0, 0, tiled=True, axis_...  9.94 us
    pallas_call x3, Pallas kernels, decode(): pl.pallas_call(kernel, in_specs=[SMEM] + [VMEM] * len(operands), out_spec...  9.28 us
    ppermute x7, waiting for transfers between devices, per_device(): got = [lax.ppermute(send[d], 'feat', hop(d)) for d in (4, 3, 5, 2, 6, 1, 7)]  8.63 us
    ppermute x1, starting transfers between devices, per_device(): back_a = lax.ppermute(lent_sum, 'sec', [(0, 2), (1, 3)])  8.3 us
    ppermute x1, waiting for transfers between devices, gather_inputs(): b1 = lax.ppermute(block, 'feat', BOTH)  7.17 us
    ppermute x2, waiting for transfers between devices, gather_rows(): before = lax.ppermute(own, 'row', ring(1))  6.71 us
  transfers between devices with their start and end apart: 30, of which 13 were waited for; matrix products, arithmetic and copies ran while one was open for 16% of the time, Pallas kernels for 6%

commit v1 on v0

v1 whole, which is shorter than its diff:
```python
import jax
import jax.numpy as jnp
from jax import lax
from jax.experimental import pallas as pl
from jax.experimental.pallas import tpu as pltpu
from jax.sharding import PartitionSpec as P


CHIPS = 8
ROWS = 4
PIECE = 64
ANY = pl.BlockSpec(memory_space=pl.ANY)
VMEM = pl.BlockSpec(memory_space=pltpu.VMEM)
SMEM = pl.BlockSpec(memory_space=pltpu.SMEM)
PARAMS = pltpu.CompilerParams(vmem_limit_bytes=12 << 20)


def ring(shift):
    return [(i, (i + shift) % ROWS) for i in range(ROWS)]


def hop(shift):
    return [(i, ((i // 2 + shift) % CHIPS) * 2 + i % 2) for i in range(2 * CHIPS)]


SWAP = [(i, i ^ 1) for i in range(2 * CHIPS)]
BOTH = [(i, ((i // 2 + (1 if i % 2 == 0 else -1)) % CHIPS) * 2 + i % 2) for i in range(2 * CHIPS)]


def in_vmem(values):
    return [pltpu.with_memory_space_constraint(v, pltpu.VMEM) for v in values]


def call(kernel, where, vmem, rest, out, scratch):
    return pl.pallas_call(
        kernel,
        in_specs=[SMEM] + [VMEM] * len(vmem) + [ANY] * len(rest),
        out_specs=tuple(VMEM for _ in out),
        out_shape=tuple(pltpu.VMEM(shape, dtype) for shape, dtype in out),
        scratch_shapes=scratch,
        compiler_params=PARAMS,
    )(where, *in_vmem(vmem), *rest)


def copy_lent(where, decoders):
    _, width, count = decoders.shape

    def kernel(where_ref, source, a_ref, b_ref, sems):
        first = pltpu.make_async_copy(source.at[where_ref[3]], a_ref, sems.at[0])
        second = pltpu.make_async_copy(source.at[2], b_ref, sems.at[1])
        first.start()
        second.start()
        first.wait()
        second.wait()

    out = [((width, count), decoders.dtype)] * 2
    return call(kernel, where, [], [decoders], out, [pltpu.SemaphoreType.DMA((2,))])


def encode(where, pieces, shifts, weight, start, bias):
    size = 2 * weight.shape[0] // (2 * CHIPS)
    tokens = pieces[0].shape[1]
    width = weight.shape[1]
    count = len(shifts)
    vmem = list(pieces) + ([start] if start is not None else []) + ([bias] if bias is not None else [])

    def kernel(where_ref, *refs):
        pieces_refs, refs = refs[: len(pieces)], refs[len(pieces) :]
        if start is not None:
            start_ref, *refs = refs
        if bias is not None:
            bias_ref, *refs = refs
        weight_ref, out_ref, rows, sems = refs
        sign = 1 - 2 * where_ref[0]
        copies = []
        for i, shift in enumerate(shifts):
            at = (where_ref[1] + sign * shift) & (CHIPS - 1)
            copies.append(
                pltpu.make_async_copy(
                    weight_ref.at[pl.ds(pl.multiple_of(at * size, 16), size)],
                    rows.at[pl.ds(i * size, size)],
                    sems.at[i],
                )
            )
        for copy in copies:
            copy.start()
        block = jnp.concatenate([p[...] for p in pieces_refs]).T
        for copy in copies:
            copy.wait()
        hidden = jnp.dot(block, rows[...], preferred_element_type=jnp.float32)
        if start is not None:
            hidden = hidden + start_ref[...]
        if bias is not None:
            hidden = jnp.maximum(hidden + bias_ref[...], 0.0)
        out_ref[...] = hidden.astype(out_ref.dtype)

    out = [((tokens, width), jnp.float32 if bias is None else jnp.bfloat16)]
    scratch = [pltpu.VMEM((count * size, width), weight.dtype), pltpu.SemaphoreType.DMA((count,))]
    return call(kernel, where, vmem, [weight], out, scratch)[0]


def gather_and_encode(where, core, own, weight, bias):
    other = lax.ppermute(own, "feat", SWAP)
    block = jnp.where(core == 0, jnp.concatenate([own, other]), jnp.concatenate([other, own]))
    b1 = lax.ppermute(block, "feat", BOTH)
    b2 = lax.ppermute(b1, "feat", BOTH)
    s1 = lax.ppermute(b1, "feat", SWAP)
    b3 = lax.ppermute(b2, "feat", BOTH)
    s2 = lax.ppermute(b2, "feat", SWAP)
    sums = encode(where, [block, b1, s1], (0, -1, 1), weight, None, None)
    b4 = lax.ppermute(b3, "feat", BOTH)
    s3 = lax.ppermute(b3, "feat", SWAP)
    sums = encode(where, [b2, s2, b3], (-2, 2, -3), weight, sums, None)
    return encode(where, [s3, b4], (3, -4), weight, sums, bias)


def gather_rows(own):
    half = own.shape[0] // 2
    before = lax.ppermute(own, "row", ring(1))
    after = lax.ppermute(own, "row", ring(-1))
    first = lax.ppermute(before[:half], "row", ring(1))
    second = lax.ppermute(after[half:], "row", ring(-1))
    return own, before, after, first, second


def decode(where, rows, weights, start, split):
    tokens, count = rows[0].shape
    width = weights[0].shape[0]
    n = len(weights)
    has_start = start is not None

    def kernel(where_ref, own, before, after, first, second, *rest):
        core, chip, row = where_ref[0], where_ref[1], where_ref[2]
        weight = rest[0][...]
        for other in rest[1:n]:
            weight = weight + other[...]
        rest = rest[n:]
        if has_start:
            start_ref, *rest = rest
        if split:
            mine_ref, theirs_ref, turned = rest
        else:
            out_ref, turned = rest
        turned[...] = weight.T
        for j, parts in enumerate(((own,), (after,), (first, second), (before,))):
            block = parts[0][...] if len(parts) == 1 else jnp.concatenate([p[...] for p in parts])
            value = jnp.dot(block, turned[...], preferred_element_type=jnp.float32)
            if has_start:
                value = value + start_ref[j]
            if not split:
                out_ref[j] = value
                continue
            for h in range(2):
                at = (2 * ((row + j) & (ROWS - 1)) + h - chip) & (CHIPS - 1)
                low = value[2 * h * PIECE : (2 * h + 1) * PIECE]
                high = value[(2 * h + 1) * PIECE : (2 * h + 2) * PIECE]
                mine_ref[at] = jnp.where(core == 0, low, high)
                theirs_ref[at] = jnp.where(core == 0, high, low).astype(jnp.bfloat16)

    if split:
        shape = (CHIPS, PIECE, width)
        out = [(shape, jnp.float32), (shape, jnp.bfloat16)]
    else:
        out = [((ROWS, tokens, width), jnp.float32)]
    vmem = list(rows) + list(weights) + ([start] if has_start else [])
    return call(kernel, where, vmem, [], out, [pltpu.VMEM((count, width), jnp.bfloat16)])


def per_device(inputs, enc_weight, enc_bias, dec_weight, dec_bias):
    decoders = jnp.swapaxes(dec_weight[0], 1, 2)
    sec = lax.axis_index("sec")
    feat = lax.axis_index("feat")
    row = lax.axis_index("row")
    core, chip = feat & 1, feat >> 1
    where = jnp.stack([core, chip, row, jnp.where(sec == 3, 1, 0)]).astype(jnp.int32)

    lent_a, lent_b = copy_lent(where, decoders)
    lent_a = lax.ppermute(lent_a, "sec", [(2, 0), (3, 1)])
    lent_b = lax.ppermute(lent_b, "sec", [(3, 2)])

    features = gather_and_encode(where, core, inputs[0].T, enc_weight[0], enc_bias)

    every_own = gather_rows(features)
    brought_a = lax.ppermute(features, "sec", [(0, 1), (1, 2)])
    brought_b = lax.ppermute(features, "sec", [(0, 3)])
    every_brought = gather_rows(brought_a + brought_b)

    mine, theirs = decode(where, every_own, (lent_a, lent_b), None, True)
    pair = mine + lax.ppermute(theirs, "feat", SWAP).astype(jnp.float32)
    pair = pair.astype(jnp.bfloat16)
    back_a = lax.ppermute(pair, "sec", [(0, 2), (1, 3)])
    back_b = lax.ppermute(pair, "sec", [(2, 3)])

    late, _ = lax.optimization_barrier((decoders, features))
    own_weight = lax.dynamic_index_in_dim(late, sec, 0, keepdims=False)
    brought_weight = lax.dynamic_index_in_dim(late, jnp.where(sec == 2, 1, 0), 0, keepdims=False)
    (start,) = decode(where, every_own, (own_weight,), None, False)
    mine, theirs = decode(where, every_brought, (brought_weight,), start, True)
    pair = mine + lax.ppermute(theirs, "feat", SWAP).astype(jnp.float32)
    pair = pair + back_a.astype(jnp.float32) + back_b.astype(jnp.float32)
    send = pair.astype(jnp.bfloat16)
    got = [lax.ppermute(send[d], "feat", hop(d)) for d in (4, 3, 5, 2, 6, 1, 7)]
    total = pair[0]
    for g in got:
        total = total + g.astype(jnp.float32)
    return (total + dec_bias[0]).astype(jnp.bfloat16)[None]


def solution(mesh):
    in_specs = (
        P("sec", "row", "feat"),
        P("sec", None, "feat"),
        P("sec", "feat"),
        P("sec", None, "feat", "row"),
        P("sec", "row"),
    )
    out_specs = P("sec", "feat", "row")

    return jax.shard_map(per_device, mesh=mesh, in_specs=in_specs, out_specs=out_specs, check_vma=False)
```

time: 151 us -> 149 us (0.987)
  the two profiles are of different devices: /device:TPU:24 before, /device:TPU:6 now
where the time goes in v1:
time: 149 us; the launch traced here: 147 us
  waiting for transfers between devices  81.7 us (55%)
  starting transfers between devices  40 us (27%)
  Pallas kernels  15.1 us (10%)
  local copies, waits for them, and re-layouts  6.01 us (4%)
  other arithmetic  3.56 us (2%)
    ppermute x1, waiting for transfers between devices, per_device(): back_a = lax.ppermute(pair, 'sec', [(0, 2), (1, 3)])  17.9 us
    pallas_call x7, Pallas kernels, call(): pl.pallas_call(kernel, in_specs=[SMEM] + [VMEM] * len(vmem) + [ANY] * len...  15.1 us
    ppermute x7, starting transfers between devices, per_device(): got = [lax.ppermute(send[d], 'feat', hop(d)) for d in (4, 3, 5, 2, 6, 1, 7)]  13.8 us
    ppermute x1, waiting for transfers between devices, per_device(): brought_b = lax.ppermute(features, 'sec', [(0, 3)])  11.3 us
    ppermute x1, waiting for transfers between devices, per_device(): lent_b = lax.ppermute(lent_b, 'sec', [(3, 2)])  10.5 us
    ppermute x2, waiting for transfers between devices, gather_rows(): before = lax.ppermute(own, 'row', ring(1))  9.42 us
    ppermute x7, waiting for transfers between devices, per_device(): got = [lax.ppermute(send[d], 'feat', hop(d)) for d in (4, 3, 5, 2, 6, 1, 7)]  9.02 us
    ppermute x1, waiting for transfers between devices, gather_and_encode(): b1 = lax.ppermute(block, 'feat', BOTH)  7.06 us
  transfers between devices with their start and end apart: 31, of which 14 were waited for; matrix products, arithmetic and copies ran while one was open for 3% of the time, Pallas kernels for 10%

profile of v1, /device:TPU:6, one launch (start us, length us, event | category | flops | bytes accessed | tf_op | source)
XLA Modules:
  0.0 146.7 jit_solution(2109837802934984090)
XLA Ops:
  0.0 1.5 %collective-permute-done = bf16[144,256]{1,0:T(8,128)(2,1)S(1)} collective-permute-done((bf16[144,256]{1,0:T(8,128)(2,1)}, bf16[144,256]{1,0:T(8,128)(2,1)S(1)}, u32[]{:S(2)}, u32[]{:S(2)}) %collective-permute-start) | collective-permute-done | bytes 73760 | tf_op jit(solution)/shard_map/ppermute | solution.py:103
  1.5 1.0 maximum_select_fusion.refs_0_
  2.5 2.0 %collective-permute-start.1 = (bf16[288,256]{1,0:T(8,128)(2,1)S(1)}, bf16[288,256]{1,0:T(8,128)(2,1)S(1)}, u32[]{:S(2)}, u32[]{:S(2)}) collective-permute-start(bf16[288,256]{1,0:T(8,128)(2,1)S(1)} %maximum_select_fusion.refs_0_), channel_id=1, source_target_pairs={{0,8},{4,60},{8,16},{12,4},{16,24},{20,12},{24,32},{28,20},{32,40}... | collective-permute-start | bytes 442376 | tf_op jit(solution)/shard_map/ppermute | solution.py:105
  4.5 7.1 %collective-permute-done.1.refs_1_ = bf16[288,256]{1,0:T(8,128)(2,1)S(1)} collective-permute-done((bf16[288,256]{1,0:T(8,128)(2,1)S(1)}, bf16[288,256]{1,0:T(8,128)(2,1)S(1)}, u32[]{:S(2)}, u32[]{:S(2)}) %collective-permute-start.1) | collective-permute-done | bytes 147488 | tf_op jit(solution)/shard_map/ppermute | solution.py:105
  11.5 6.4 %collective-permute-done.2.refs_0_ = bf16[288,256]{1,0:T(8,128)(2,1)S(1)} collective-permute-done((bf16[288,256]{1,0:T(8,128)(2,1)S(1)}, bf16[288,256]{1,0:T(8,128)(2,1)S(1)}, u32[]{:S(2)}, u32[]{:S(2)}) %collective-permute-start.2) | collective-permute-done | bytes 147488 | tf_op jit(solution)/shard_map/ppermute | solution.py:106
  17.9 0.0 collective-permute-start.3
  17.9 0.8 collective-permute-start.7
  18.7 5.5 %collective-permute-done.3.refs_2_ = bf16[288,256]{1,0:T(8,128)(2,1)S(1)} collective-permute-done((bf16[288,256]{1,0:T(8,128)(2,1)S(1)}, bf16[288,256]{1,0:T(8,128)(2,1)S(1)}, u32[]{:S(2)}, u32[]{:S(2)}) %collective-permute-start.3) | collective-permute-done | bytes 147488 | tf_op jit(solution)/shard_map/ppermute | solution.py:108
  24.3 0.1 pad_add_fusion.where_ref
  24.3 2.3 %copy-done.1 = bf16[1,4,1024,576]{2,3,1,0:T(8,128)(2,1)S(1)} copy-done((bf16[1,4,1024,576]{2,3,1,0:T(8,128)(2,1)S(1)}, bf16[1,4,1024,576]{2,3,1,0:T(8,128)(2,1)}, u32[]{:S(2)}) %copy-start.1) | copy-done | bytes 4718616
  26.7 1.0 shard_map.60
  27.7 3.5 %collective-permute-start.19 = (bf16[576,1024]{1,0:T(8,128)(2,1)S(1)}, bf16[576,1024]{1,0:T(8,128)(2,1)S(1)}, u32[]{:S(2)}, u32[]{:S(2)}) collective-permute-start(bf16[576,1024]{1,0:T(8,128)(2,1)S(1)} %get-tuple-element.15), channel_id=1, source_target_pairs={{128,0},{192,64},{129,1},{193,65},{130,2},{194,66},{131,3},{195,67... | collective-permute-start | bytes 3538952 | tf_op jit(solution)/shard_map/ppermute | solution.py:178
  31.3 0.0 collective-permute-done.7.refs_2_
  31.3 1.8 %shard_map.55.refs_3_ = f32[256,1024]{1,0:T(8,128)S(1)} custom-call(s32[4]{0:T(128)S(1)} %pad_add_fusion.where_ref, bf16[288,256]{1,0:T(8,128)(2,1)S(1)} %maximum_select_fusion.refs_0_, bf16[288,256]{1,0:T(8,128)(2,1)S(1)} %collective-permute-done.1.refs_1_, bf16[288,256]{1,0:T(8,128)(2,1)S(1)} %collective-permute-done.7.refs_2_, bf16[2304,1024]{1,0:T(8,128)(2,1)S(1)} %bitcast.53), custom_call_target="tpu_custom_call" | custom-call | tf_op jit(solution)/shard_map/pallas_call | solution.py:35
  33.1 0.0 copy-start.10
  33.1 0.0 collective-permute-done.6.refs_1_
  33.1 1.8 %shard_map.56.refs_2_ = f32[256,1024]{1,0:T(8,128)S(1)} custom-call(s32[4]{0:T(128)S(1)} %pad_add_fusion.where_ref, bf16[288,256]{1,0:T(8,128)(2,1)S(1)} %collective-permute-done.2.refs_0_, bf16[288,256]{1,0:T(8,128)(2,1)S(1)} %collective-permute-done.6.refs_1_, bf16[288,256]{1,0:T(8,128)(2,1)S(1)} %collective-permute-done.3.refs_2_, ...), custom_call_target="tpu_custom_call" | custom-call | tf_op jit(solution)/shard_map/pallas_call | solution.py:35
  35.0 0.0 collective-permute-done.4.refs_0_
  35.0 1.5 %shard_map.57.own = bf16[256,1024]{1,0:T(8,128)(2,1)S(1)} custom-call(s32[4]{0:T(128)S(1)} %pad_add_fusion.where_ref, bf16[288,256]{1,0:T(8,128)(2,1)S(1)} %collective-permute-done.4.refs_0_, bf16[288,256]{1,0:T(8,128)(2,1)S(1)} %collective-permute-done.5.refs_1_, f32[256,1024]{1,0:T(8,128)S(1)} %shard_map.56.refs_2_, f32[1,1024]{1,0:T(1,128)S(1)} %copy-done.10, ...), custom_call_target="tpu_custom_call" | custom-call | tf_op jit(solution)/shard_map/pallas_call | solution.py:35
  36.5 1.7 %collective-permute-start.14 = (bf16[256,1024]{1,0:T(8,128)(2,1)S(1)}, bf16[256,1024]{1,0:T(8,128)(2,1)S(1)}, u32[]{:S(2)}, u32[]{:S(2)}) collective-permute-start(bf16[256,1024]{1,0:T(8,128)(2,1)S(1)} %shard_map.57.own), channel_id=1, source_target_pairs={{0,1},{1,2},{2,3},{3,0},{4,5},{5,6},{6,7},{7,4},{8,9},{9,10},{10,1... | collective-permute-start | bytes 1572872 | tf_op jit(solution)/shard_map/ppermute | solution.py:119
  38.2 1.9 %collective-permute-start.20 = (bf16[576,1024]{1,0:T(8,128)(2,1)S(1)}, bf16[576,1024]{1,0:T(8,128)(2,1)S(1)}, u32[]{:S(2)}, u32[]{:S(2)}) collective-permute-start(bf16[576,1024]{1,0:T(8,128)(2,1)S(1)} %get-tuple-element.16), channel_id=1, source_target_pairs={{192,128},{193,129},{194,130},{195,131},{196,132},{197,133},{198,1... | collective-permute-start | bytes 3538952 | tf_op jit(solution)/shard_map/ppermute | solution.py:179
  40.1 1.7 %collective-permute-start.15 = (bf16[256,1024]{1,0:T(8,128)(2,1)S(1)}, bf16[256,1024]{1,0:T(8,128)(2,1)S(1)}, u32[]{:S(2)}, u32[]{:S(2)}) collective-permute-start(bf16[256,1024]{1,0:T(8,128)(2,1)S(1)} %shard_map.57.own), channel_id=1, source_target_pairs={{0,3},{1,0},{2,1},{3,2},{4,7},{5,4},{6,5},{7,6},{8,11},{9,8},{10,9... | collective-permute-start | bytes 1572872 | tf_op jit(solution)/shard_map/ppermute | solution.py:120
  41.8 0.7 collective-permute-start.8
  42.5 9.4 %collective-permute-done.14.before = bf16[256,1024]{1,0:T(8,128)(2,1)S(1)} collective-permute-done((bf16[256,1024]{1,0:T(8,128)(2,1)S(1)}, bf16[256,1024]{1,0:T(8,128)(2,1)S(1)}, u32[]{:S(2)}, u32[]{:S(2)}) %collective-permute-start.14) | collective-permute-done | bytes 524320 | tf_op jit(solution)/shard_map/ppermute | solution.py:119
  51.9 1.3 collective-permute-start.9
  53.2 0.4 collective-permute-done.15.after
  53.7 1.6 %collective-permute-start.16 = (bf16[128,1024]{1,0:T(8,128)(2,1)S(1)}, bf16[128,1024]{1,0:T(8,128)(2,1)S(1)}, u32[]{:S(2)}, u32[]{:S(2)}) collective-permute-start(bf16[128,1024]{1,0:T(8,128)(2,1)S(1)} %slice.50), channel_id=1, source_target_pairs={{0,1},{1,2},{2,3},{3,0},{4,5},{5,6},{6,7},{7,4},{8,9},{9,10},{10,1... | collective-permute-start | bytes 786440 | tf_op jit(solution)/shard_map/ppermute | solution.py:121
  55.3 1.7 %collective-permute-start.17 = (bf16[128,1024]{1,0:T(8,128)(2,1)S(1)}, bf16[128,1024]{1,0:T(8,128)(2,1)S(1)}, u32[]{:S(2)}, u32[]{:S(2)}) collective-permute-start(bf16[128,1024]{1,0:T(8,128)(2,1)S(1)} %slice.51), channel_id=1, source_target_pairs={{0,3},{1,0},{2,1},{3,2},{4,7},{5,4},{6,5},{7,6},{8,11},{9,8},{10,9... | collective-permute-start | bytes 786440 | tf_op jit(solution)/shard_map/ppermute | solution.py:122
  57.0 11.3 %collective-permute-done.9 = bf16[256,1024]{1,0:T(8,128)(2,1)S(1)} collective-permute-done((bf16[256,1024]{1,0:T(8,128)(2,1)S(1)}, bf16[256,1024]{1,0:T(8,128)(2,1)S(1)}, u32[]{:S(2)}, u32[]{:S(2)}) %collective-permute-start.9) | collective-permute-done | bytes 524320 | tf_op jit(solution)/shard_map/ppermute | solution.py:185
  68.3 0.2 add.52.own
  68.5 0.3 collective-permute-start.10
  68.8 3.0 %collective-permute-start.11 = (bf16[256,1024]{1,0:T(8,128)(2,1)S(1)}, bf16[256,1024]{1,0:T(8,128)(2,1)S(1)}, u32[]{:S(2)}, u32[]{:S(2)}) collective-permute-start(bf16[256,1024]{1,0:T(8,128)(2,1)S(1)} %add.52.own), channel_id=1, source_target_pairs={{0,3},{1,0},{2,1},{3,2},{4,7},{5,4},{6,5},{7,6},{8,11},{9,8},{10,9... | collective-permute-start | bytes 1572872 | tf_op jit(solution)/shard_map/ppermute | solution.py:120
  71.8 10.5 %collective-permute-done.20.rest_1_ = bf16[576,1024]{1,0:T(8,128)(2,1)S(1)} collective-permute-done((bf16[576,1024]{1,0:T(8,128)(2,1)S(1)}, bf16[576,1024]{1,0:T(8,128)(2,1)S(1)}, u32[]{:S(2)}, u32[]{:S(2)}) %collective-permute-start.20) | collective-permute-done | bytes 1179680 | tf_op jit(solution)/shard_map/ppermute | solution.py:179
  82.3 0.0 collective-permute-done.16.first
  82.4 3.4 %shard_map.61 = (f32[8,64,576]{2,1,0:T(8,128)S(1)}, bf16[8,64,576]{2,1,0:T(8,128)(2,1)}) custom-call(s32[4]{0:T(128)S(1)} %pad_add_fusion.where_ref, bf16[256,1024]{1,0:T(8,128)(2,1)S(1)} %shard_map.57.own, bf16[256,1024]{1,0:T(8,128)(2,1)S(1)} %collective-permute-done.14.before, bf16[256,1024]{1,0:T(8,128)(2,1)S(1)} %collective-permute-done.15.after, ...), custom_call_target="tpu_custom_call" | custom-call | tf_op jit(solution)/shard_map/pallas_call | solution.py:35
  85.8 0.0 collective-permute-done.10.before
  85.8 0.8 slice.48
  86.6 1.6 %collective-permute-start.12 = (bf16[128,1024]{1,0:T(8,128)(2,1)}, bf16[128,1024]{1,0:T(8,128)(2,1)}, u32[]{:S(2)}, u32[]{:S(2)}) collective-permute-start(bf16[128,1024]{1,0:T(8,128)(2,1)} %slice.48), channel_id=1, source_target_pairs={{0,1},{1,2},{2,3},{3,0},{4,5},{5,6},{6,7},{7,4},{8,9},{9,10},{10,1... | collective-permute-start | bytes 786440 | tf_op jit(solution)/shard_map/ppermute | solution.py:121
  88.2 0.8 slice.49
  88.9 0.1 copy-done.4
  89.1 1.7 %collective-permute-start.13 = (bf16[128,1024]{1,0:T(8,128)(2,1)}, bf16[128,1024]{1,0:T(8,128)(2,1)}, u32[]{:S(2)}, u32[]{:S(2)}) collective-permute-start(bf16[128,1024]{1,0:T(8,128)(2,1)} %slice.49), channel_id=1, source_target_pairs={{0,3},{1,0},{2,1},{3,2},{4,7},{5,4},{6,5},{7,6},{8,11},{9,8},{10,9... | collective-permute-start | bytes 786440 | tf_op jit(solution)/shard_map/ppermute | solution.py:122
  90.7 1.9 %dynamic-slice_bitcast_fusion = (bf16[576,1024]{1,0:T(8,128)(2,1)S(1)}, bf16[576,1024]{1,0:T(8,128)(2,1)S(1)}) fusion(bf16[4,576,1024]{2,1,0:T(8,128)(2,1)} %bitcast.56, s32[]{:T(128)S(6)} %select_n.25, s32[]{:T(128)S(6)} %select_n.24), kind=kLoop, calls=%fused_computation.2 | loop fusion | bytes 4718600 | tf_op jit(solution)/shard_map/jit(dynamic_index_in_dim)/squeeze | solution.py:195
  92.7 2.5 %shard_map.58.rest_1_ = f32[4,256,576]{2,1,0:T(8,128)S(1)} custom-call(s32[4]{0:T(128)S(1)} %pad_add_fusion.where_ref, bf16[256,1024]{1,0:T(8,128)(2,1)S(1)} %shard_map.57.own, bf16[256,1024]{1,0:T(8,128)(2,1)S(1)} %collective-permute-done.14.before, bf16[256,1024]{1,0:T(8,128)(2,1)S(1)} %collective-permute-done.15.after, bf16[128,1024]{1,0:T(8,128)(2,1)S(1)} %copy-done.7, ...), custom_call_target="tpu_custom_call" | custom-call | tf_op jit(solution)/shard_map/pallas_call | solution.py:35
  95.1 1.7 %collective-permute-done.12.first = bf16[128,1024]{1,0:T(8,128)(2,1)} collective-permute-done((bf16[128,1024]{1,0:T(8,128)(2,1)}, bf16[128,1024]{1,0:T(8,128)(2,1)}, u32[]{:S(2)}, u32[]{:S(2)}) %collective-permute-start.12) | collective-permute-done | bytes 262176 | tf_op jit(solution)/shard_map/ppermute | solution.py:121
  96.9 0.9 collective-permute-done.13.second
  97.8 3.0 %shard_map.59 = (f32[8,64,576]{2,1,0:T(8,128)S(1)}, bf16[8,64,576]{2,1,0:T(8,128)(2,1)S(1)}) custom-call(s32[4]{0:T(128)S(1)} %pad_add_fusion.where_ref, bf16[256,1024]{1,0:T(8,128)(2,1)S(1)} %add.52.own, bf16[256,1024]{1,0:T(8,128)(2,1)S(1)} %copy-done.3, bf16[256,1024]{1,0:T(8,128)(2,1)S(1)} %copy-done.5, bf16[128,1024]{1,0:T(8,128)(2,1)} %collective-permute-done.12.first, ...), custom_call_target="tpu_custom_call" | custom-call | tf_op jit(solution)/shard_map/pallas_call | solution.py:35
  100.8 0.1 collective-permute-start.18
  100.9 1.2 add_convert_fusion
  102.1 1.3 collective-permute-start.22
  103.4 1.3 collective-permute-start.23
  104.7 17.9 %collective-permute-done.22 = bf16[8,64,576]{2,1,0:T(8,128)(2,1)S(1)} collective-permute-done((bf16[8,64,576]{2,1,0:T(8,128)(2,1)S(1)}, bf16[8,64,576]{2,1,0:T(8,128)(2,1)S(1)}, u32[]{:S(2)}, u32[]{:S(2)}) %collective-permute-start.22) | collective-permute-done | bytes 589856 | tf_op jit(solution)/shard_map/ppermute | solution.py:191
  122.6 0.0 collective-permute-done.23
  122.7 0.3 fusion.10
  123.0 0.1 slice_bitcast_fusion.7
  123.1 4.6 %collective-permute-start.24 = (bf16[64,576]{1,0:T(8,128)(2,1)S(1)}, bf16[64,576]{1,0:T(8,128)(2,1)S(1)}, u32[]{:S(2)}, u32[]{:S(2)}) collective-permute-start(bf16[64,576]{1,0:T(8,128)(2,1)S(1)} %get-tuple-element.23), channel_id=1, source_target_pairs={{0,32},{4,36},{8,40},{12,44},{16,48},{20,52},{24,56},{28,60},{32,0... | collective-permute-start | bytes 221192 | tf_op jit(solution)/shard_map/ppermute | solution.py:202
  127.7 0.0 collective-permute-start.25
  127.7 5.0 %collective-permute-start.26 = (bf16[64,576]{1,0:T(8,128)(2,1)S(1)}, bf16[64,576]{1,0:T(8,128)(2,1)S(1)}, u32[]{:S(2)}, u32[]{:S(2)}) collective-permute-start(bf16[64,576]{1,0:T(8,128)(2,1)S(1)} %get-tuple-element.28), channel_id=1, source_target_pairs={{0,40},{4,44},{8,48},{12,52},{16,56},{20,60},{24,0},{28,4},{32,8},... | collective-permute-start | bytes 221192 | tf_op jit(solution)/shard_map/ppermute | solution.py:202
  132.7 0.0 collective-permute-start.27
  132.7 4.1 %collective-permute-start.28 = (bf16[64,576]{1,0:T(8,128)(2,1)S(1)}, bf16[64,576]{1,0:T(8,128)(2,1)S(1)}, u32[]{:S(2)}, u32[]{:S(2)}) collective-permute-start(bf16[64,576]{1,0:T(8,128)(2,1)S(1)} %get-tuple-element.26), channel_id=1, source_target_pairs={{0,48},{4,52},{8,56},{12,60},{16,0},{20,4},{24,8},{28,12},{32,16},... | collective-permute-start | bytes 221192 | tf_op jit(solution)/shard_map/ppermute | solution.py:202
  136.9 4.6 %collective-permute-done.25 = bf16[64,576]{1,0:T(8,128)(2,1)S(1)} collective-permute-done((bf16[64,576]{1,0:T(8,128)(2,1)S(1)}, bf16[64,576]{1,0:T(8,128)(2,1)S(1)}, u32[]{:S(2)}, u32[]{:S(2)}) %collective-permute-start.25) | collective-permute-done | bytes 73760 | tf_op jit(solution)/shard_map/ppermute | solution.py:202
  141.5 0.0 collective-permute-start.30
  141.6 1.0 collective-permute-done.29
  142.5 3.4 %collective-permute-done.30 = bf16[64,576]{1,0:T(8,128)(2,1)S(1)} collective-permute-done((bf16[64,576]{1,0:T(8,128)(2,1)S(1)}, bf16[64,576]{1,0:T(8,128)(2,1)S(1)}, u32[]{:S(2)}, u32[]{:S(2)}) %collective-permute-start.30) | collective-permute-done | bytes 73760 | tf_op jit(solution)/shard_map/ppermute | solution.py:202
  146.0 0.7 fusion.9
  (42 shorter events, 0.1 us)
Async XLA Ops:
  0.0 1.5 %collective-permute-start = (bf16[144,256]{1,0:T(8,128)(2,1)}, bf16[144,256]{1,0:T(8,128)(2,1)S(1)}, u32[]{:S(2)}, u32[]{:S(2)}) collective-permute-start(bf16[144,256]{1,0:T(8,128)(2,1)} %bitcast.58), channel_id=1, source_target_pairs={{0,4},{4,0},{8,12},{12,8},{16,20},{20,16},{24,28},{28,24},{32,36},... | collective-permute-start | bytes 221192 | tf_op jit(solution)/shard_map/ppermute | solution.py:103
  2.5 9.1 %collective-permute-start.1 = (bf16[288,256]{1,0:T(8,128)(2,1)S(1)}, bf16[288,256]{1,0:T(8,128)(2,1)S(1)}, u32[]{:S(2)}, u32[]{:S(2)}) collective-permute-start(bf16[288,256]{1,0:T(8,128)(2,1)S(1)} %maximum_select_fusion.refs_0_), channel_id=1, source_target_pairs={{0,8},{4,60},{8,16},{12,4},{16,24},{20,12},{24,32},{28,20},{32,40}... | collective-permute-start | bytes 442376 | tf_op jit(solution)/shard_map/ppermute | solution.py:105
  11.5 6.4 %collective-permute-start.2 = (bf16[288,256]{1,0:T(8,128)(2,1)S(1)}, bf16[288,256]{1,0:T(8,128)(2,1)S(1)}, u32[]{:S(2)}, u32[]{:S(2)}) collective-permute-start(bf16[288,256]{1,0:T(8,128)(2,1)S(1)} %collective-permute-done.1.refs_1_), channel_id=1, source_target_pairs={{0,8},{4,60},{8,16},{12,4},{16,24},{20,12},{24,32},{28,20},{32,40}... | collective-permute-start | bytes 442376 | tf_op jit(solution)/shard_map/ppermute | solution.py:106
  17.9 6.4 %collective-permute-start.3 = (bf16[288,256]{1,0:T(8,128)(2,1)S(1)}, bf16[288,256]{1,0:T(8,128)(2,1)S(1)}, u32[]{:S(2)}, u32[]{:S(2)}) collective-permute-start(bf16[288,256]{1,0:T(8,128)(2,1)S(1)} %collective-permute-done.2.refs_0_), channel_id=1, source_target_pairs={{0,8},{4,60},{8,16},{12,4},{16,24},{20,12},{24,32},{28,20},{32,40}... | collective-permute-start | bytes 442376 | tf_op jit(solution)/shard_map/ppermute | solution.py:108
  17.9 13.4 %collective-permute-start.7 = (bf16[288,256]{1,0:T(8,128)(2,1)S(1)}, bf16[288,256]{1,0:T(8,128)(2,1)S(1)}, u32[]{:S(2)}, u32[]{:S(2)}) collective-permute-start(bf16[288,256]{1,0:T(8,128)(2,1)S(1)} %collective-permute-done.1.refs_1_), channel_id=1, source_target_pairs={{0,4},{4,0},{8,12},{12,8},{16,20},{20,16},{24,28},{28,24},{32,36},... | collective-permute-start | bytes 442376 | tf_op jit(solution)/shard_map/ppermute | solution.py:107
  18.7 14.4 %collective-permute-start.6 = (bf16[288,256]{1,0:T(8,128)(2,1)S(1)}, bf16[288,256]{1,0:T(8,128)(2,1)S(1)}, u32[]{:S(2)}, u32[]{:S(2)}) collective-permute-start(bf16[288,256]{1,0:T(8,128)(2,1)S(1)} %collective-permute-done.2.refs_0_), channel_id=1, source_target_pairs={{0,4},{4,0},{8,12},{12,8},{16,20},{20,16},{24,28},{28,24},{32,36},... | collective-permute-start | bytes 442376 | tf_op jit(solution)/shard_map/ppermute | solution.py:109
  24.2 10.7 %collective-permute-start.4 = (bf16[288,256]{1,0:T(8,128)(2,1)S(1)}, bf16[288,256]{1,0:T(8,128)(2,1)S(1)}, u32[]{:S(2)}, u32[]{:S(2)}) collective-permute-start(bf16[288,256]{1,0:T(8,128)(2,1)S(1)} %collective-permute-done.3.refs_2_), channel_id=1, source_target_pairs={{0,4},{4,0},{8,12},{12,8},{16,20},{20,16},{24,28},{28,24},{32,36},... | collective-permute-start | bytes 442376 | tf_op jit(solution)/shard_map/ppermute | solution.py:112
  24.3 10.7 %collective-permute-start.5 = (bf16[288,256]{1,0:T(8,128)(2,1)S(1)}, bf16[288,256]{1,0:T(8,128)(2,1)S(1)}, u32[]{:S(2)}, u32[]{:S(2)}) collective-permute-start(bf16[288,256]{1,0:T(8,128)(2,1)S(1)} %collective-permute-done.3.refs_2_), channel_id=1, source_target_pairs={{0,8},{4,60},{8,16},{12,4},{16,24},{20,12},{24,32},{28,20},{32,40}... | collective-permute-start | bytes 442376 | tf_op jit(solution)/shard_map/ppermute | solution.py:111
  24.3 2.3 %copy-start.1 = (bf16[1,4,1024,576]{2,3,1,0:T(8,128)(2,1)S(1)}, bf16[1,4,1024,576]{2,3,1,0:T(8,128)(2,1)}, u32[]{:S(2)}) copy-start(bf16[1,4,1024,576]{2,3,1,0:T(8,128)(2,1)} %param.8) | copy-start | bytes 14155780
  26.7 4.6 %copy-start = (bf16[1,2304,1024]{2,1,0:T(8,128)(2,1)S(1)}, bf16[1,2304,1024]{2,1,0:T(8,128)(2,1)}, u32[]{:S(2)}) copy-start(bf16[1,2304,1024]{2,1,0:T(8,128)(2,1)} %param.6) | copy-start | bytes 14155780
  27.7 41.1 %collective-permute-start.19 = (bf16[576,1024]{1,0:T(8,128)(2,1)S(1)}, bf16[576,1024]{1,0:T(8,128)(2,1)S(1)}, u32[]{:S(2)}, u32[]{:S(2)}) collective-permute-start(bf16[576,1024]{1,0:T(8,128)(2,1)S(1)} %get-tuple-element.15), channel_id=1, source_target_pairs={{128,0},{192,64},{129,1},{193,65},{130,2},{194,66},{131,3},{195,67... | collective-permute-start | bytes 3538952 | tf_op jit(solution)/shard_map/ppermute | solution.py:178
  33.1 1.9 %copy-start.10 = (f32[1,1024]{1,0:T(1,128)S(1)}, f32[1,1024]{1,0:T(1,128)}, u32[]{:S(2)}) copy-start(f32[1,1024]{1,0:T(1,128)} %refs_3_.1) | copy-start | bytes 12292
  36.5 15.4 %collective-permute-start.14 = (bf16[256,1024]{1,0:T(8,128)(2,1)S(1)}, bf16[256,1024]{1,0:T(8,128)(2,1)S(1)}, u32[]{:S(2)}, u32[]{:S(2)}) collective-permute-start(bf16[256,1024]{1,0:T(8,128)(2,1)S(1)} %shard_map.57.own), channel_id=1, source_target_pairs={{0,1},{1,2},{2,3},{3,0},{4,5},{5,6},{6,7},{7,4},{8,9},{9,10},{10,1... | collective-permute-start | bytes 1572872 | tf_op jit(solution)/shard_map/ppermute | solution.py:119
  38.2 44.2 %collective-permute-start.20 = (bf16[576,1024]{1,0:T(8,128)(2,1)S(1)}, bf16[576,1024]{1,0:T(8,128)(2,1)S(1)}, u32[]{:S(2)}, u32[]{:S(2)}) collective-permute-start(bf16[576,1024]{1,0:T(8,128)(2,1)S(1)} %get-tuple-element.16), channel_id=1, source_target_pairs={{192,128},{193,129},{194,130},{195,131},{196,132},{197,133},{198,1... | collective-permute-start | bytes 3538952 | tf_op jit(solution)/shard_map/ppermute | solution.py:179
  40.1 13.6 %collective-permute-start.15 = (bf16[256,1024]{1,0:T(8,128)(2,1)S(1)}, bf16[256,1024]{1,0:T(8,128)(2,1)S(1)}, u32[]{:S(2)}, u32[]{:S(2)}) collective-permute-start(bf16[256,1024]{1,0:T(8,128)(2,1)S(1)} %shard_map.57.own), channel_id=1, source_target_pairs={{0,3},{1,0},{2,1},{3,2},{4,7},{5,4},{6,5},{7,6},{8,11},{9,8},{10,9... | collective-permute-start | bytes 1572872 | tf_op jit(solution)/shard_map/ppermute | solution.py:120
  41.8 13.4 %collective-permute-start.8 = (bf16[256,1024]{1,0:T(8,128)(2,1)S(1)}, bf16[256,1024]{1,0:T(8,128)(2,1)S(1)}, u32[]{:S(2)}, u32[]{:S(2)}) collective-permute-start(bf16[256,1024]{1,0:T(8,128)(2,1)S(1)} %shard_map.57.own), channel_id=1, source_target_pairs={{0,64},{64,128},{1,65},{65,129},{2,66},{66,130},{3,67},{67,131},{4... | collective-permute-start | bytes 1572872 | tf_op jit(solution)/shard_map/ppermute | solution.py:184
  51.9 16.4 %collective-permute-start.9 = (bf16[256,1024]{1,0:T(8,128)(2,1)S(1)}, bf16[256,1024]{1,0:T(8,128)(2,1)S(1)}, u32[]{:S(2)}, u32[]{:S(2)}) collective-permute-start(bf16[256,1024]{1,0:T(8,128)(2,1)S(1)} %shard_map.57.own), channel_id=1, source_target_pairs={{0,192},{1,193},{2,194},{3,195},{4,196},{5,197},{6,198},{7,199},{8... | collective-permute-start | bytes 1572872 | tf_op jit(solution)/shard_map/ppermute | solution.py:185
  53.7 28.7 %collective-permute-start.16 = (bf16[128,1024]{1,0:T(8,128)(2,1)S(1)}, bf16[128,1024]{1,0:T(8,128)(2,1)S(1)}, u32[]{:S(2)}, u32[]{:S(2)}) collective-permute-start(bf16[128,1024]{1,0:T(8,128)(2,1)S(1)} %slice.50), channel_id=1, source_target_pairs={{0,1},{1,2},{2,3},{3,0},{4,5},{5,6},{6,7},{7,4},{8,9},{9,10},{10,1... | collective-permute-start | bytes 786440 | tf_op jit(solution)/shard_map/ppermute | solution.py:121
  55.3 27.1 %collective-permute-start.17 = (bf16[128,1024]{1,0:T(8,128)(2,1)S(1)}, bf16[128,1024]{1,0:T(8,128)(2,1)S(1)}, u32[]{:S(2)}, u32[]{:S(2)}) collective-permute-start(bf16[128,1024]{1,0:T(8,128)(2,1)S(1)} %slice.51), channel_id=1, source_target_pairs={{0,3},{1,0},{2,1},{3,2},{4,7},{5,4},{6,5},{7,6},{8,11},{9,8},{10,9... | collective-permute-start | bytes 786440 | tf_op jit(solution)/shard_map/ppermute | solution.py:122
  68.5 17.3 %collective-permute-start.10 = (bf16[256,1024]{1,0:T(8,128)(2,1)S(1)}, bf16[256,1024]{1,0:T(8,128)(2,1)S(1)}, u32[]{:S(2)}, u32[]{:S(2)}) collective-permute-start(bf16[256,1024]{1,0:T(8,128)(2,1)S(1)} %add.52.own), channel_id=1, source_target_pairs={{0,1},{1,2},{2,3},{3,0},{4,5},{5,6},{6,7},{7,4},{8,9},{9,10},{10,1... | collective-permute-start | bytes 1572872 | tf_op jit(solution)/shard_map/ppermute | solution.py:119
  68.8 19.3 %collective-permute-start.11 = (bf16[256,1024]{1,0:T(8,128)(2,1)S(1)}, bf16[256,1024]{1,0:T(8,128)(2,1)S(1)}, u32[]{:S(2)}, u32[]{:S(2)}) collective-permute-start(bf16[256,1024]{1,0:T(8,128)(2,1)S(1)} %add.52.own), channel_id=1, source_target_pairs={{0,3},{1,0},{2,1},{3,2},{4,7},{5,4},{6,5},{7,6},{8,11},{9,8},{10,9... | collective-permute-start | bytes 1572872 | tf_op jit(solution)/shard_map/ppermute | solution.py:120
  82.3 3.4 %copy-start.6 = (bf16[128,1024]{1,0:T(8,128)(2,1)}, bf16[128,1024]{1,0:T(8,128)(2,1)S(1)}, u32[]{:S(2)}) copy-start(bf16[128,1024]{1,0:T(8,128)(2,1)S(1)} %collective-permute-done.16.first) | copy-start | bytes 786436
  82.3 3.4 %copy-start.8 = (bf16[128,1024]{1,0:T(8,128)(2,1)}, bf16[128,1024]{1,0:T(8,128)(2,1)S(1)}, u32[]{:S(2)}) copy-start(bf16[128,1024]{1,0:T(8,128)(2,1)S(1)} %collective-permute-done.17.second) | copy-start | bytes 786436
  85.8 15.1 %collective-permute-start.21 = (bf16[8,64,576]{2,1,0:T(8,128)(2,1)}, bf16[8,64,576]{2,1,0:T(8,128)(2,1)}, u32[]{:S(2)}, u32[]{:S(2)}) collective-permute-start(bf16[8,64,576]{2,1,0:T(8,128)(2,1)} %get-tuple-element.18), channel_id=1, source_target_pairs={{0,4},{4,0},{8,12},{12,8},{16,20},{20,16},{24,28},{28,24},{32,36},... | collective-permute-start | bytes 1769480 | tf_op jit(solution)/shard_map/ppermute | solution.py:189
  85.8 2.3 %copy-start.2 = (bf16[256,1024]{1,0:T(8,128)(2,1)}, bf16[256,1024]{1,0:T(8,128)(2,1)S(1)}, u32[]{:S(2)}) copy-start(bf16[256,1024]{1,0:T(8,128)(2,1)S(1)} %collective-permute-done.10.before) | copy-start | bytes 1572868
  86.6 10.3 %collective-permute-start.12 = (bf16[128,1024]{1,0:T(8,128)(2,1)}, bf16[128,1024]{1,0:T(8,128)(2,1)}, u32[]{:S(2)}, u32[]{:S(2)}) collective-permute-start(bf16[128,1024]{1,0:T(8,128)(2,1)} %slice.48), channel_id=1, source_target_pairs={{0,1},{1,2},{2,3},{3,0},{4,5},{5,6},{6,7},{7,4},{8,9},{9,10},{10,1... | collective-permute-start | bytes 786440 | tf_op jit(solution)/shard_map/ppermute | solution.py:121
  88.2 0.9 copy-start.4
  89.1 8.7 %collective-permute-start.13 = (bf16[128,1024]{1,0:T(8,128)(2,1)}, bf16[128,1024]{1,0:T(8,128)(2,1)}, u32[]{:S(2)}, u32[]{:S(2)}) collective-permute-start(bf16[128,1024]{1,0:T(8,128)(2,1)} %slice.49), channel_id=1, source_target_pairs={{0,3},{1,0},{2,1},{3,2},{4,7},{5,4},{6,5},{7,6},{8,11},{9,8},{10,9... | collective-permute-start | bytes 786440 | tf_op jit(solution)/shard_map/ppermute | solution.py:122
  90.7 1.9 %copy-start.7 = (bf16[128,1024]{1,0:T(8,128)(2,1)S(1)}, bf16[128,1024]{1,0:T(8,128)(2,1)}, u32[]{:S(2)}) copy-start(bf16[128,1024]{1,0:T(8,128)(2,1)} %copy-done.6) | copy-start | bytes 786436
  90.7 1.9 %copy-start.9 = (bf16[128,1024]{1,0:T(8,128)(2,1)S(1)}, bf16[128,1024]{1,0:T(8,128)(2,1)}, u32[]{:S(2)}) copy-start(bf16[128,1024]{1,0:T(8,128)(2,1)} %copy-done.8) | copy-start | bytes 786436
  92.6 5.2 %copy-start.3 = (bf16[256,1024]{1,0:T(8,128)(2,1)S(1)}, bf16[256,1024]{1,0:T(8,128)(2,1)}, u32[]{:S(2)}) copy-start(bf16[256,1024]{1,0:T(8,128)(2,1)} %copy-done.2) | copy-start | bytes 1572868
  92.6 5.2 %copy-start.5 = (bf16[256,1024]{1,0:T(8,128)(2,1)S(1)}, bf16[256,1024]{1,0:T(8,128)(2,1)}, u32[]{:S(2)}) copy-start(bf16[256,1024]{1,0:T(8,128)(2,1)} %copy-done.4) | copy-start | bytes 1572868
  100.8 3.9 %collective-permute-start.18 = (bf16[8,64,576]{2,1,0:T(8,128)(2,1)S(1)}, bf16[8,64,576]{2,1,0:T(8,128)(2,1)S(1)}, u32[]{:S(2)}, u32[]{:S(2)}) collective-permute-start(bf16[8,64,576]{2,1,0:T(8,128)(2,1)S(1)} %get-tuple-element.14), channel_id=1, source_target_pairs={{0,4},{4,0},{8,12},{12,8},{16,20},{20,16},{24,28},{28,24},{32,36},... | collective-permute-start | bytes 1769480 | tf_op jit(solution)/shard_map/ppermute | solution.py:199
  102.1 20.5 %collective-permute-start.22 = (bf16[8,64,576]{2,1,0:T(8,128)(2,1)S(1)}, bf16[8,64,576]{2,1,0:T(8,128)(2,1)S(1)}, u32[]{:S(2)}, u32[]{:S(2)}) collective-permute-start(bf16[8,64,576]{2,1,0:T(8,128)(2,1)S(1)} %add_convert_fusion), channel_id=1, source_target_pairs={{0,128},{64,192},{1,129},{65,193},{2,130},{66,194},{3,131},{67,195... | collective-permute-start | bytes 1769480 | tf_op jit(solution)/shard_map/ppermute | solution.py:191
  103.4 19.2 %collective-permute-start.23 = (bf16[8,64,576]{2,1,0:T(8,128)(2,1)S(1)}, bf16[8,64,576]{2,1,0:T(8,128)(2,1)S(1)}, u32[]{:S(2)}, u32[]{:S(2)}) collective-permute-start(bf16[8,64,576]{2,1,0:T(8,128)(2,1)S(1)} %add_convert_fusion), channel_id=1, source_target_pairs={{128,192},{129,193},{130,194},{131,195},{132,196},{133,197},{134,1... | collective-permute-start | bytes 1769480 | tf_op jit(solution)/shard_map/ppermute | solution.py:192
  122.7 18.9 %copy-start.11 = (f32[1,576]{1,0:T(1,128)S(1)}, f32[1,576]{1,0:T(1,128)}, u32[]{:S(2)}) copy-start(f32[1,576]{1,0:T(1,128)} %param.9) | copy-start | bytes 6916
  123.1 13.8 %collective-permute-start.24 = (bf16[64,576]{1,0:T(8,128)(2,1)S(1)}, bf16[64,576]{1,0:T(8,128)(2,1)S(1)}, u32[]{:S(2)}, u32[]{:S(2)}) collective-permute-start(bf16[64,576]{1,0:T(8,128)(2,1)S(1)} %get-tuple-element.23), channel_id=1, source_target_pairs={{0,32},{4,36},{8,40},{12,44},{16,48},{20,52},{24,56},{28,60},{32,0... | collective-permute-start | bytes 221192 | tf_op jit(solution)/shard_map/ppermute | solution.py:202
  127.7 13.8 %collective-permute-start.25 = (bf16[64,576]{1,0:T(8,128)(2,1)S(1)}, bf16[64,576]{1,0:T(8,128)(2,1)S(1)}, u32[]{:S(2)}, u32[]{:S(2)}) collective-permute-start(bf16[64,576]{1,0:T(8,128)(2,1)S(1)} %get-tuple-element.29), channel_id=1, source_target_pairs={{0,24},{4,28},{8,32},{12,36},{16,40},{20,44},{24,48},{28,52},{32,5... | collective-permute-start | bytes 221192 | tf_op jit(solution)/shard_map/ppermute | solution.py:202
  127.7 13.8 %collective-permute-start.26 = (bf16[64,576]{1,0:T(8,128)(2,1)S(1)}, bf16[64,576]{1,0:T(8,128)(2,1)S(1)}, u32[]{:S(2)}, u32[]{:S(2)}) collective-permute-start(bf16[64,576]{1,0:T(8,128)(2,1)S(1)} %get-tuple-element.28), channel_id=1, source_target_pairs={{0,40},{4,44},{8,48},{12,52},{16,56},{20,60},{24,0},{28,4},{32,8},... | collective-permute-start | bytes 221192 | tf_op jit(solution)/shard_map/ppermute | solution.py:202
  132.7 8.8 %collective-permute-start.27 = (bf16[64,576]{1,0:T(8,128)(2,1)S(1)}, bf16[64,576]{1,0:T(8,128)(2,1)S(1)}, u32[]{:S(2)}, u32[]{:S(2)}) collective-permute-start(bf16[64,576]{1,0:T(8,128)(2,1)S(1)} %get-tuple-element.27), channel_id=1, source_target_pairs={{0,16},{4,20},{8,24},{12,28},{16,32},{20,36},{24,40},{28,44},{32,4... | collective-permute-start | bytes 221192 | tf_op jit(solution)/shard_map/ppermute | solution.py:202
  132.7 8.8 %collective-permute-start.28 = (bf16[64,576]{1,0:T(8,128)(2,1)S(1)}, bf16[64,576]{1,0:T(8,128)(2,1)S(1)}, u32[]{:S(2)}, u32[]{:S(2)}) collective-permute-start(bf16[64,576]{1,0:T(8,128)(2,1)S(1)} %get-tuple-element.26), channel_id=1, source_target_pairs={{0,48},{4,52},{8,56},{12,60},{16,0},{20,4},{24,8},{28,12},{32,16},... | collective-permute-start | bytes 221192 | tf_op jit(solution)/shard_map/ppermute | solution.py:202
  136.9 5.7 %collective-permute-start.29 = (bf16[64,576]{1,0:T(8,128)(2,1)S(1)}, bf16[64,576]{1,0:T(8,128)(2,1)S(1)}, u32[]{:S(2)}, u32[]{:S(2)}) collective-permute-start(bf16[64,576]{1,0:T(8,128)(2,1)S(1)} %get-tuple-element.25), channel_id=1, source_target_pairs={{0,8},{4,12},{8,16},{12,20},{16,24},{20,28},{24,32},{28,36},{32,40... | collective-permute-start | bytes 221192 | tf_op jit(solution)/shard_map/ppermute | solution.py:202
  141.5 4.4 %collective-permute-start.30 = (bf16[64,576]{1,0:T(8,128)(2,1)S(1)}, bf16[64,576]{1,0:T(8,128)(2,1)S(1)}, u32[]{:S(2)}, u32[]{:S(2)}) collective-permute-start(bf16[64,576]{1,0:T(8,128)(2,1)S(1)} %get-tuple-element.24), channel_id=1, source_target_pairs={{0,56},{4,60},{8,0},{12,4},{16,8},{20,12},{24,16},{28,20},{32,24},... | collective-permute-start | bytes 221192 | tf_op jit(solution)/shard_map/ppermute | solution.py:202

commit v2 on v1

--- a/solution.py
+++ b/solution.py
@@ -15,8 +15,8 @@
 PARAMS = pltpu.CompilerParams(vmem_limit_bytes=12 << 20)
 
 
-def ring(shift):
-    return [(i, (i + shift) % ROWS) for i in range(ROWS)]
+def ring(shift, sections=(0, 1, 2, 3)):
+    return [(s * ROWS + i, s * ROWS + (i + shift) % ROWS) for s in sections for i in range(ROWS)]
 
 
 def hop(shift):
@@ -54,6 +54,7 @@
         second.wait()
 
     out = [((width, count), decoders.dtype)] * 2
+    decoders = pltpu.with_memory_space_constraint(decoders, pltpu.HBM)
     return call(kernel, where, [], [decoders], out, [pltpu.SemaphoreType.DMA((2,))])
 
 
@@ -114,22 +115,32 @@
     return encode(where, [s3, b4], (3, -4), weight, sums, bias)
 
 
-def gather_rows(own):
+def gather_rows(own, sections):
     half = own.shape[0] // 2
-    before = lax.ppermute(own, "row", ring(1))
-    after = lax.ppermute(own, "row", ring(-1))
-    first = lax.ppermute(before[:half], "row", ring(1))
-    second = lax.ppermute(after[half:], "row", ring(-1))
+    axes = ("sec", "row")
+    before = lax.ppermute(own, axes, ring(1, sections))
+    after = lax.ppermute(own, axes, ring(-1, sections))
+    first = lax.ppermute(before[:half], axes, ring(1, sections))
+    second = lax.ppermute(after[half:], axes, ring(-1, sections))
     return own, before, after, first, second
 
 
-def decode(where, rows, weights, start, split):
+def decode(where, rows, weights, start, split, only=None):
     tokens, count = rows[0].shape
     width = weights[0].shape[0]
     n = len(weights)
     has_start = start is not None
 
     def kernel(where_ref, own, before, after, first, second, *rest):
+        if only is None:
+            work(where_ref, own, before, after, first, second, *rest)
+        else:
+
+            @pl.when(where_ref[4] == only)
+            def _():
+                work(where_ref, own, before, after, first, second, *rest)
+
+    def work(where_ref, own, before, after, first, second, *rest):
         core, chip, row = where_ref[0], where_ref[1], where_ref[2]
         weight = rest[0][...]
         for other in rest[1:n]:
@@ -172,32 +183,36 @@
     feat = lax.axis_index("feat")
     row = lax.axis_index("row")
     core, chip = feat & 1, feat >> 1
-    where = jnp.stack([core, chip, row, jnp.where(sec == 3, 1, 0)]).astype(jnp.int32)
+    where = jnp.stack([core, chip, row, jnp.where(sec == 2, 1, 0), sec]).astype(jnp.int32)
 
     lent_a, lent_b = copy_lent(where, decoders)
-    lent_a = lax.ppermute(lent_a, "sec", [(2, 0), (3, 1)])
+    lent_c = lax.ppermute(lent_a, "sec", [(1, 0)])
+    lent_a = lax.ppermute(lent_a, "sec", [(2, 1), (3, 0)])
     lent_b = lax.ppermute(lent_b, "sec", [(3, 2)])
 
     features = gather_and_encode(where, core, inputs[0].T, enc_weight[0], enc_bias)
 
-    every_own = gather_rows(features)
-    brought_a = lax.ppermute(features, "sec", [(0, 1), (1, 2)])
-    brought_b = lax.ppermute(features, "sec", [(0, 3)])
-    every_brought = gather_rows(brought_a + brought_b)
+    every_own = gather_rows(features, (0, 1, 2, 3))
+    brought = lax.ppermute(features, "sec", [(0, 2), (1, 3)])
+    every_brought = gather_rows(brought, (2, 3))
 
     mine, theirs = decode(where, every_own, (lent_a, lent_b), None, True)
     pair = mine + lax.ppermute(theirs, "feat", SWAP).astype(jnp.float32)
     pair = pair.astype(jnp.bfloat16)
-    back_a = lax.ppermute(pair, "sec", [(0, 2), (1, 3)])
+    back_a = lax.ppermute(pair, "sec", [(0, 3), (1, 2)])
     back_b = lax.ppermute(pair, "sec", [(2, 3)])
+    mine, theirs = decode(where, every_own, (lent_c,), None, True, only=0)
+    pair = mine + lax.ppermute(theirs, ("sec", "feat"), SWAP).astype(jnp.float32)
+    back_c = lax.ppermute(pair.astype(jnp.bfloat16), "sec", [(0, 1)])
 
     late, _ = lax.optimization_barrier((decoders, features))
     own_weight = lax.dynamic_index_in_dim(late, sec, 0, keepdims=False)
-    brought_weight = lax.dynamic_index_in_dim(late, jnp.where(sec == 2, 1, 0), 0, keepdims=False)
+    brought_weight = lax.dynamic_index_in_dim(late, jnp.where(sec == 3, 1, 0), 0, keepdims=False)
     (start,) = decode(where, every_own, (own_weight,), None, False)
     mine, theirs = decode(where, every_brought, (brought_weight,), start, True)
     pair = mine + lax.ppermute(theirs, "feat", SWAP).astype(jnp.float32)
-    pair = pair + back_a.astype(jnp.float32) + back_b.astype(jnp.float32)
+    for back in (back_a, back_b, back_c):
+        pair = pair + back.astype(jnp.float32)
     send = pair.astype(jnp.bfloat16)
     got = [lax.ppermute(send[d], "feat", hop(d)) for d in (4, 3, 5, 2, 6, 1, 7)]
     total = pair[0]

time: 149 us -> 156 us (1.047)
  the two profiles are of different devices: /device:TPU:6 before, /device:TPU:26 now
where the time goes in v2:
time: 156 us
  waiting for transfers between devices  75.6 us (48%)
  starting transfers between devices  50.8 us (33%)
  Pallas kernels  18.1 us (12%)
  local copies, waits for them, and re-layouts  6.24 us (4%)
  other arithmetic  4.79 us (3%)
    ppermute x1, waiting for transfers between devices, per_device(): brought = lax.ppermute(features, 'sec', [(0, 2), (1, 3)])  18.5 us
    pallas_call x8, Pallas kernels, call(): pl.pallas_call(kernel, in_specs=[SMEM] + [VMEM] * len(vmem) + [ANY] * len...  18.1 us
    ppermute x7, starting transfers between devices, per_device(): got = [lax.ppermute(send[d], 'feat', hop(d)) for d in (4, 3, 5, 2, 6, 1, 7)]  16 us
    ppermute x1, waiting for transfers between devices, per_device(): back_c = lax.ppermute(pair.astype(jnp.bfloat16), 'sec', [(0, 1)])  14.1 us
    ppermute x1, waiting for transfers between devices, per_device(): back_a = lax.ppermute(pair, 'sec', [(0, 3), (1, 2)])  11.3 us
    ppermute x1, starting transfers between devices, per_device(): back_a = lax.ppermute(pair, 'sec', [(0, 3), (1, 2)])  10.1 us
    ppermute x2, waiting for transfers between devices, gather_rows(): before = lax.ppermute(own, axes, ring(1, sections))  8.88 us
    ppermute x1, waiting for transfers between devices, gather_and_encode(): b1 = lax.ppermute(block, 'feat', BOTH)  7.06 us
  transfers between devices with their start and end apart: 33, of which 13 were waited for; matrix products, arithmetic and copies ran while one was open for 4% of the time, Pallas kernels for 12%

profile of v2, /device:TPU:26, one launch (start us, length us, event | category | flops | bytes accessed | tf_op | source)
XLA Modules:
  0.0 155.9 jit_solution(8916590910784629341)
XLA Ops:
  0.0 1.5 collective-permute-done
  1.5 1.0 maximum_select_fusion.refs_0_
  2.5 2.0 %collective-permute-start.1 = (bf16[288,256]{1,0:T(8,128)(2,1)S(1)}, bf16[288,256]{1,0:T(8,128)(2,1)S(1)}, u32[]{:S(2)}, u32[]{:S(2)}) collective-permute-start(bf16[288,256]{1,0:T(8,128)(2,1)S(1)} %maximum_select_fusion.refs_0_), channel_id=1, source_target_pairs={{0,8},{4,60},{8,16},{12,4},{16,24},{20,12},{24,32},{28,20},{32,40}... | collective-permute-start | bytes 442376 | tf_op jit(solution)/shard_map/ppermute | solution.py:106
  4.5 7.1 %collective-permute-done.1.refs_1_ = bf16[288,256]{1,0:T(8,128)(2,1)S(1)} collective-permute-done((bf16[288,256]{1,0:T(8,128)(2,1)S(1)}, bf16[288,256]{1,0:T(8,128)(2,1)S(1)}, u32[]{:S(2)}, u32[]{:S(2)}) %collective-permute-start.1) | collective-permute-done | bytes 147488 | tf_op jit(solution)/shard_map/ppermute | solution.py:106
  11.6 6.4 %collective-permute-done.2.refs_0_ = bf16[288,256]{1,0:T(8,128)(2,1)S(1)} collective-permute-done((bf16[288,256]{1,0:T(8,128)(2,1)S(1)}, bf16[288,256]{1,0:T(8,128)(2,1)S(1)}, u32[]{:S(2)}, u32[]{:S(2)}) %collective-permute-start.2) | collective-permute-done | bytes 147488 | tf_op jit(solution)/shard_map/ppermute | solution.py:107
  17.9 0.0 collective-permute-start.3
  17.9 0.8 collective-permute-start.7
  18.7 0.1 stack.23.where_ref
  18.8 2.5 %shard_map.60 = (bf16[576,1024]{1,0:T(8,128)(2,1)S(1)}, bf16[576,1024]{1,0:T(8,128)(2,1)S(1)}) custom-call(s32[5]{0:T(128)S(1)} %stack.23.where_ref, bf16[4,576,1024]{2,1,0:T(8,128)(2,1)} %bitcast.57), custom_call_target="tpu_custom_call" | custom-call | tf_op jit(solution)/shard_map/pallas_call | solution.py:35
  21.3 1.3 collective-permute-start.18
  22.6 0.1 collective-permute-start.6
  22.7 1.6 %collective-permute-done.3.refs_2_ = bf16[288,256]{1,0:T(8,128)(2,1)S(1)} collective-permute-done((bf16[288,256]{1,0:T(8,128)(2,1)S(1)}, bf16[288,256]{1,0:T(8,128)(2,1)S(1)}, u32[]{:S(2)}, u32[]{:S(2)}) %collective-permute-start.3) | collective-permute-done | bytes 147488 | tf_op jit(solution)/shard_map/ppermute | solution.py:109
  24.3 0.7 collective-permute-start.19
  25.0 1.8 %shard_map.55.refs_3_ = f32[256,1024]{1,0:T(8,128)S(1)} custom-call(s32[5]{0:T(128)S(1)} %stack.23.where_ref, bf16[288,256]{1,0:T(8,128)(2,1)S(1)} %maximum_select_fusion.refs_0_, bf16[288,256]{1,0:T(8,128)(2,1)S(1)} %collective-permute-done.1.refs_1_, bf16[288,256]{1,0:T(8,128)(2,1)S(1)} %collective-permute-done.7.refs_2_, bf16[2304,1024]{1,0:T(8,128)(2,1)S(1)} %bitcast.54), custom_call_target="tpu_custom_call" | custom-call | tf_op jit(solution)/shard_map/pallas_call | solution.py:35
  26.8 0.0 copy-start.9
  26.9 1.8 %shard_map.56.refs_2_ = f32[256,1024]{1,0:T(8,128)S(1)} custom-call(s32[5]{0:T(128)S(1)} %stack.23.where_ref, bf16[288,256]{1,0:T(8,128)(2,1)S(1)} %collective-permute-done.2.refs_0_, bf16[288,256]{1,0:T(8,128)(2,1)S(1)} %collective-permute-done.6.refs_1_, bf16[288,256]{1,0:T(8,128)(2,1)S(1)} %collective-permute-done.3.refs_2_, ...), custom_call_target="tpu_custom_call" | custom-call | tf_op jit(solution)/shard_map/pallas_call | solution.py:35
  28.7 0.0 collective-permute-done.4.refs_0_
  28.7 1.9 %collective-permute-done.5.refs_1_ = bf16[288,256]{1,0:T(8,128)(2,1)S(1)} collective-permute-done((bf16[288,256]{1,0:T(8,128)(2,1)S(1)}, bf16[288,256]{1,0:T(8,128)(2,1)S(1)}, u32[]{:S(2)}, u32[]{:S(2)}) %collective-permute-start.5) | collective-permute-done | bytes 147488 | tf_op jit(solution)/shard_map/ppermute | solution.py:112
  30.6 1.5 shard_map.57.own
  32.1 0.3 collective-permute-start.13
  32.4 2.5 %collective-permute-start.23 = (bf16[576,1024]{1,0:T(8,128)(2,1)S(1)}, bf16[576,1024]{1,0:T(8,128)(2,1)S(1)}, u32[]{:S(2)}, u32[]{:S(2)}) collective-permute-start(bf16[576,1024]{1,0:T(8,128)(2,1)S(1)} %get-tuple-element.17), channel_id=1, source_target_pairs={{64,0},{65,1},{66,2},{67,3},{68,4},{69,5},{70,6},{71,7},{72,8},{73... | collective-permute-start | bytes 3538952 | tf_op jit(solution)/shard_map/ppermute | solution.py:189
  35.0 1.9 %collective-permute-start.14 = (bf16[256,1024]{1,0:T(8,128)(2,1)S(1)}, bf16[256,1024]{1,0:T(8,128)(2,1)S(1)}, u32[]{:S(2)}, u32[]{:S(2)}) collective-permute-start(bf16[256,1024]{1,0:T(8,128)(2,1)S(1)} %shard_map.57.own), channel_id=1, source_target_pairs={{0,3},{1,0},{2,1},{3,2},{64,67},{65,64},{66,65},{67,66},{128,131},... | collective-permute-start | bytes 1572872 | tf_op jit(solution)/shard_map/ppermute | solution.py:122
  36.8 8.9 %collective-permute-done.13.before = bf16[256,1024]{1,0:T(8,128)(2,1)S(1)} collective-permute-done((bf16[256,1024]{1,0:T(8,128)(2,1)S(1)}, bf16[256,1024]{1,0:T(8,128)(2,1)S(1)}, u32[]{:S(2)}, u32[]{:S(2)}) %collective-permute-start.13) | collective-permute-done | bytes 524320 | tf_op jit(solution)/shard_map/ppermute | solution.py:121
  45.7 4.5 %collective-permute-start.8 = (bf16[256,1024]{1,0:T(8,128)(2,1)S(1)}, bf16[256,1024]{1,0:T(8,128)(2,1)S(1)}, u32[]{:S(2)}, u32[]{:S(2)}) collective-permute-start(bf16[256,1024]{1,0:T(8,128)(2,1)S(1)} %shard_map.57.own), channel_id=1, source_target_pairs={{0,128},{64,192},{1,129},{65,193},{2,130},{66,194},{3,131},{67,195... | collective-permute-start | bytes 1572872 | tf_op jit(solution)/shard_map/ppermute | solution.py:196
  50.3 1.4 collective-permute-start.15
  51.8 0.7 collective-permute-start.16
  52.5 18.5 %collective-permute-done.8.own = bf16[256,1024]{1,0:T(8,128)(2,1)S(1)} collective-permute-done((bf16[256,1024]{1,0:T(8,128)(2,1)S(1)}, bf16[256,1024]{1,0:T(8,128)(2,1)S(1)}, u32[]{:S(2)}, u32[]{:S(2)}) %collective-permute-start.8) | collective-permute-done | bytes 524320 | tf_op jit(solution)/shard_map/ppermute | solution.py:196
  71.0 0.7 collective-permute-start.9
  71.7 0.0 collective-permute-done.19.rest_1_
  71.7 0.9 collective-permute-start.10
  72.6 3.5 %shard_map.61 = (f32[8,64,576]{2,1,0:T(8,128)S(1)}, bf16[8,64,576]{2,1,0:T(8,128)(2,1)}) custom-call(s32[5]{0:T(128)S(1)} %stack.23.where_ref, bf16[256,1024]{1,0:T(8,128)(2,1)S(1)} %shard_map.57.own, bf16[256,1024]{1,0:T(8,128)(2,1)S(1)} %collective-permute-done.13.before, bf16[256,1024]{1,0:T(8,128)(2,1)S(1)} %collective-permute-done.14.after, ...), custom_call_target="tpu_custom_call" | custom-call | tf_op jit(solution)/shard_map/pallas_call | solution.py:35
  76.0 1.1 copy-done.1
  77.2 1.4 shard_map.62
  78.6 1.5 collective-permute-start.24
  80.1 0.7 slice.48
  80.8 0.8 copy-done.3
  81.6 1.4 collective-permute-start.11
  83.0 0.7 slice.49
  83.7 0.8 copy-done.5
  84.5 1.4 collective-permute-start.12
  85.9 1.8 %dynamic-slice_bitcast_fusion = (bf16[576,1024]{1,0:T(8,128)(2,1)S(1)}, bf16[576,1024]{1,0:T(8,128)(2,1)S(1)}) fusion(bf16[4,576,1024]{2,1,0:T(8,128)(2,1)} %bitcast.58, s32[]{:T(128)S(6)} %select_n.25, s32[]{:T(128)S(6)} %select_n.24), kind=kLoop, calls=%fused_computation.3 | loop fusion | bytes 4718600 | tf_op jit(solution)/shard_map/jit(dynamic_index_in_dim)/squeeze | solution.py:209
  87.8 2.5 %shard_map.58.rest_1_ = f32[4,256,576]{2,1,0:T(8,128)S(1)} custom-call(s32[5]{0:T(128)S(1)} %stack.23.where_ref, bf16[256,1024]{1,0:T(8,128)(2,1)S(1)} %shard_map.57.own, bf16[256,1024]{1,0:T(8,128)(2,1)S(1)} %collective-permute-done.13.before, bf16[256,1024]{1,0:T(8,128)(2,1)S(1)} %collective-permute-done.14.after, ...), custom_call_target="tpu_custom_call" | custom-call | tf_op jit(solution)/shard_map/pallas_call | solution.py:35
  90.3 3.1 %shard_map.59 = (f32[8,64,576]{2,1,0:T(8,128)S(1)}, bf16[8,64,576]{2,1,0:T(8,128)(2,1)S(1)}) custom-call(s32[5]{0:T(128)S(1)} %stack.23.where_ref, bf16[256,1024]{1,0:T(8,128)(2,1)S(1)} %copy-done.8, bf16[256,1024]{1,0:T(8,128)(2,1)S(1)} %copy-done.4, bf16[256,1024]{1,0:T(8,128)(2,1)S(1)} %copy-done.6, bf16[128,1024]{1,0:T(8,128)(2,1)} %collective-permute-done.11.first, ...), custom_call_target="tpu_custom_call" | custom-call | tf_op jit(solution)/shard_map/pallas_call | solution.py:35
  93.5 0.6 collective-permute-start.17
  94.0 1.3 add_convert_fusion.1
  95.3 10.1 %collective-permute-start.21 = (bf16[8,64,576]{2,1,0:T(8,128)(2,1)S(1)}, bf16[8,64,576]{2,1,0:T(8,128)(2,1)S(1)}, u32[]{:S(2)}, u32[]{:S(2)}) collective-permute-start(bf16[8,64,576]{2,1,0:T(8,128)(2,1)S(1)} %add_convert_fusion.1), channel_id=1, source_target_pairs={{0,192},{64,128},{1,193},{65,129},{2,194},{66,130},{3,195},{67,131... | collective-permute-start | bytes 1769480 | tf_op jit(solution)/shard_map/ppermute | solution.py:202
  105.4 0.7 collective-permute-start.22
  106.1 1.3 add_convert_fusion
  107.4 1.3 collective-permute-start.25
  108.7 11.3 %collective-permute-done.21 = bf16[8,64,576]{2,1,0:T(8,128)(2,1)S(1)} collective-permute-done((bf16[8,64,576]{2,1,0:T(8,128)(2,1)S(1)}, bf16[8,64,576]{2,1,0:T(8,128)(2,1)S(1)}, u32[]{:S(2)}, u32[]{:S(2)}) %collective-permute-start.21) | collective-permute-done | bytes 589856 | tf_op jit(solution)/shard_map/ppermute | solution.py:202
  120.0 14.1 %collective-permute-done.25 = bf16[8,64,576]{2,1,0:T(8,128)(2,1)S(1)} collective-permute-done((bf16[8,64,576]{2,1,0:T(8,128)(2,1)S(1)}, bf16[8,64,576]{2,1,0:T(8,128)(2,1)S(1)}, u32[]{:S(2)}, u32[]{:S(2)}) %collective-permute-start.25) | collective-permute-done | bytes 589856 | tf_op jit(solution)/shard_map/ppermute | solution.py:206
  134.1 0.5 fusion.10
  134.6 0.1 slice_bitcast_fusion.7
  134.7 4.7 %collective-permute-start.26 = (bf16[64,576]{1,0:T(8,128)(2,1)S(1)}, bf16[64,576]{1,0:T(8,128)(2,1)S(1)}, u32[]{:S(2)}, u32[]{:S(2)}) collective-permute-start(bf16[64,576]{1,0:T(8,128)(2,1)S(1)} %get-tuple-element.27), channel_id=1, source_target_pairs={{0,32},{4,36},{8,40},{12,44},{16,48},{20,52},{24,56},{28,60},{32,0... | collective-permute-start | bytes 221192 | tf_op jit(solution)/shard_map/ppermute | solution.py:217
  139.3 0.0 collective-permute-start.27
  139.4 5.0 %collective-permute-start.28 = (bf16[64,576]{1,0:T(8,128)(2,1)S(1)}, bf16[64,576]{1,0:T(8,128)(2,1)S(1)}, u32[]{:S(2)}, u32[]{:S(2)}) collective-permute-start(bf16[64,576]{1,0:T(8,128)(2,1)S(1)} %get-tuple-element.32), channel_id=1, source_target_pairs={{0,40},{4,44},{8,48},{12,52},{16,56},{20,60},{24,0},{28,4},{32,8},... | collective-permute-start | bytes 221192 | tf_op jit(solution)/shard_map/ppermute | solution.py:217
  144.4 4.1 %collective-permute-start.30 = (bf16[64,576]{1,0:T(8,128)(2,1)S(1)}, bf16[64,576]{1,0:T(8,128)(2,1)S(1)}, u32[]{:S(2)}, u32[]{:S(2)}) collective-permute-start(bf16[64,576]{1,0:T(8,128)(2,1)S(1)} %get-tuple-element.30), channel_id=1, source_target_pairs={{0,48},{4,52},{8,56},{12,60},{16,0},{20,4},{24,8},{28,12},{32,16},... | collective-permute-start | bytes 221192 | tf_op jit(solution)/shard_map/ppermute | solution.py:217
  148.5 1.1 collective-permute-start.31
  149.6 1.1 collective-permute-done.27
  150.7 1.0 collective-permute-start.32
  151.8 2.4 %collective-permute-done.29 = bf16[64,576]{1,0:T(8,128)(2,1)S(1)} collective-permute-done((bf16[64,576]{1,0:T(8,128)(2,1)S(1)}, bf16[64,576]{1,0:T(8,128)(2,1)S(1)}, u32[]{:S(2)}, u32[]{:S(2)}) %collective-permute-start.29) | collective-permute-done | bytes 73760 | tf_op jit(solution)/shard_map/ppermute | solution.py:217
  154.2 0.4 collective-permute-done.31
  154.6 0.6 collective-permute-done.32
  155.2 0.7 fusion.9
  (45 shorter events, 0.1 us)
Async XLA Ops:
  0.0 1.5 collective-permute-start
  2.5 9.1 %collective-permute-start.1 = (bf16[288,256]{1,0:T(8,128)(2,1)S(1)}, bf16[288,256]{1,0:T(8,128)(2,1)S(1)}, u32[]{:S(2)}, u32[]{:S(2)}) collective-permute-start(bf16[288,256]{1,0:T(8,128)(2,1)S(1)} %maximum_select_fusion.refs_0_), channel_id=1, source_target_pairs={{0,8},{4,60},{8,16},{12,4},{16,24},{20,12},{24,32},{28,20},{32,40}... | collective-permute-start | bytes 442376 | tf_op jit(solution)/shard_map/ppermute | solution.py:106
  11.5 6.4 %collective-permute-start.2 = (bf16[288,256]{1,0:T(8,128)(2,1)S(1)}, bf16[288,256]{1,0:T(8,128)(2,1)S(1)}, u32[]{:S(2)}, u32[]{:S(2)}) collective-permute-start(bf16[288,256]{1,0:T(8,128)(2,1)S(1)} %collective-permute-done.1.refs_1_), channel_id=1, source_target_pairs={{0,8},{4,60},{8,16},{12,4},{16,24},{20,12},{24,32},{28,20},{32,40}... | collective-permute-start | bytes 442376 | tf_op jit(solution)/shard_map/ppermute | solution.py:107
  17.9 6.4 %collective-permute-start.3 = (bf16[288,256]{1,0:T(8,128)(2,1)S(1)}, bf16[288,256]{1,0:T(8,128)(2,1)S(1)}, u32[]{:S(2)}, u32[]{:S(2)}) collective-permute-start(bf16[288,256]{1,0:T(8,128)(2,1)S(1)} %collective-permute-done.2.refs_0_), channel_id=1, source_target_pairs={{0,8},{4,60},{8,16},{12,4},{16,24},{20,12},{24,32},{28,20},{32,40}... | collective-permute-start | bytes 442376 | tf_op jit(solution)/shard_map/ppermute | solution.py:109
  17.9 6.4 %collective-permute-start.7 = (bf16[288,256]{1,0:T(8,128)(2,1)S(1)}, bf16[288,256]{1,0:T(8,128)(2,1)S(1)}, u32[]{:S(2)}, u32[]{:S(2)}) collective-permute-start(bf16[288,256]{1,0:T(8,128)(2,1)S(1)} %collective-permute-done.1.refs_1_), channel_id=1, source_target_pairs={{0,4},{4,0},{8,12},{12,8},{16,20},{20,16},{24,28},{28,24},{32,36},... | collective-permute-start | bytes 442376 | tf_op jit(solution)/shard_map/ppermute | solution.py:108
  18.8 6.2 %copy-start = (bf16[1,2304,1024]{2,1,0:T(8,128)(2,1)S(1)}, bf16[1,2304,1024]{2,1,0:T(8,128)(2,1)}, u32[]{:S(2)}) copy-start(bf16[1,2304,1024]{2,1,0:T(8,128)(2,1)} %param.6) | copy-start | bytes 14155780
  21.3 30.5 %collective-permute-start.18 = (bf16[576,1024]{1,0:T(8,128)(2,1)S(1)}, bf16[576,1024]{1,0:T(8,128)(2,1)S(1)}, u32[]{:S(2)}, u32[]{:S(2)}) collective-permute-start(bf16[576,1024]{1,0:T(8,128)(2,1)S(1)} %get-tuple-element.17), channel_id=1, source_target_pairs={{128,64},{192,0},{129,65},{193,1},{130,66},{194,2},{131,67},{195,3... | collective-permute-start | bytes 3538952 | tf_op jit(solution)/shard_map/ppermute | solution.py:190
  22.6 4.3 %collective-permute-start.6 = (bf16[288,256]{1,0:T(8,128)(2,1)S(1)}, bf16[288,256]{1,0:T(8,128)(2,1)S(1)}, u32[]{:S(2)}, u32[]{:S(2)}) collective-permute-start(bf16[288,256]{1,0:T(8,128)(2,1)S(1)} %collective-permute-done.2.refs_0_), channel_id=1, source_target_pairs={{0,4},{4,0},{8,12},{12,8},{16,20},{20,16},{24,28},{28,24},{32,36},... | collective-permute-start | bytes 442376 | tf_op jit(solution)/shard_map/ppermute | solution.py:110
  24.3 4.5 %collective-permute-start.4 = (bf16[288,256]{1,0:T(8,128)(2,1)S(1)}, bf16[288,256]{1,0:T(8,128)(2,1)S(1)}, u32[]{:S(2)}, u32[]{:S(2)}) collective-permute-start(bf16[288,256]{1,0:T(8,128)(2,1)S(1)} %collective-permute-done.3.refs_2_), channel_id=1, source_target_pairs={{0,4},{4,0},{8,12},{12,8},{16,20},{20,16},{24,28},{28,24},{32,36},... | collective-permute-start | bytes 442376 | tf_op jit(solution)/shard_map/ppermute | solution.py:113
  24.3 6.4 %collective-permute-start.5 = (bf16[288,256]{1,0:T(8,128)(2,1)S(1)}, bf16[288,256]{1,0:T(8,128)(2,1)S(1)}, u32[]{:S(2)}, u32[]{:S(2)}) collective-permute-start(bf16[288,256]{1,0:T(8,128)(2,1)S(1)} %collective-permute-done.3.refs_2_), channel_id=1, source_target_pairs={{0,8},{4,60},{8,16},{12,4},{16,24},{20,12},{24,32},{28,20},{32,40}... | collective-permute-start | bytes 442376 | tf_op jit(solution)/shard_map/ppermute | solution.py:112
  24.3 47.4 %collective-permute-start.19 = (bf16[576,1024]{1,0:T(8,128)(2,1)S(1)}, bf16[576,1024]{1,0:T(8,128)(2,1)S(1)}, u32[]{:S(2)}, u32[]{:S(2)}) collective-permute-start(bf16[576,1024]{1,0:T(8,128)(2,1)S(1)} %get-tuple-element.18), channel_id=1, source_target_pairs={{192,128},{193,129},{194,130},{195,131},{196,132},{197,133},{198,1... | collective-permute-start | bytes 3538952 | tf_op jit(solution)/shard_map/ppermute | solution.py:191
  26.8 3.8 %copy-start.9 = (f32[1,1024]{1,0:T(1,128)S(1)}, f32[1,1024]{1,0:T(1,128)}, u32[]{:S(2)}) copy-start(f32[1,1024]{1,0:T(1,128)} %refs_3_.1) | copy-start | bytes 12292
  32.1 13.6 %collective-permute-start.13 = (bf16[256,1024]{1,0:T(8,128)(2,1)S(1)}, bf16[256,1024]{1,0:T(8,128)(2,1)S(1)}, u32[]{:S(2)}, u32[]{:S(2)}) collective-permute-start(bf16[256,1024]{1,0:T(8,128)(2,1)S(1)} %shard_map.57.own), channel_id=1, source_target_pairs={{0,1},{1,2},{2,3},{3,0},{64,65},{65,66},{66,67},{67,64},{128,129},... | collective-permute-start | bytes 1572872 | tf_op jit(solution)/shard_map/ppermute | solution.py:121
  32.4 44.7 %collective-permute-start.23 = (bf16[576,1024]{1,0:T(8,128)(2,1)S(1)}, bf16[576,1024]{1,0:T(8,128)(2,1)S(1)}, u32[]{:S(2)}, u32[]{:S(2)}) collective-permute-start(bf16[576,1024]{1,0:T(8,128)(2,1)S(1)} %get-tuple-element.17), channel_id=1, source_target_pairs={{64,0},{65,1},{66,2},{67,3},{68,4},{69,5},{70,6},{71,7},{72,8},{73... | collective-permute-start | bytes 3538952 | tf_op jit(solution)/shard_map/ppermute | solution.py:189
  35.0 15.3 %collective-permute-start.14 = (bf16[256,1024]{1,0:T(8,128)(2,1)S(1)}, bf16[256,1024]{1,0:T(8,128)(2,1)S(1)}, u32[]{:S(2)}, u32[]{:S(2)}) collective-permute-start(bf16[256,1024]{1,0:T(8,128)(2,1)S(1)} %shard_map.57.own), channel_id=1, source_target_pairs={{0,3},{1,0},{2,1},{3,2},{64,67},{65,64},{66,65},{67,66},{128,131},... | collective-permute-start | bytes 1572872 | tf_op jit(solution)/shard_map/ppermute | solution.py:122
  45.7 25.2 %collective-permute-start.8 = (bf16[256,1024]{1,0:T(8,128)(2,1)S(1)}, bf16[256,1024]{1,0:T(8,128)(2,1)S(1)}, u32[]{:S(2)}, u32[]{:S(2)}) collective-permute-start(bf16[256,1024]{1,0:T(8,128)(2,1)S(1)} %shard_map.57.own), channel_id=1, source_target_pairs={{0,128},{64,192},{1,129},{65,193},{2,130},{66,194},{3,131},{67,195... | collective-permute-start | bytes 1572872 | tf_op jit(solution)/shard_map/ppermute | solution.py:196
  50.3 22.3 %collective-permute-start.15 = (bf16[128,1024]{1,0:T(8,128)(2,1)S(1)}, bf16[128,1024]{1,0:T(8,128)(2,1)S(1)}, u32[]{:S(2)}, u32[]{:S(2)}) collective-permute-start(bf16[128,1024]{1,0:T(8,128)(2,1)S(1)} %slice.50), channel_id=1, source_target_pairs={{0,1},{1,2},{2,3},{3,0},{64,65},{65,66},{66,67},{67,64},{128,129},... | collective-permute-start | bytes 786440 | tf_op jit(solution)/shard_map/ppermute | solution.py:123
  51.8 20.8 %collective-permute-start.16 = (bf16[128,1024]{1,0:T(8,128)(2,1)S(1)}, bf16[128,1024]{1,0:T(8,128)(2,1)S(1)}, u32[]{:S(2)}, u32[]{:S(2)}) collective-permute-start(bf16[128,1024]{1,0:T(8,128)(2,1)S(1)} %slice.51), channel_id=1, source_target_pairs={{0,3},{1,0},{2,1},{3,2},{64,67},{65,64},{66,65},{67,66},{128,131},... | collective-permute-start | bytes 786440 | tf_op jit(solution)/shard_map/ppermute | solution.py:124
  71.0 5.1 %copy-start.7 = (bf16[256,1024]{1,0:T(8,128)(2,1)}, bf16[256,1024]{1,0:T(8,128)(2,1)S(1)}, u32[]{:S(2)}) copy-start(bf16[256,1024]{1,0:T(8,128)(2,1)S(1)} %collective-permute-done.8.own) | copy-start | bytes 1572868
  71.0 9.1 %collective-permute-start.9 = (bf16[256,1024]{1,0:T(8,128)(2,1)S(1)}, bf16[256,1024]{1,0:T(8,128)(2,1)S(1)}, u32[]{:S(2)}, u32[]{:S(2)}) collective-permute-start(bf16[256,1024]{1,0:T(8,128)(2,1)S(1)} %collective-permute-done.8.own), channel_id=1, source_target_pairs={{128,129},{129,130},{130,131},{131,128},{192,193},{193,194},{194,1... | collective-permute-start | bytes 1572872 | tf_op jit(solution)/shard_map/ppermute | solution.py:121
  71.7 11.3 %collective-permute-start.10 = (bf16[256,1024]{1,0:T(8,128)(2,1)S(1)}, bf16[256,1024]{1,0:T(8,128)(2,1)S(1)}, u32[]{:S(2)}, u32[]{:S(2)}) collective-permute-start(bf16[256,1024]{1,0:T(8,128)(2,1)S(1)} %collective-permute-done.8.own), channel_id=1, source_target_pairs={{128,131},{129,128},{130,129},{131,130},{192,195},{193,192},{194,1... | collective-permute-start | bytes 1572872 | tf_op jit(solution)/shard_map/ppermute | solution.py:122
  76.0 1.1 copy-start.1
  77.2 16.9 %collective-permute-start.20 = (bf16[8,64,576]{2,1,0:T(8,128)(2,1)}, bf16[8,64,576]{2,1,0:T(8,128)(2,1)}, u32[]{:S(2)}, u32[]{:S(2)}) collective-permute-start(bf16[8,64,576]{2,1,0:T(8,128)(2,1)} %get-tuple-element.20), channel_id=1, source_target_pairs={{0,4},{4,0},{8,12},{12,8},{16,20},{20,16},{24,28},{28,24},{32,36},... | collective-permute-start | bytes 1769480 | tf_op jit(solution)/shard_map/ppermute | solution.py:200
  78.6 27.6 %collective-permute-start.24 = (bf16[8,64,576]{2,1,0:T(8,128)(2,1)}, bf16[8,64,576]{2,1,0:T(8,128)(2,1)}, u32[]{:S(2)}, u32[]{:S(2)}) collective-permute-start(bf16[8,64,576]{2,1,0:T(8,128)(2,1)} %get-tuple-element.22), channel_id=1, source_target_pairs={{0,4},{4,0},{8,12},{12,8},{16,20},{20,16},{24,28},{28,24},{32,36},... | collective-permute-start | bytes 1769480 | tf_op jit(solution)/shard_map/ppermute | solution.py:205
  80.8 0.8 copy-start.3
  81.6 8.6 %collective-permute-start.11 = (bf16[128,1024]{1,0:T(8,128)(2,1)}, bf16[128,1024]{1,0:T(8,128)(2,1)}, u32[]{:S(2)}, u32[]{:S(2)}) collective-permute-start(bf16[128,1024]{1,0:T(8,128)(2,1)} %slice.48), channel_id=1, source_target_pairs={{128,129},{129,130},{130,131},{131,128},{192,193},{193,194},{194,1... | collective-permute-start | bytes 786440 | tf_op jit(solution)/shard_map/ppermute | solution.py:123
  83.7 0.8 copy-start.5
  84.5 5.7 %collective-permute-start.12 = (bf16[128,1024]{1,0:T(8,128)(2,1)}, bf16[128,1024]{1,0:T(8,128)(2,1)}, u32[]{:S(2)}, u32[]{:S(2)}) collective-permute-start(bf16[128,1024]{1,0:T(8,128)(2,1)} %slice.49), channel_id=1, source_target_pairs={{128,131},{129,128},{130,129},{131,130},{192,195},{193,192},{194,1... | collective-permute-start | bytes 786440 | tf_op jit(solution)/shard_map/ppermute | solution.py:124
  87.7 2.5 %copy-start.4 = (bf16[256,1024]{1,0:T(8,128)(2,1)S(1)}, bf16[256,1024]{1,0:T(8,128)(2,1)}, u32[]{:S(2)}) copy-start(bf16[256,1024]{1,0:T(8,128)(2,1)} %copy-done.3) | copy-start | bytes 1572868
  87.7 2.5 %copy-start.6 = (bf16[256,1024]{1,0:T(8,128)(2,1)S(1)}, bf16[256,1024]{1,0:T(8,128)(2,1)}, u32[]{:S(2)}) copy-start(bf16[256,1024]{1,0:T(8,128)(2,1)} %copy-done.5) | copy-start | bytes 1572868
  87.8 2.5 %copy-start.8 = (bf16[256,1024]{1,0:T(8,128)(2,1)S(1)}, bf16[256,1024]{1,0:T(8,128)(2,1)}, u32[]{:S(2)}) copy-start(bf16[256,1024]{1,0:T(8,128)(2,1)} %copy-done.7) | copy-start | bytes 1572868
  90.3 3.8 %copy-start.2 = (f32[8,64,576]{2,1,0:T(8,128)S(1)}, f32[8,64,576]{2,1,0:T(8,128)}, u32[]{:S(2)}) copy-start(f32[8,64,576]{2,1,0:T(8,128)} %copy-done.1) | copy-start | bytes 3538948
  93.5 15.3 %collective-permute-start.17 = (bf16[8,64,576]{2,1,0:T(8,128)(2,1)S(1)}, bf16[8,64,576]{2,1,0:T(8,128)(2,1)S(1)}, u32[]{:S(2)}, u32[]{:S(2)}) collective-permute-start(bf16[8,64,576]{2,1,0:T(8,128)(2,1)S(1)} %get-tuple-element.16), channel_id=1, source_target_pairs={{0,4},{4,0},{8,12},{12,8},{16,20},{20,16},{24,28},{28,24},{32,36},... | collective-permute-start | bytes 1769480 | tf_op jit(solution)/shard_map/ppermute | solution.py:213
  95.3 24.7 %collective-permute-start.21 = (bf16[8,64,576]{2,1,0:T(8,128)(2,1)S(1)}, bf16[8,64,576]{2,1,0:T(8,128)(2,1)S(1)}, u32[]{:S(2)}, u32[]{:S(2)}) collective-permute-start(bf16[8,64,576]{2,1,0:T(8,128)(2,1)S(1)} %add_convert_fusion.1), channel_id=1, source_target_pairs={{0,192},{64,128},{1,193},{65,129},{2,194},{66,130},{3,195},{67,131... | collective-permute-start | bytes 1769480 | tf_op jit(solution)/shard_map/ppermute | solution.py:202
  105.4 14.6 %collective-permute-start.22 = (bf16[8,64,576]{2,1,0:T(8,128)(2,1)S(1)}, bf16[8,64,576]{2,1,0:T(8,128)(2,1)S(1)}, u32[]{:S(2)}, u32[]{:S(2)}) collective-permute-start(bf16[8,64,576]{2,1,0:T(8,128)(2,1)S(1)} %add_convert_fusion.1), channel_id=1, source_target_pairs={{128,192},{129,193},{130,194},{131,195},{132,196},{133,197},{134,1... | collective-permute-start | bytes 1769480 | tf_op jit(solution)/shard_map/ppermute | solution.py:203
  107.4 26.7 %collective-permute-start.25 = (bf16[8,64,576]{2,1,0:T(8,128)(2,1)S(1)}, bf16[8,64,576]{2,1,0:T(8,128)(2,1)S(1)}, u32[]{:S(2)}, u32[]{:S(2)}) collective-permute-start(bf16[8,64,576]{2,1,0:T(8,128)(2,1)S(1)} %add_convert_fusion), channel_id=1, source_target_pairs={{0,64},{1,65},{2,66},{3,67},{4,68},{5,69},{6,70},{7,71},{8,72},{9,... | collective-permute-start | bytes 1769480 | tf_op jit(solution)/shard_map/ppermute | solution.py:206
  134.1 17.6 %copy-start.10 = (f32[1,576]{1,0:T(1,128)S(1)}, f32[1,576]{1,0:T(1,128)}, u32[]{:S(2)}) copy-start(f32[1,576]{1,0:T(1,128)} %param.9) | copy-start | bytes 6916
  134.7 13.8 %collective-permute-start.26 = (bf16[64,576]{1,0:T(8,128)(2,1)S(1)}, bf16[64,576]{1,0:T(8,128)(2,1)S(1)}, u32[]{:S(2)}, u32[]{:S(2)}) collective-permute-start(bf16[64,576]{1,0:T(8,128)(2,1)S(1)} %get-tuple-element.27), channel_id=1, source_target_pairs={{0,32},{4,36},{8,40},{12,44},{16,48},{20,52},{24,56},{28,60},{32,0... | collective-permute-start | bytes 221192 | tf_op jit(solution)/shard_map/ppermute | solution.py:217
  139.3 11.4 %collective-permute-start.27 = (bf16[64,576]{1,0:T(8,128)(2,1)S(1)}, bf16[64,576]{1,0:T(8,128)(2,1)S(1)}, u32[]{:S(2)}, u32[]{:S(2)}) collective-permute-start(bf16[64,576]{1,0:T(8,128)(2,1)S(1)} %get-tuple-element.33), channel_id=1, source_target_pairs={{0,24},{4,28},{8,32},{12,36},{16,40},{20,44},{24,48},{28,52},{32,5... | collective-permute-start | bytes 221192 | tf_op jit(solution)/shard_map/ppermute | solution.py:217
  139.4 12.4 %collective-permute-start.28 = (bf16[64,576]{1,0:T(8,128)(2,1)S(1)}, bf16[64,576]{1,0:T(8,128)(2,1)S(1)}, u32[]{:S(2)}, u32[]{:S(2)}) collective-permute-start(bf16[64,576]{1,0:T(8,128)(2,1)S(1)} %get-tuple-element.32), channel_id=1, source_target_pairs={{0,40},{4,44},{8,48},{12,52},{16,56},{20,60},{24,0},{28,4},{32,8},... | collective-permute-start | bytes 221192 | tf_op jit(solution)/shard_map/ppermute | solution.py:217
  144.4 9.8 %collective-permute-start.29 = (bf16[64,576]{1,0:T(8,128)(2,1)S(1)}, bf16[64,576]{1,0:T(8,128)(2,1)S(1)}, u32[]{:S(2)}, u32[]{:S(2)}) collective-permute-start(bf16[64,576]{1,0:T(8,128)(2,1)S(1)} %get-tuple-element.31), channel_id=1, source_target_pairs={{0,16},{4,20},{8,24},{12,28},{16,32},{20,36},{24,40},{28,44},{32,4... | collective-permute-start | bytes 221192 | tf_op jit(solution)/shard_map/ppermute | solution.py:217
  144.4 9.8 %collective-permute-start.30 = (bf16[64,576]{1,0:T(8,128)(2,1)S(1)}, bf16[64,576]{1,0:T(8,128)(2,1)S(1)}, u32[]{:S(2)}, u32[]{:S(2)}) collective-permute-start(bf16[64,576]{1,0:T(8,128)(2,1)S(1)} %get-tuple-element.30), channel_id=1, source_target_pairs={{0,48},{4,52},{8,56},{12,60},{16,0},{20,4},{24,8},{28,12},{32,16},... | collective-permute-start | bytes 221192 | tf_op jit(solution)/shard_map/ppermute | solution.py:217
  148.5 6.1 %collective-permute-start.31 = (bf16[64,576]{1,0:T(8,128)(2,1)S(1)}, bf16[64,576]{1,0:T(8,128)(2,1)S(1)}, u32[]{:S(2)}, u32[]{:S(2)}) collective-permute-start(bf16[64,576]{1,0:T(8,128)(2,1)S(1)} %get-tuple-element.29), channel_id=1, source_target_pairs={{0,8},{4,12},{8,16},{12,20},{16,24},{20,28},{24,32},{28,36},{32,40... | collective-permute-start | bytes 221192 | tf_op jit(solution)/shard_map/ppermute | solution.py:217
  150.7 4.4 %collective-permute-start.32 = (bf16[64,576]{1,0:T(8,128)(2,1)S(1)}, bf16[64,576]{1,0:T(8,128)(2,1)S(1)}, u32[]{:S(2)}, u32[]{:S(2)}) collective-permute-start(bf16[64,576]{1,0:T(8,128)(2,1)S(1)} %get-tuple-element.28), channel_id=1, source_target_pairs={{0,56},{4,60},{8,0},{12,4},{16,8},{20,12},{24,16},{28,20},{32,24},... | collective-permute-start | bytes 221192 | tf_op jit(solution)/shard_map/ppermute | solution.py:217

commit v3 on v2

--- a/solution.py
+++ b/solution.py
@@ -15,8 +15,8 @@
 PARAMS = pltpu.CompilerParams(vmem_limit_bytes=12 << 20)
 
 
-def ring(shift, sections=(0, 1, 2, 3)):
-    return [(s * ROWS + i, s * ROWS + (i + shift) % ROWS) for s in sections for i in range(ROWS)]
+def ring(shift):
+    return [(i, (i + shift) % ROWS) for i in range(ROWS)]
 
 
 def hop(shift):
@@ -24,7 +24,10 @@
 
 
 SWAP = [(i, i ^ 1) for i in range(2 * CHIPS)]
-BOTH = [(i, ((i // 2 + (1 if i % 2 == 0 else -1)) % CHIPS) * 2 + i % 2) for i in range(2 * CHIPS)]
+
+
+def both(shift):
+    return [(i, ((i // 2 + (shift if i % 2 == 0 else -shift)) % CHIPS) * 2 + i % 2) for i in range(2 * CHIPS)]
 
 
 def in_vmem(values):
@@ -42,20 +45,29 @@
     )(where, *in_vmem(vmem), *rest)
 
 
-def copy_lent(where, decoders):
+def copy_weights(where, decoders, picks):
     _, width, count = decoders.shape
-
-    def kernel(where_ref, source, a_ref, b_ref, sems):
-        first = pltpu.make_async_copy(source.at[where_ref[3]], a_ref, sems.at[0])
-        second = pltpu.make_async_copy(source.at[2], b_ref, sems.at[1])
-        first.start()
-        second.start()
-        first.wait()
-        second.wait()
-
-    out = [((width, count), decoders.dtype)] * 2
+    n = len(picks)
+
+    def kernel(where_ref, source, *refs):
+        third = width // 3
+        copies = [
+            pltpu.make_async_copy(
+                source.at[where_ref[pick], pl.ds(part * third, third)],
+                refs[i].at[pl.ds(part * third, third)],
+                refs[n].at[3 * i + part],
+            )
+            for i, pick in enumerate(picks)
+            for part in range(3)
+        ]
+        for copy in copies:
+            copy.start()
+        for copy in copies:
+            copy.wait()
+
+    out = [((width, count), decoders.dtype)] * n
     decoders = pltpu.with_memory_space_constraint(decoders, pltpu.HBM)
-    return call(kernel, where, [], [decoders], out, [pltpu.SemaphoreType.DMA((2,))])
+    return call(kernel, where, [], [decoders], out, [pltpu.SemaphoreType.DMA((3 * n,))])
 
 
 def encode(where, pieces, shifts, weight, start, bias):
@@ -103,25 +115,25 @@
 def gather_and_encode(where, core, own, weight, bias):
     other = lax.ppermute(own, "feat", SWAP)
     block = jnp.where(core == 0, jnp.concatenate([own, other]), jnp.concatenate([other, own]))
-    b1 = lax.ppermute(block, "feat", BOTH)
-    b2 = lax.ppermute(b1, "feat", BOTH)
+    b1 = lax.ppermute(block, "feat", both(1))
+    b2 = lax.ppermute(block, "feat", both(2))
+    b3 = lax.ppermute(b1, "feat", both(2))
+    b4 = lax.ppermute(b2, "feat", both(2))
     s1 = lax.ppermute(b1, "feat", SWAP)
-    b3 = lax.ppermute(b2, "feat", BOTH)
     s2 = lax.ppermute(b2, "feat", SWAP)
+    s3 = lax.ppermute(b3, "feat", SWAP)
     sums = encode(where, [block, b1, s1], (0, -1, 1), weight, None, None)
-    b4 = lax.ppermute(b3, "feat", BOTH)
-    s3 = lax.ppermute(b3, "feat", SWAP)
     sums = encode(where, [b2, s2, b3], (-2, 2, -3), weight, sums, None)
     return encode(where, [s3, b4], (3, -4), weight, sums, bias)
 
 
-def gather_rows(own, sections):
+def gather_rows(own):
     half = own.shape[0] // 2
-    axes = ("sec", "row")
-    before = lax.ppermute(own, axes, ring(1, sections))
-    after = lax.ppermute(own, axes, ring(-1, sections))
-    first = lax.ppermute(before[:half], axes, ring(1, sections))
-    second = lax.ppermute(after[half:], axes, ring(-1, sections))
+    before = lax.ppermute(own, "row", ring(1))
+    after = lax.ppermute(own, "row", ring(-1))
+    before_half, after_half = before[:half], after[half:]
+    first = lax.ppermute(before_half, "row", ring(1))
+    second = lax.ppermute(after_half, "row", ring(-1))
     return own, before, after, first, second
 
 
@@ -183,18 +195,19 @@
     feat = lax.axis_index("feat")
     row = lax.axis_index("row")
     core, chip = feat & 1, feat >> 1
-    where = jnp.stack([core, chip, row, jnp.where(sec == 2, 1, 0), sec]).astype(jnp.int32)
-
-    lent_a, lent_b = copy_lent(where, decoders)
+    where = jnp.stack([core, chip, row, jnp.where(sec == 2, 1, 0), sec, jnp.where(sec == 3, 1, 0), 2])
+    where = where.astype(jnp.int32)
+
+    lent_a, lent_b = copy_weights(where, decoders, (3, 6))
     lent_c = lax.ppermute(lent_a, "sec", [(1, 0)])
     lent_a = lax.ppermute(lent_a, "sec", [(2, 1), (3, 0)])
     lent_b = lax.ppermute(lent_b, "sec", [(3, 2)])
 
     features = gather_and_encode(where, core, inputs[0].T, enc_weight[0], enc_bias)
 
-    every_own = gather_rows(features, (0, 1, 2, 3))
+    every_own = gather_rows(features)
     brought = lax.ppermute(features, "sec", [(0, 2), (1, 3)])
-    every_brought = gather_rows(brought, (2, 3))
+    every_brought = gather_rows(brought)
 
     mine, theirs = decode(where, every_own, (lent_a, lent_b), None, True)
     pair = mine + lax.ppermute(theirs, "feat", SWAP).astype(jnp.float32)
@@ -205,16 +218,19 @@
     pair = mine + lax.ppermute(theirs, ("sec", "feat"), SWAP).astype(jnp.float32)
     back_c = lax.ppermute(pair.astype(jnp.bfloat16), "sec", [(0, 1)])
 
-    late, _ = lax.optimization_barrier((decoders, features))
-    own_weight = lax.dynamic_index_in_dim(late, sec, 0, keepdims=False)
-    brought_weight = lax.dynamic_index_in_dim(late, jnp.where(sec == 3, 1, 0), 0, keepdims=False)
+    own_weight, brought_weight = copy_weights(where, decoders, (4, 5))
     (start,) = decode(where, every_own, (own_weight,), None, False)
     mine, theirs = decode(where, every_brought, (brought_weight,), start, True)
     pair = mine + lax.ppermute(theirs, "feat", SWAP).astype(jnp.float32)
     for back in (back_a, back_b, back_c):
         pair = pair + back.astype(jnp.float32)
     send = pair.astype(jnp.bfloat16)
-    got = [lax.ppermute(send[d], "feat", hop(d)) for d in (4, 3, 5, 2, 6, 1, 7)]
+    up = lax.ppermute(jnp.stack([send[4], send[2]]), "feat", hop(1))
+    down = lax.ppermute(send[6], "feat", hop(-1))
+    got = [lax.ppermute(send[5], "feat", hop(-3))]
+    for piece, extra, shift in ((3, up[0], 3), (1, up[1], 1), (7, down, -1)):
+        merged = (pair[piece] + extra.astype(jnp.float32)).astype(jnp.bfloat16)
+        got.append(lax.ppermute(merged, "feat", hop(shift)))
     total = pair[0]
     for g in got:
         total = total + g.astype(jnp.float32)

time: 156 us -> 144 us (0.923)
  the two profiles are of different devices: /device:TPU:26 before, /device:TPU:6 now
where the time goes in v3:
time: 144 us; the launch traced here: 142 us
  waiting for transfers between devices  73.5 us (51%)
  starting transfers between devices  47 us (33%)
  Pallas kernels  18 us (12%)
  other arithmetic  2.51 us (2%)
    ppermute x1, waiting for transfers between devices, per_device(): brought = lax.ppermute(features, 'sec', [(0, 2), (1, 3)])  21.9 us
    pallas_call x9, Pallas kernels, call(): pl.pallas_call(kernel, in_specs=[SMEM] + [VMEM] * len(vmem) + [ANY] * len...  18 us
    ppermute x1, waiting for transfers between devices, per_device(): back_a = lax.ppermute(pair, 'sec', [(0, 3), (1, 2)])  16.8 us
    ppermute x2, waiting for transfers between devices, gather_rows(): before = lax.ppermute(own, 'row', ring(1))  13.8 us
    ppermute x3, starting transfers between devices, per_device(): got.append(lax.ppermute(merged, 'feat', hop(shift)))  6.93 us
    ppermute x2, starting transfers between devices, gather_rows(): second = lax.ppermute(after_half, 'row', ring(-1))  4.86 us
    ppermute x1, starting transfers between devices, per_device(): got = [lax.ppermute(send[5], 'feat', hop(-3))]  4.71 us
    ppermute x2, starting transfers between devices, gather_rows(): after = lax.ppermute(own, 'row', ring(-1))  4.69 us
  transfers between devices with their start and end apart: 32, of which 12 were waited for; matrix products, arithmetic and copies ran while one was open for 0% of the time, Pallas kernels for 13%

profile of v3, /device:TPU:6, one launch (start us, length us, event | category | flops | bytes accessed | tf_op | source)
XLA Modules:
  0.0 141.6 jit_solution(17377695808907576838)
XLA Ops:
  0.0 1.5 %collective-permute-done = bf16[144,256]{1,0:T(8,128)(2,1)S(1)} collective-permute-done((bf16[144,256]{1,0:T(8,128)(2,1)}, bf16[144,256]{1,0:T(8,128)(2,1)S(1)}, u32[]{:S(2)}, u32[]{:S(2)}) %collective-permute-start) | collective-permute-done | bytes 73760 | tf_op jit(solution)/shard_map/ppermute | solution.py:116
  1.5 1.0 maximum_select_fusion.refs_0_
  2.5 2.0 %collective-permute-start.1 = (bf16[288,256]{1,0:T(8,128)(2,1)S(1)}, bf16[288,256]{1,0:T(8,128)(2,1)S(1)}, u32[]{:S(2)}, u32[]{:S(2)}) collective-permute-start(bf16[288,256]{1,0:T(8,128)(2,1)S(1)} %maximum_select_fusion.refs_0_), channel_id=1, source_target_pairs={{0,8},{4,60},{8,16},{12,4},{16,24},{20,12},{24,32},{28,20},{32,40}... | collective-permute-start | bytes 442376 | tf_op jit(solution)/shard_map/ppermute | solution.py:118
  4.5 3.3 %collective-permute-start.4 = (bf16[288,256]{1,0:T(8,128)(2,1)S(1)}, bf16[288,256]{1,0:T(8,128)(2,1)S(1)}, u32[]{:S(2)}, u32[]{:S(2)}) collective-permute-start(bf16[288,256]{1,0:T(8,128)(2,1)S(1)} %maximum_select_fusion.refs_0_), channel_id=1, source_target_pairs={{0,16},{4,52},{8,24},{12,60},{16,32},{20,4},{24,40},{28,12},{32,48... | collective-permute-start | bytes 442376 | tf_op jit(solution)/shard_map/ppermute | solution.py:119
  7.8 3.8 %collective-permute-done.1.refs_1_ = bf16[288,256]{1,0:T(8,128)(2,1)S(1)} collective-permute-done((bf16[288,256]{1,0:T(8,128)(2,1)S(1)}, bf16[288,256]{1,0:T(8,128)(2,1)S(1)}, u32[]{:S(2)}, u32[]{:S(2)}) %collective-permute-start.1) | collective-permute-done | bytes 147488 | tf_op jit(solution)/shard_map/ppermute | solution.py:118
  11.5 1.5 %collective-permute-start.7 = (bf16[288,256]{1,0:T(8,128)(2,1)S(1)}, bf16[288,256]{1,0:T(8,128)(2,1)S(1)}, u32[]{:S(2)}, u32[]{:S(2)}) collective-permute-start(bf16[288,256]{1,0:T(8,128)(2,1)S(1)} %collective-permute-done.1.refs_1_), channel_id=1, source_target_pairs={{0,4},{4,0},{8,12},{12,8},{16,20},{20,16},{24,28},{28,24},{32,36},... | collective-permute-start | bytes 442376 | tf_op jit(solution)/shard_map/ppermute | solution.py:122
  13.0 2.1 %collective-permute-done.4.refs_0_ = bf16[288,256]{1,0:T(8,128)(2,1)S(1)} collective-permute-done((bf16[288,256]{1,0:T(8,128)(2,1)S(1)}, bf16[288,256]{1,0:T(8,128)(2,1)S(1)}, u32[]{:S(2)}, u32[]{:S(2)}) %collective-permute-start.4) | collective-permute-done | bytes 147488 | tf_op jit(solution)/shard_map/ppermute | solution.py:119
  15.1 2.1 %collective-permute-start.5 = (bf16[288,256]{1,0:T(8,128)(2,1)S(1)}, bf16[288,256]{1,0:T(8,128)(2,1)S(1)}, u32[]{:S(2)}, u32[]{:S(2)}) collective-permute-start(bf16[288,256]{1,0:T(8,128)(2,1)S(1)} %collective-permute-done.4.refs_0_), channel_id=1, source_target_pairs={{0,16},{4,52},{8,24},{12,60},{16,32},{20,4},{24,40},{28,12},{32,48... | collective-permute-start | bytes 442376 | tf_op jit(solution)/shard_map/ppermute | solution.py:121
  17.2 2.2 %collective-permute-done.2.refs_2_ = bf16[288,256]{1,0:T(8,128)(2,1)S(1)} collective-permute-done((bf16[288,256]{1,0:T(8,128)(2,1)S(1)}, bf16[288,256]{1,0:T(8,128)(2,1)S(1)}, u32[]{:S(2)}, u32[]{:S(2)}) %collective-permute-start.2) | collective-permute-done | bytes 147488 | tf_op jit(solution)/shard_map/ppermute | solution.py:120
  19.3 0.0 collective-permute-start.3
  19.3 0.1 stack.30.where_ref
  19.4 2.5 %shard_map.61 = (bf16[576,1024]{1,0:T(8,128)(2,1)S(1)}, bf16[576,1024]{1,0:T(8,128)(2,1)S(1)}) custom-call(s32[7]{0:T(128)S(1)} %stack.30.where_ref, bf16[4,576,1024]{2,1,0:T(8,128)(2,1)} %bitcast.48), custom_call_target="tpu_custom_call" | custom-call | tf_op jit(solution)/shard_map/pallas_call | solution.py:38
  21.9 2.5 %collective-permute-start.18 = (bf16[576,1024]{1,0:T(8,128)(2,1)S(1)}, bf16[576,1024]{1,0:T(8,128)(2,1)S(1)}, u32[]{:S(2)}, u32[]{:S(2)}) collective-permute-start(bf16[576,1024]{1,0:T(8,128)(2,1)S(1)} %get-tuple-element.19), channel_id=1, source_target_pairs={{128,64},{192,0},{129,65},{193,1},{130,66},{194,2},{131,67},{195,3... | collective-permute-start | bytes 3538952 | tf_op jit(solution)/shard_map/ppermute | solution.py:203
  24.4 2.9 %collective-permute-start.19 = (bf16[576,1024]{1,0:T(8,128)(2,1)S(1)}, bf16[576,1024]{1,0:T(8,128)(2,1)S(1)}, u32[]{:S(2)}, u32[]{:S(2)}) collective-permute-start(bf16[576,1024]{1,0:T(8,128)(2,1)S(1)} %get-tuple-element.20), channel_id=1, source_target_pairs={{192,128},{193,129},{194,130},{195,131},{196,132},{197,133},{198,1... | collective-permute-start | bytes 3538952 | tf_op jit(solution)/shard_map/ppermute | solution.py:204
  27.3 1.8 %shard_map.55.refs_3_ = f32[256,1024]{1,0:T(8,128)S(1)} custom-call(s32[7]{0:T(128)S(1)} %stack.30.where_ref, bf16[288,256]{1,0:T(8,128)(2,1)S(1)} %maximum_select_fusion.refs_0_, bf16[288,256]{1,0:T(8,128)(2,1)S(1)} %collective-permute-done.1.refs_1_, bf16[288,256]{1,0:T(8,128)(2,1)S(1)} %collective-permute-done.7.refs_2_, bf16[2304,1024]{1,0:T(8,128)(2,1)S(1)} %bitcast.45), custom_call_target="tpu_custom_call" | custom-call | tf_op jit(solution)/shard_map/pallas_call | solution.py:38
  29.1 0.0 copy-start.1
  29.1 0.0 collective-permute-done.6.refs_1_
  29.1 1.8 %shard_map.56.refs_2_ = f32[256,1024]{1,0:T(8,128)S(1)} custom-call(s32[7]{0:T(128)S(1)} %stack.30.where_ref, bf16[288,256]{1,0:T(8,128)(2,1)S(1)} %collective-permute-done.4.refs_0_, bf16[288,256]{1,0:T(8,128)(2,1)S(1)} %collective-permute-done.6.refs_1_, bf16[288,256]{1,0:T(8,128)(2,1)S(1)} %collective-permute-done.2.refs_2_, ...), custom_call_target="tpu_custom_call" | custom-call | tf_op jit(solution)/shard_map/pallas_call | solution.py:38
  30.9 0.0 collective-permute-done.5.refs_1_
  31.0 1.5 %shard_map.57.own = bf16[256,1024]{1,0:T(8,128)(2,1)S(1)} custom-call(s32[7]{0:T(128)S(1)} %stack.30.where_ref, bf16[288,256]{1,0:T(8,128)(2,1)S(1)} %collective-permute-done.3.refs_0_, bf16[288,256]{1,0:T(8,128)(2,1)S(1)} %collective-permute-done.5.refs_1_, f32[256,1024]{1,0:T(8,128)S(1)} %shard_map.56.refs_2_, f32[1,1024]{1,0:T(1,128)S(1)} %copy-done.1, ...), custom_call_target="tpu_custom_call" | custom-call | tf_op jit(solution)/shard_map/pallas_call | solution.py:38
  32.5 1.7 %collective-permute-start.13 = (bf16[256,1024]{1,0:T(8,128)(2,1)S(1)}, bf16[256,1024]{1,0:T(8,128)(2,1)S(1)}, u32[]{:S(2)}, u32[]{:S(2)}) collective-permute-start(bf16[256,1024]{1,0:T(8,128)(2,1)S(1)} %shard_map.57.own), channel_id=1, source_target_pairs={{0,1},{1,2},{2,3},{3,0},{4,5},{5,6},{6,7},{7,4},{8,9},{9,10},{10,1... | collective-permute-start | bytes 1572872 | tf_op jit(solution)/shard_map/ppermute | solution.py:132
  34.2 0.7 collective-permute-start.23
  34.9 1.7 %collective-permute-start.14 = (bf16[256,1024]{1,0:T(8,128)(2,1)S(1)}, bf16[256,1024]{1,0:T(8,128)(2,1)S(1)}, u32[]{:S(2)}, u32[]{:S(2)}) collective-permute-start(bf16[256,1024]{1,0:T(8,128)(2,1)S(1)} %shard_map.57.own), channel_id=1, source_target_pairs={{0,3},{1,0},{2,1},{3,2},{4,7},{5,4},{6,5},{7,6},{8,11},{9,8},{10,9... | collective-permute-start | bytes 1572872 | tf_op jit(solution)/shard_map/ppermute | solution.py:133
  36.6 11.0 %collective-permute-done.13.before = bf16[256,1024]{1,0:T(8,128)(2,1)S(1)} collective-permute-done((bf16[256,1024]{1,0:T(8,128)(2,1)S(1)}, bf16[256,1024]{1,0:T(8,128)(2,1)S(1)}, u32[]{:S(2)}, u32[]{:S(2)}) %collective-permute-start.13) | collective-permute-done | bytes 524320 | tf_op jit(solution)/shard_map/ppermute | solution.py:132
  47.6 1.3 collective-permute-start.8
  49.0 0.0 collective-permute-done.14.after
  49.0 1.1 collective-permute-start.15
  50.1 21.9 %collective-permute-done.8.own = bf16[256,1024]{1,0:T(8,128)(2,1)S(1)} collective-permute-done((bf16[256,1024]{1,0:T(8,128)(2,1)S(1)}, bf16[256,1024]{1,0:T(8,128)(2,1)S(1)}, u32[]{:S(2)}, u32[]{:S(2)}) %collective-permute-start.8) | collective-permute-done | bytes 524320 | tf_op jit(solution)/shard_map/ppermute | solution.py:209
  72.0 1.7 %collective-permute-start.16 = (bf16[128,1024]{1,0:T(8,128)(2,1)S(1)}, bf16[128,1024]{1,0:T(8,128)(2,1)S(1)}, u32[]{:S(2)}, u32[]{:S(2)}) collective-permute-start(bf16[128,1024]{1,0:T(8,128)(2,1)S(1)} %slice.59), channel_id=1, source_target_pairs={{0,3},{1,0},{2,1},{3,2},{4,7},{5,4},{6,5},{7,6},{8,11},{9,8},{10,9... | collective-permute-start | bytes 786440 | tf_op jit(solution)/shard_map/ppermute | solution.py:136
  73.7 0.0 collective-permute-done.18.rest_0_
  73.8 0.3 collective-permute-start.9
  74.0 3.0 %collective-permute-start.10 = (bf16[256,1024]{1,0:T(8,128)(2,1)S(1)}, bf16[256,1024]{1,0:T(8,128)(2,1)S(1)}, u32[]{:S(2)}, u32[]{:S(2)}) collective-permute-start(bf16[256,1024]{1,0:T(8,128)(2,1)S(1)} %collective-permute-done.8.own), channel_id=1, source_target_pairs={{0,3},{1,0},{2,1},{3,2},{4,7},{5,4},{6,5},{7,6},{8,11},{9,8},{10,9... | collective-permute-start | bytes 1572872 | tf_op jit(solution)/shard_map/ppermute | solution.py:133
  77.0 0.0 collective-permute-done.15.first
  77.0 4.2 %collective-permute-done.16.second = bf16[128,1024]{1,0:T(8,128)(2,1)S(1)} collective-permute-done((bf16[128,1024]{1,0:T(8,128)(2,1)S(1)}, bf16[128,1024]{1,0:T(8,128)(2,1)S(1)}, u32[]{:S(2)}, u32[]{:S(2)}) %collective-permute-start.16) | collective-permute-done | bytes 262176 | tf_op jit(solution)/shard_map/ppermute | solution.py:136
  81.2 2.6 %shard_map.62 = (f32[8,64,576]{2,1,0:T(8,128)S(1)}, bf16[8,64,576]{2,1,0:T(8,128)(2,1)S(1)}) custom-call(s32[7]{0:T(128)S(1)} %stack.30.where_ref, bf16[256,1024]{1,0:T(8,128)(2,1)S(1)} %shard_map.57.own, bf16[256,1024]{1,0:T(8,128)(2,1)S(1)} %collective-permute-done.13.before, bf16[256,1024]{1,0:T(8,128)(2,1)S(1)} %collective-permute-done.14.after, ...), custom_call_target="tpu_custom_call" | custom-call | tf_op jit(solution)/shard_map/pallas_call | solution.py:38
  83.8 0.1 collective-permute-start.20
  83.9 0.0 collective-permute-done.23.rest_0_
  83.9 0.6 shard_map.63
  84.5 0.7 collective-permute-start.24
  85.2 2.8 %collective-permute-done.9.before = bf16[256,1024]{1,0:T(8,128)(2,1)S(1)} collective-permute-done((bf16[256,1024]{1,0:T(8,128)(2,1)S(1)}, bf16[256,1024]{1,0:T(8,128)(2,1)S(1)}, u32[]{:S(2)}, u32[]{:S(2)}) %collective-permute-start.9) | collective-permute-done | bytes 524320 | tf_op jit(solution)/shard_map/ppermute | solution.py:132
  88.0 0.1 collective-permute-start.11
  88.1 2.7 %collective-permute-done.10.after = bf16[256,1024]{1,0:T(8,128)(2,1)S(1)} collective-permute-done((bf16[256,1024]{1,0:T(8,128)(2,1)S(1)}, bf16[256,1024]{1,0:T(8,128)(2,1)S(1)}, u32[]{:S(2)}, u32[]{:S(2)}) %collective-permute-start.10) | collective-permute-done | bytes 524320 | tf_op jit(solution)/shard_map/ppermute | solution.py:133
  90.8 3.1 %collective-permute-start.12 = (bf16[128,1024]{1,0:T(8,128)(2,1)S(1)}, bf16[128,1024]{1,0:T(8,128)(2,1)S(1)}, u32[]{:S(2)}, u32[]{:S(2)}) collective-permute-start(bf16[128,1024]{1,0:T(8,128)(2,1)S(1)} %slice.57), channel_id=1, source_target_pairs={{0,3},{1,0},{2,1},{3,2},{4,7},{5,4},{6,5},{7,6},{8,11},{9,8},{10,9... | collective-permute-start | bytes 786440 | tf_op jit(solution)/shard_map/ppermute | solution.py:136
  94.0 2.2 %shard_map.58 = (bf16[576,1024]{1,0:T(8,128)(2,1)S(1)}, bf16[576,1024]{1,0:T(8,128)(2,1)S(1)}) custom-call(s32[7]{0:T(128)S(1)} %stack.30.where_ref, bf16[4,576,1024]{2,1,0:T(8,128)(2,1)} %bitcast.49), custom_call_target="tpu_custom_call" | custom-call | tf_op jit(solution)/shard_map/pallas_call | solution.py:38
  96.1 2.5 %shard_map.59.rest_1_ = f32[4,256,576]{2,1,0:T(8,128)S(1)} custom-call(s32[7]{0:T(128)S(1)} %stack.30.where_ref, bf16[256,1024]{1,0:T(8,128)(2,1)S(1)} %shard_map.57.own, bf16[256,1024]{1,0:T(8,128)(2,1)S(1)} %collective-permute-done.13.before, bf16[256,1024]{1,0:T(8,128)(2,1)S(1)} %collective-permute-done.14.after, ...), custom_call_target="tpu_custom_call" | custom-call | tf_op jit(solution)/shard_map/pallas_call | solution.py:38
  98.6 2.6 %shard_map.60 = (f32[8,64,576]{2,1,0:T(8,128)S(1)}, bf16[8,64,576]{2,1,0:T(8,128)(2,1)S(1)}) custom-call(s32[7]{0:T(128)S(1)} %stack.30.where_ref, bf16[256,1024]{1,0:T(8,128)(2,1)S(1)} %collective-permute-done.8.own, bf16[256,1024]{1,0:T(8,128)(2,1)S(1)} %collective-permute-done.9.before, bf16[256,1024]{1,0:T(8,128)(2,1)S(1)} %collective-permute-done.10.after, ...), custom_call_target="tpu_custom_call" | custom-call | tf_op jit(solution)/shard_map/pallas_call | solution.py:38
  101.2 0.1 collective-permute-start.17
  101.3 0.1 add_convert_fusion.1
  101.5 1.3 collective-permute-start.21
  102.8 1.3 collective-permute-start.22
  104.1 0.1 add_convert_fusion
  104.2 0.7 collective-permute-start.25
  104.9 16.8 %collective-permute-done.21 = bf16[8,64,576]{2,1,0:T(8,128)(2,1)S(1)} collective-permute-done((bf16[8,64,576]{2,1,0:T(8,128)(2,1)S(1)}, bf16[8,64,576]{2,1,0:T(8,128)(2,1)S(1)}, u32[]{:S(2)}, u32[]{:S(2)}) %collective-permute-start.21) | collective-permute-done | bytes 589856 | tf_op jit(solution)/shard_map/ppermute | solution.py:215
  121.7 0.1 collective-permute-done.22
  121.8 0.4 fusion.13
  122.2 0.0 copy-start.2
  122.3 2.1 %collective-permute-start.30 = (bf16[64,576]{1,0:T(8,128)(2,1)S(1)}, bf16[64,576]{1,0:T(8,128)(2,1)S(1)}, u32[]{:S(2)}, u32[]{:S(2)}) collective-permute-start(bf16[64,576]{1,0:T(8,128)(2,1)S(1)} %get-tuple-element.30), channel_id=1, source_target_pairs={{0,56},{4,60},{8,0},{12,4},{16,8},{20,12},{24,16},{28,20},{32,24},... | collective-permute-start | bytes 221192 | tf_op jit(solution)/shard_map/ppermute | solution.py:229
  124.4 0.3 collective-permute-start.27
  124.7 4.7 %collective-permute-start.26 = (bf16[64,576]{1,0:T(8,128)(2,1)S(1)}, bf16[64,576]{1,0:T(8,128)(2,1)S(1)}, u32[]{:S(2)}, u32[]{:S(2)}) collective-permute-start(bf16[64,576]{1,0:T(8,128)(2,1)S(1)} %get-tuple-element.29), channel_id=1, source_target_pairs={{0,40},{4,44},{8,48},{12,52},{16,56},{20,60},{24,0},{28,4},{32,8},... | collective-permute-start | bytes 221192 | tf_op jit(solution)/shard_map/ppermute | solution.py:230
  129.5 2.0 %collective-permute-start.31 = (bf16[64,576]{1,0:T(8,128)(2,1)S(1)}, bf16[64,576]{1,0:T(8,128)(2,1)S(1)}, u32[]{:S(2)}, u32[]{:S(2)}) collective-permute-start(bf16[64,576]{1,0:T(8,128)(2,1)S(1)} %fusion.1), channel_id=1, source_target_pairs={{0,56},{4,60},{8,0},{12,4},{16,8},{20,12},{24,16},{28,20},{32,24},... | collective-permute-start | bytes 221192 | tf_op jit(solution)/shard_map/ppermute | solution.py:233
  131.5 1.4 %collective-permute-start.28 = (bf16[64,576]{1,0:T(8,128)(2,1)S(1)}, bf16[64,576]{1,0:T(8,128)(2,1)S(1)}, u32[]{:S(2)}, u32[]{:S(2)}) collective-permute-start(bf16[64,576]{1,0:T(8,128)(2,1)S(1)} %get-tuple-element.27), channel_id=1, source_target_pairs={{0,24},{4,28},{8,32},{12,36},{16,40},{20,44},{24,48},{28,52},{32,5... | collective-permute-start | bytes 221192 | tf_op jit(solution)/shard_map/ppermute | solution.py:233
  133.0 3.5 %collective-permute-start.29 = (bf16[64,576]{1,0:T(8,128)(2,1)S(1)}, bf16[64,576]{1,0:T(8,128)(2,1)S(1)}, u32[]{:S(2)}, u32[]{:S(2)}) collective-permute-start(bf16[64,576]{1,0:T(8,128)(2,1)S(1)} %get-tuple-element.28), channel_id=1, source_target_pairs={{0,8},{4,12},{8,16},{12,20},{16,24},{20,28},{24,32},{28,36},{32,40... | collective-permute-start | bytes 221192 | tf_op jit(solution)/shard_map/ppermute | solution.py:233
  136.5 4.5 %collective-permute-done.28 = bf16[64,576]{1,0:T(8,128)(2,1)S(1)} collective-permute-done((bf16[64,576]{1,0:T(8,128)(2,1)S(1)}, bf16[64,576]{1,0:T(8,128)(2,1)S(1)}, u32[]{:S(2)}, u32[]{:S(2)}) %collective-permute-start.28) | collective-permute-done | bytes 73760 | tf_op jit(solution)/shard_map/ppermute | solution.py:233
  140.9 0.7 fusion.10
  (30 shorter events, 0.3 us)
Async XLA Ops:
  0.0 1.5 %collective-permute-start = (bf16[144,256]{1,0:T(8,128)(2,1)}, bf16[144,256]{1,0:T(8,128)(2,1)S(1)}, u32[]{:S(2)}, u32[]{:S(2)}) collective-permute-start(bf16[144,256]{1,0:T(8,128)(2,1)} %bitcast.50), channel_id=1, source_target_pairs={{0,4},{4,0},{8,12},{12,8},{16,20},{20,16},{24,28},{28,24},{32,36},... | collective-permute-start | bytes 221192 | tf_op jit(solution)/shard_map/ppermute | solution.py:116
  2.5 9.1 %collective-permute-start.1 = (bf16[288,256]{1,0:T(8,128)(2,1)S(1)}, bf16[288,256]{1,0:T(8,128)(2,1)S(1)}, u32[]{:S(2)}, u32[]{:S(2)}) collective-permute-start(bf16[288,256]{1,0:T(8,128)(2,1)S(1)} %maximum_select_fusion.refs_0_), channel_id=1, source_target_pairs={{0,8},{4,60},{8,16},{12,4},{16,24},{20,12},{24,32},{28,20},{32,40}... | collective-permute-start | bytes 442376 | tf_op jit(solution)/shard_map/ppermute | solution.py:118
  4.5 10.6 %collective-permute-start.4 = (bf16[288,256]{1,0:T(8,128)(2,1)S(1)}, bf16[288,256]{1,0:T(8,128)(2,1)S(1)}, u32[]{:S(2)}, u32[]{:S(2)}) collective-permute-start(bf16[288,256]{1,0:T(8,128)(2,1)S(1)} %maximum_select_fusion.refs_0_), channel_id=1, source_target_pairs={{0,16},{4,52},{8,24},{12,60},{16,32},{20,4},{24,40},{28,12},{32,48... | collective-permute-start | bytes 442376 | tf_op jit(solution)/shard_map/ppermute | solution.py:119
  11.5 7.8 %collective-permute-start.2 = (bf16[288,256]{1,0:T(8,128)(2,1)S(1)}, bf16[288,256]{1,0:T(8,128)(2,1)S(1)}, u32[]{:S(2)}, u32[]{:S(2)}) collective-permute-start(bf16[288,256]{1,0:T(8,128)(2,1)S(1)} %collective-permute-done.1.refs_1_), channel_id=1, source_target_pairs={{0,16},{4,52},{8,24},{12,60},{16,32},{20,4},{24,40},{28,12},{32,48... | collective-permute-start | bytes 442376 | tf_op jit(solution)/shard_map/ppermute | solution.py:120
  11.5 12.8 %collective-permute-start.7 = (bf16[288,256]{1,0:T(8,128)(2,1)S(1)}, bf16[288,256]{1,0:T(8,128)(2,1)S(1)}, u32[]{:S(2)}, u32[]{:S(2)}) collective-permute-start(bf16[288,256]{1,0:T(8,128)(2,1)S(1)} %collective-permute-done.1.refs_1_), channel_id=1, source_target_pairs={{0,4},{4,0},{8,12},{12,8},{16,20},{20,16},{24,28},{28,24},{32,36},... | collective-permute-start | bytes 442376 | tf_op jit(solution)/shard_map/ppermute | solution.py:122
  15.1 14.0 %collective-permute-start.6 = (bf16[288,256]{1,0:T(8,128)(2,1)S(1)}, bf16[288,256]{1,0:T(8,128)(2,1)S(1)}, u32[]{:S(2)}, u32[]{:S(2)}) collective-permute-start(bf16[288,256]{1,0:T(8,128)(2,1)S(1)} %collective-permute-done.4.refs_0_), channel_id=1, source_target_pairs={{0,4},{4,0},{8,12},{12,8},{16,20},{20,16},{24,28},{28,24},{32,36},... | collective-permute-start | bytes 442376 | tf_op jit(solution)/shard_map/ppermute | solution.py:123
  15.1 15.8 %collective-permute-start.5 = (bf16[288,256]{1,0:T(8,128)(2,1)S(1)}, bf16[288,256]{1,0:T(8,128)(2,1)S(1)}, u32[]{:S(2)}, u32[]{:S(2)}) collective-permute-start(bf16[288,256]{1,0:T(8,128)(2,1)S(1)} %collective-permute-done.4.refs_0_), channel_id=1, source_target_pairs={{0,16},{4,52},{8,24},{12,60},{16,32},{20,4},{24,40},{28,12},{32,48... | collective-permute-start | bytes 442376 | tf_op jit(solution)/shard_map/ppermute | solution.py:121
  19.3 11.6 %collective-permute-start.3 = (bf16[288,256]{1,0:T(8,128)(2,1)S(1)}, bf16[288,256]{1,0:T(8,128)(2,1)S(1)}, u32[]{:S(2)}, u32[]{:S(2)}) collective-permute-start(bf16[288,256]{1,0:T(8,128)(2,1)S(1)} %collective-permute-done.2.refs_2_), channel_id=1, source_target_pairs={{0,4},{4,0},{8,12},{12,8},{16,20},{20,16},{24,28},{28,24},{32,36},... | collective-permute-start | bytes 442376 | tf_op jit(solution)/shard_map/ppermute | solution.py:124
  19.4 7.8 %copy-start = (bf16[1,2304,1024]{2,1,0:T(8,128)(2,1)S(1)}, bf16[1,2304,1024]{2,1,0:T(8,128)(2,1)}, u32[]{:S(2)}) copy-start(bf16[1,2304,1024]{2,1,0:T(8,128)(2,1)} %param.6) | copy-start | bytes 14155780
  21.9 51.9 %collective-permute-start.18 = (bf16[576,1024]{1,0:T(8,128)(2,1)S(1)}, bf16[576,1024]{1,0:T(8,128)(2,1)S(1)}, u32[]{:S(2)}, u32[]{:S(2)}) collective-permute-start(bf16[576,1024]{1,0:T(8,128)(2,1)S(1)} %get-tuple-element.19), channel_id=1, source_target_pairs={{128,64},{192,0},{129,65},{193,1},{130,66},{194,2},{131,67},{195,3... | collective-permute-start | bytes 3538952 | tf_op jit(solution)/shard_map/ppermute | solution.py:203
  24.4 49.7 %collective-permute-start.19 = (bf16[576,1024]{1,0:T(8,128)(2,1)S(1)}, bf16[576,1024]{1,0:T(8,128)(2,1)S(1)}, u32[]{:S(2)}, u32[]{:S(2)}) collective-permute-start(bf16[576,1024]{1,0:T(8,128)(2,1)S(1)} %get-tuple-element.20), channel_id=1, source_target_pairs={{192,128},{193,129},{194,130},{195,131},{196,132},{197,133},{198,1... | collective-permute-start | bytes 3538952 | tf_op jit(solution)/shard_map/ppermute | solution.py:204
  29.1 1.9 %copy-start.1 = (f32[1,1024]{1,0:T(1,128)S(1)}, f32[1,1024]{1,0:T(1,128)}, u32[]{:S(2)}) copy-start(f32[1,1024]{1,0:T(1,128)} %refs_3_.1) | copy-start | bytes 12292
  32.5 15.1 %collective-permute-start.13 = (bf16[256,1024]{1,0:T(8,128)(2,1)S(1)}, bf16[256,1024]{1,0:T(8,128)(2,1)S(1)}, u32[]{:S(2)}, u32[]{:S(2)}) collective-permute-start(bf16[256,1024]{1,0:T(8,128)(2,1)S(1)} %shard_map.57.own), channel_id=1, source_target_pairs={{0,1},{1,2},{2,3},{3,0},{4,5},{5,6},{6,7},{7,4},{8,9},{9,10},{10,1... | collective-permute-start | bytes 1572872 | tf_op jit(solution)/shard_map/ppermute | solution.py:132
  34.2 49.7 %collective-permute-start.23 = (bf16[576,1024]{1,0:T(8,128)(2,1)S(1)}, bf16[576,1024]{1,0:T(8,128)(2,1)S(1)}, u32[]{:S(2)}, u32[]{:S(2)}) collective-permute-start(bf16[576,1024]{1,0:T(8,128)(2,1)S(1)} %get-tuple-element.19), channel_id=1, source_target_pairs={{64,0},{65,1},{66,2},{67,3},{68,4},{69,5},{70,6},{71,7},{72,8},{73... | collective-permute-start | bytes 3538952 | tf_op jit(solution)/shard_map/ppermute | solution.py:202
  34.9 14.1 %collective-permute-start.14 = (bf16[256,1024]{1,0:T(8,128)(2,1)S(1)}, bf16[256,1024]{1,0:T(8,128)(2,1)S(1)}, u32[]{:S(2)}, u32[]{:S(2)}) collective-permute-start(bf16[256,1024]{1,0:T(8,128)(2,1)S(1)} %shard_map.57.own), channel_id=1, source_target_pairs={{0,3},{1,0},{2,1},{3,2},{4,7},{5,4},{6,5},{7,6},{8,11},{9,8},{10,9... | collective-permute-start | bytes 1572872 | tf_op jit(solution)/shard_map/ppermute | solution.py:133
  47.6 24.4 %collective-permute-start.8 = (bf16[256,1024]{1,0:T(8,128)(2,1)S(1)}, bf16[256,1024]{1,0:T(8,128)(2,1)S(1)}, u32[]{:S(2)}, u32[]{:S(2)}) collective-permute-start(bf16[256,1024]{1,0:T(8,128)(2,1)S(1)} %shard_map.57.own), channel_id=1, source_target_pairs={{0,128},{64,192},{1,129},{65,193},{2,130},{66,194},{3,131},{67,195... | collective-permute-start | bytes 1572872 | tf_op jit(solution)/shard_map/ppermute | solution.py:209
  49.0 28.0 %collective-permute-start.15 = (bf16[128,1024]{1,0:T(8,128)(2,1)S(1)}, bf16[128,1024]{1,0:T(8,128)(2,1)S(1)}, u32[]{:S(2)}, u32[]{:S(2)}) collective-permute-start(bf16[128,1024]{1,0:T(8,128)(2,1)S(1)} %slice.58), channel_id=1, source_target_pairs={{0,1},{1,2},{2,3},{3,0},{4,5},{5,6},{6,7},{7,4},{8,9},{9,10},{10,1... | collective-permute-start | bytes 786440 | tf_op jit(solution)/shard_map/ppermute | solution.py:135
  72.0 9.2 %collective-permute-start.16 = (bf16[128,1024]{1,0:T(8,128)(2,1)S(1)}, bf16[128,1024]{1,0:T(8,128)(2,1)S(1)}, u32[]{:S(2)}, u32[]{:S(2)}) collective-permute-start(bf16[128,1024]{1,0:T(8,128)(2,1)S(1)} %slice.59), channel_id=1, source_target_pairs={{0,3},{1,0},{2,1},{3,2},{4,7},{5,4},{6,5},{7,6},{8,11},{9,8},{10,9... | collective-permute-start | bytes 786440 | tf_op jit(solution)/shard_map/ppermute | solution.py:136
  73.8 14.2 %collective-permute-start.9 = (bf16[256,1024]{1,0:T(8,128)(2,1)S(1)}, bf16[256,1024]{1,0:T(8,128)(2,1)S(1)}, u32[]{:S(2)}, u32[]{:S(2)}) collective-permute-start(bf16[256,1024]{1,0:T(8,128)(2,1)S(1)} %collective-permute-done.8.own), channel_id=1, source_target_pairs={{0,1},{1,2},{2,3},{3,0},{4,5},{5,6},{6,7},{7,4},{8,9},{9,10},{10,1... | collective-permute-start | bytes 1572872 | tf_op jit(solution)/shard_map/ppermute | solution.py:132
  74.0 16.8 %collective-permute-start.10 = (bf16[256,1024]{1,0:T(8,128)(2,1)S(1)}, bf16[256,1024]{1,0:T(8,128)(2,1)S(1)}, u32[]{:S(2)}, u32[]{:S(2)}) collective-permute-start(bf16[256,1024]{1,0:T(8,128)(2,1)S(1)} %collective-permute-done.8.own), channel_id=1, source_target_pairs={{0,3},{1,0},{2,1},{3,2},{4,7},{5,4},{6,5},{7,6},{8,11},{9,8},{10,9... | collective-permute-start | bytes 1572872 | tf_op jit(solution)/shard_map/ppermute | solution.py:133
  83.8 17.5 %collective-permute-start.20 = (bf16[8,64,576]{2,1,0:T(8,128)(2,1)S(1)}, bf16[8,64,576]{2,1,0:T(8,128)(2,1)S(1)}, u32[]{:S(2)}, u32[]{:S(2)}) collective-permute-start(bf16[8,64,576]{2,1,0:T(8,128)(2,1)S(1)} %get-tuple-element.22), channel_id=1, source_target_pairs={{0,4},{4,0},{8,12},{12,8},{16,20},{20,16},{24,28},{28,24},{32,36},... | collective-permute-start | bytes 1769480 | tf_op jit(solution)/shard_map/ppermute | solution.py:213
  84.5 19.6 %collective-permute-start.24 = (bf16[8,64,576]{2,1,0:T(8,128)(2,1)S(1)}, bf16[8,64,576]{2,1,0:T(8,128)(2,1)S(1)}, u32[]{:S(2)}, u32[]{:S(2)}) collective-permute-start(bf16[8,64,576]{2,1,0:T(8,128)(2,1)S(1)} %get-tuple-element.24), channel_id=1, source_target_pairs={{0,4},{4,0},{8,12},{12,8},{16,20},{20,16},{24,28},{28,24},{32,36},... | collective-permute-start | bytes 1769480 | tf_op jit(solution)/shard_map/ppermute | solution.py:218
  88.0 10.6 %collective-permute-start.11 = (bf16[128,1024]{1,0:T(8,128)(2,1)S(1)}, bf16[128,1024]{1,0:T(8,128)(2,1)S(1)}, u32[]{:S(2)}, u32[]{:S(2)}) collective-permute-start(bf16[128,1024]{1,0:T(8,128)(2,1)S(1)} %slice.56), channel_id=1, source_target_pairs={{0,1},{1,2},{2,3},{3,0},{4,5},{5,6},{6,7},{7,4},{8,9},{9,10},{10,1... | collective-permute-start | bytes 786440 | tf_op jit(solution)/shard_map/ppermute | solution.py:135
  90.8 7.8 %collective-permute-start.12 = (bf16[128,1024]{1,0:T(8,128)(2,1)S(1)}, bf16[128,1024]{1,0:T(8,128)(2,1)S(1)}, u32[]{:S(2)}, u32[]{:S(2)}) collective-permute-start(bf16[128,1024]{1,0:T(8,128)(2,1)S(1)} %slice.57), channel_id=1, source_target_pairs={{0,3},{1,0},{2,1},{3,2},{4,7},{5,4},{6,5},{7,6},{8,11},{9,8},{10,9... | collective-permute-start | bytes 786440 | tf_op jit(solution)/shard_map/ppermute | solution.py:136
  101.2 3.7 %collective-permute-start.17 = (bf16[8,64,576]{2,1,0:T(8,128)(2,1)S(1)}, bf16[8,64,576]{2,1,0:T(8,128)(2,1)S(1)}, u32[]{:S(2)}, u32[]{:S(2)}) collective-permute-start(bf16[8,64,576]{2,1,0:T(8,128)(2,1)S(1)} %get-tuple-element.18), channel_id=1, source_target_pairs={{0,4},{4,0},{8,12},{12,8},{16,20},{20,16},{24,28},{28,24},{32,36},... | collective-permute-start | bytes 1769480 | tf_op jit(solution)/shard_map/ppermute | solution.py:224
  101.5 20.2 %collective-permute-start.21 = (bf16[8,64,576]{2,1,0:T(8,128)(2,1)S(1)}, bf16[8,64,576]{2,1,0:T(8,128)(2,1)S(1)}, u32[]{:S(2)}, u32[]{:S(2)}) collective-permute-start(bf16[8,64,576]{2,1,0:T(8,128)(2,1)S(1)} %add_convert_fusion.1), channel_id=1, source_target_pairs={{0,192},{64,128},{1,193},{65,129},{2,194},{66,130},{3,195},{67,131... | collective-permute-start | bytes 1769480 | tf_op jit(solution)/shard_map/ppermute | solution.py:215
  102.8 19.0 %collective-permute-start.22 = (bf16[8,64,576]{2,1,0:T(8,128)(2,1)S(1)}, bf16[8,64,576]{2,1,0:T(8,128)(2,1)S(1)}, u32[]{:S(2)}, u32[]{:S(2)}) collective-permute-start(bf16[8,64,576]{2,1,0:T(8,128)(2,1)S(1)} %add_convert_fusion.1), channel_id=1, source_target_pairs={{128,192},{129,193},{130,194},{131,195},{132,196},{133,197},{134,1... | collective-permute-start | bytes 1769480 | tf_op jit(solution)/shard_map/ppermute | solution.py:216
  104.2 17.6 %collective-permute-start.25 = (bf16[8,64,576]{2,1,0:T(8,128)(2,1)S(1)}, bf16[8,64,576]{2,1,0:T(8,128)(2,1)S(1)}, u32[]{:S(2)}, u32[]{:S(2)}) collective-permute-start(bf16[8,64,576]{2,1,0:T(8,128)(2,1)S(1)} %add_convert_fusion), channel_id=1, source_target_pairs={{0,64},{1,65},{2,66},{3,67},{4,68},{5,69},{6,70},{7,71},{8,72},{9,... | collective-permute-start | bytes 1769480 | tf_op jit(solution)/shard_map/ppermute | solution.py:219
  122.2 14.2 %copy-start.2 = (f32[1,576]{1,0:T(1,128)S(1)}, f32[1,576]{1,0:T(1,128)}, u32[]{:S(2)}) copy-start(f32[1,576]{1,0:T(1,128)} %param.9) | copy-start | bytes 6916
  122.3 7.2 %collective-permute-start.30 = (bf16[64,576]{1,0:T(8,128)(2,1)S(1)}, bf16[64,576]{1,0:T(8,128)(2,1)S(1)}, u32[]{:S(2)}, u32[]{:S(2)}) collective-permute-start(bf16[64,576]{1,0:T(8,128)(2,1)S(1)} %get-tuple-element.30), channel_id=1, source_target_pairs={{0,56},{4,60},{8,0},{12,4},{16,8},{20,12},{24,16},{28,20},{32,24},... | collective-permute-start | bytes 221192 | tf_op jit(solution)/shard_map/ppermute | solution.py:229
  124.4 7.0 %collective-permute-start.27 = (bf16[2,64,576]{2,1,0:T(8,128)(2,1)S(1)}, bf16[2,64,576]{2,1,0:T(8,128)(2,1)S(1)}, u32[]{:S(2)}, u32[]{:S(2)}) collective-permute-start(bf16[2,64,576]{2,1,0:T(8,128)(2,1)S(1)} %pad_maximum_fusion), channel_id=1, source_target_pairs={{0,8},{4,12},{8,16},{12,20},{16,24},{20,28},{24,32},{28,36},{32,40... | collective-permute-start | bytes 442376 | tf_op jit(solution)/shard_map/ppermute | solution.py:228
  124.7 11.7 %collective-permute-start.26 = (bf16[64,576]{1,0:T(8,128)(2,1)S(1)}, bf16[64,576]{1,0:T(8,128)(2,1)S(1)}, u32[]{:S(2)}, u32[]{:S(2)}) collective-permute-start(bf16[64,576]{1,0:T(8,128)(2,1)S(1)} %get-tuple-element.29), channel_id=1, source_target_pairs={{0,40},{4,44},{8,48},{12,52},{16,56},{20,60},{24,0},{28,4},{32,8},... | collective-permute-start | bytes 221192 | tf_op jit(solution)/shard_map/ppermute | solution.py:230
  129.5 7.0 %collective-permute-start.31 = (bf16[64,576]{1,0:T(8,128)(2,1)S(1)}, bf16[64,576]{1,0:T(8,128)(2,1)S(1)}, u32[]{:S(2)}, u32[]{:S(2)}) collective-permute-start(bf16[64,576]{1,0:T(8,128)(2,1)S(1)} %fusion.1), channel_id=1, source_target_pairs={{0,56},{4,60},{8,0},{12,4},{16,8},{20,12},{24,16},{28,20},{32,24},... | collective-permute-start | bytes 221192 | tf_op jit(solution)/shard_map/ppermute | solution.py:233
  131.5 9.4 %collective-permute-start.28 = (bf16[64,576]{1,0:T(8,128)(2,1)S(1)}, bf16[64,576]{1,0:T(8,128)(2,1)S(1)}, u32[]{:S(2)}, u32[]{:S(2)}) collective-permute-start(bf16[64,576]{1,0:T(8,128)(2,1)S(1)} %get-tuple-element.27), channel_id=1, source_target_pairs={{0,24},{4,28},{8,32},{12,36},{16,40},{20,44},{24,48},{28,52},{32,5... | collective-permute-start | bytes 221192 | tf_op jit(solution)/shard_map/ppermute | solution.py:233
  133.0 8.0 %collective-permute-start.29 = (bf16[64,576]{1,0:T(8,128)(2,1)S(1)}, bf16[64,576]{1,0:T(8,128)(2,1)S(1)}, u32[]{:S(2)}, u32[]{:S(2)}) collective-permute-start(bf16[64,576]{1,0:T(8,128)(2,1)S(1)} %get-tuple-element.28), channel_id=1, source_target_pairs={{0,8},{4,12},{8,16},{12,20},{16,24},{20,28},{24,32},{28,36},{32,40... | collective-permute-start | bytes 221192 | tf_op jit(solution)/shard_map/ppermute | solution.py:233

commit v4 on v3

--- a/solution.py
+++ b/solution.py
@@ -34,7 +34,7 @@
     return [pltpu.with_memory_space_constraint(v, pltpu.VMEM) for v in values]
 
 
-def call(kernel, where, vmem, rest, out, scratch):
+def call(kernel, where, vmem, rest, out, scratch, aliases=None):
     return pl.pallas_call(
         kernel,
         in_specs=[SMEM] + [VMEM] * len(vmem) + [ANY] * len(rest),
@@ -42,6 +42,7 @@
         out_shape=tuple(pltpu.VMEM(shape, dtype) for shape, dtype in out),
         scratch_shapes=scratch,
         compiler_params=PARAMS,
+        input_output_aliases={1 + i: o for i, o in (aliases or {}).items()},
     )(where, *in_vmem(vmem), *rest)
 
 
@@ -70,37 +71,29 @@
     return call(kernel, where, [], [decoders], out, [pltpu.SemaphoreType.DMA((3 * n,))])
 
 
-def encode(where, pieces, shifts, weight, start, bias):
-    size = 2 * weight.shape[0] // (2 * CHIPS)
-    tokens = pieces[0].shape[1]
+def encode(where, pieces, weight, start, bias):
+    half = weight.shape[0] // (2 * CHIPS)
+    tokens = pieces[0][0].shape[1]
     width = weight.shape[1]
-    count = len(shifts)
-    vmem = list(pieces) + ([start] if start is not None else []) + ([bias] if bias is not None else [])
-
-    def kernel(where_ref, *refs):
-        pieces_refs, refs = refs[: len(pieces)], refs[len(pieces) :]
+    arrays = [array for array, _ in pieces]
+    halves = [place for _, places in pieces for place in places]
+    vmem = [weight] + arrays + ([start] if start is not None else []) + ([bias] if bias is not None else [])
+
+    def kernel(where_ref, weight_ref, *refs):
+        pieces_refs, refs = refs[: len(arrays)], refs[len(arrays) :]
         if start is not None:
             start_ref, *refs = refs
         if bias is not None:
             bias_ref, *refs = refs
-        weight_ref, out_ref, rows, sems = refs
-        sign = 1 - 2 * where_ref[0]
-        copies = []
-        for i, shift in enumerate(shifts):
-            at = (where_ref[1] + sign * shift) & (CHIPS - 1)
-            copies.append(
-                pltpu.make_async_copy(
-                    weight_ref.at[pl.ds(pl.multiple_of(at * size, 16), size)],
-                    rows.at[pl.ds(i * size, size)],
-                    sems.at[i],
-                )
-            )
-        for copy in copies:
-            copy.start()
+        (out_ref,) = refs
+        core = where_ref[0]
+        sign = 1 - 2 * core
+        rows = []
+        for shift, other in halves:
+            at = 2 * ((where_ref[1] + sign * shift) & (CHIPS - 1)) + (1 - core if other else core)
+            rows.append(weight_ref[pl.ds(pl.multiple_of(at * half, 16), half), :])
         block = jnp.concatenate([p[...] for p in pieces_refs]).T
-        for copy in copies:
-            copy.wait()
-        hidden = jnp.dot(block, rows[...], preferred_element_type=jnp.float32)
+        hidden = jnp.dot(block, jnp.concatenate(rows), preferred_element_type=jnp.float32)
         if start is not None:
             hidden = hidden + start_ref[...]
         if bias is not None:
@@ -108,13 +101,12 @@
         out_ref[...] = hidden.astype(out_ref.dtype)
 
     out = [((tokens, width), jnp.float32 if bias is None else jnp.bfloat16)]
-    scratch = [pltpu.VMEM((count * size, width), weight.dtype), pltpu.SemaphoreType.DMA((count,))]
-    return call(kernel, where, vmem, [weight], out, scratch)[0]
-
-
-def gather_and_encode(where, core, own, weight, bias):
+    return call(kernel, where, vmem, [], out, [])[0]
+
+
+def gather_and_encode(where, own, weight, bias):
     other = lax.ppermute(own, "feat", SWAP)
-    block = jnp.where(core == 0, jnp.concatenate([own, other]), jnp.concatenate([other, own]))
+    block = jnp.concatenate([own, other])
     b1 = lax.ppermute(block, "feat", both(1))
     b2 = lax.ppermute(block, "feat", both(2))
     b3 = lax.ppermute(b1, "feat", both(2))
@@ -122,9 +114,16 @@
     s1 = lax.ppermute(b1, "feat", SWAP)
     s2 = lax.ppermute(b2, "feat", SWAP)
     s3 = lax.ppermute(b3, "feat", SWAP)
-    sums = encode(where, [block, b1, s1], (0, -1, 1), weight, None, None)
-    sums = encode(where, [b2, s2, b3], (-2, 2, -3), weight, sums, None)
-    return encode(where, [s3, b4], (3, -4), weight, sums, bias)
+
+    def direct(piece, shift):
+        return piece, [(shift, 0), (shift, 1)]
+
+    def swapped(piece, shift):
+        return piece, [(shift, 1), (shift, 0)]
+
+    first = [direct(block, 0), direct(b1, -1), swapped(s1, 1), direct(b2, -2), swapped(s2, 2)]
+    sums = encode(where, first, weight, None, None)
+    return encode(where, [direct(b3, -3), swapped(s3, 3), direct(b4, -4)], weight, sums, bias)
 
 
 def gather_rows(own):
@@ -137,27 +136,51 @@
     return own, before, after, first, second
 
 
+def spread(where_ref, value, j, mine_ref, theirs_ref):
+    core, chip, row = where_ref[0], where_ref[1], where_ref[2]
+    for h in range(2):
+        at = (2 * ((row + j) & (ROWS - 1)) + h - chip) & (CHIPS - 1)
+        low = value[2 * h * PIECE : (2 * h + 1) * PIECE]
+        high = value[(2 * h + 1) * PIECE : (2 * h + 2) * PIECE]
+        mine_ref[at] = jnp.where(core == 0, low, high)
+        theirs_ref[at] = jnp.where(core == 0, high, low).astype(jnp.bfloat16)
+
+
+def decode_far(where, rows, turned, start, mine, theirs):
+    first, second = rows
+
+    def kernel(where_ref, first, second, turned_ref, start_ref, mine_in, theirs_in, mine_ref, theirs_ref):
+        block = jnp.concatenate([first[...], second[...]])
+        value = jnp.dot(block, turned_ref[...], preferred_element_type=jnp.float32) + start_ref[2]
+        spread(where_ref, value, 2, mine_ref, theirs_ref)
+
+    out = [(mine.shape, mine.dtype), (theirs.shape, theirs.dtype)]
+    return call(kernel, where, [first, second, turned, start, mine, theirs], [], out, [], {4: 0, 5: 1})
+
+
 def decode(where, rows, weights, start, split, only=None):
     tokens, count = rows[0].shape
     width = weights[0].shape[0]
     n = len(weights)
+    m = len(rows)
     has_start = start is not None
 
-    def kernel(where_ref, own, before, after, first, second, *rest):
+    def kernel(where_ref, *refs):
         if only is None:
-            work(where_ref, own, before, after, first, second, *rest)
+            work(where_ref, *refs)
         else:
 
             @pl.when(where_ref[4] == only)
             def _():
-                work(where_ref, own, before, after, first, second, *rest)
-
-    def work(where_ref, own, before, after, first, second, *rest):
-        core, chip, row = where_ref[0], where_ref[1], where_ref[2]
-        weight = rest[0][...]
-        for other in rest[1:n]:
+                work(where_ref, *refs)
+
+    def work(where_ref, *refs):
+        own, before, after = refs[:3]
+        blocks = [(0, (own,)), (1, (after,)), (3, (before,))] + ([(2, refs[3:m])] if m == 5 else [])
+        weight = refs[m][...]
+        for other in refs[m + 1 : m + n]:
             weight = weight + other[...]
-        rest = rest[n:]
+        rest = refs[m + n :]
         if has_start:
             start_ref, *rest = rest
         if split:
@@ -165,20 +188,15 @@
         else:
             out_ref, turned = rest
         turned[...] = weight.T
-        for j, parts in enumerate(((own,), (after,), (first, second), (before,))):
+        for j, parts in blocks:
             block = parts[0][...] if len(parts) == 1 else jnp.concatenate([p[...] for p in parts])
             value = jnp.dot(block, turned[...], preferred_element_type=jnp.float32)
             if has_start:
                 value = value + start_ref[j]
-            if not split:
+            if split:
+                spread(where_ref, value, j, mine_ref, theirs_ref)
+            else:
                 out_ref[j] = value
-                continue
-            for h in range(2):
-                at = (2 * ((row + j) & (ROWS - 1)) + h - chip) & (CHIPS - 1)
-                low = value[2 * h * PIECE : (2 * h + 1) * PIECE]
-                high = value[(2 * h + 1) * PIECE : (2 * h + 2) * PIECE]
-                mine_ref[at] = jnp.where(core == 0, low, high)
-                theirs_ref[at] = jnp.where(core == 0, high, low).astype(jnp.bfloat16)
 
     if split:
         shape = (CHIPS, PIECE, width)
@@ -186,7 +204,10 @@
     else:
         out = [((ROWS, tokens, width), jnp.float32)]
     vmem = list(rows) + list(weights) + ([start] if has_start else [])
-    return call(kernel, where, vmem, [], out, [pltpu.VMEM((count, width), jnp.bfloat16)])
+    turned = ((count, width), jnp.bfloat16)
+    if m == 3:
+        return call(kernel, where, vmem, [], out + [turned], [])
+    return call(kernel, where, vmem, [], out, [pltpu.VMEM(*turned)])
 
 
 def per_device(inputs, enc_weight, enc_bias, dec_weight, dec_bias):
@@ -203,7 +224,7 @@
     lent_a = lax.ppermute(lent_a, "sec", [(2, 1), (3, 0)])
     lent_b = lax.ppermute(lent_b, "sec", [(3, 2)])
 
-    features = gather_and_encode(where, core, inputs[0].T, enc_weight[0], enc_bias)
+    features = gather_and_encode(where, inputs[0].T, enc_weight[0], enc_bias)
 
     every_own = gather_rows(features)
     brought = lax.ppermute(features, "sec", [(0, 2), (1, 3)])
@@ -220,7 +241,8 @@
 
     own_weight, brought_weight = copy_weights(where, decoders, (4, 5))
     (start,) = decode(where, every_own, (own_weight,), None, False)
-    mine, theirs = decode(where, every_brought, (brought_weight,), start, True)
+    mine, theirs, turned = decode(where, every_brought[:3], (brought_weight,), start, True)
+    mine, theirs = decode_far(where, every_brought[3:], turned, start, mine, theirs)
     pair = mine + lax.ppermute(theirs, "feat", SWAP).astype(jnp.float32)
     for back in (back_a, back_b, back_c):
         pair = pair + back.astype(jnp.float32)

time: 144 us -> 142 us (0.986)
  Pallas kernels: 18 us -> 16.4 us
    pallas_call x9, Pallas kernels: 18 us -> 16.4 us  [call(): pl.pallas_call(kernel, in_specs=[SMEM] + [VMEM] * len(vmem) + [ANY] * len...]
  transfers between devices with their start and end apart: 32 -> 32, of which waited for: 12 -> 12; matrix products, arithmetic and copies ran while one was open for 0% -> 0% of each run, Pallas kernels for 13% -> 12%
where the time goes in v4:
time: 142 us; the launch traced here: 140 us
  waiting for transfers between devices  73.5 us (52%)
  starting transfers between devices  47 us (33%)
  Pallas kernels  16.4 us (12%)
  other arithmetic  2.42 us (2%)
    ppermute x1, waiting for transfers between devices, per_device(): brought = lax.ppermute(features, 'sec', [(0, 2), (1, 3)])  21.9 us
    ppermute x1, waiting for transfers between devices, per_device(): back_a = lax.ppermute(pair, 'sec', [(0, 3), (1, 2)])  16.8 us
    pallas_call x9, Pallas kernels, call(): pl.pallas_call(kernel, in_specs=[SMEM] + [VMEM] * len(vmem) + [ANY] * len...  16.4 us
    ppermute x2, waiting for transfers between devices, gather_rows(): before = lax.ppermute(own, 'row', ring(1))  13.8 us
    ppermute x3, starting transfers between devices, per_device(): got.append(lax.ppermute(merged, 'feat', hop(shift)))  6.93 us
    ppermute x2, starting transfers between devices, gather_rows(): second = lax.ppermute(after_half, 'row', ring(-1))  4.85 us
    ppermute x1, starting transfers between devices, per_device(): got = [lax.ppermute(send[5], 'feat', hop(-3))]  4.73 us
    ppermute x2, starting transfers between devices, gather_rows(): after = lax.ppermute(own, 'row', ring(-1))  4.68 us
  transfers between devices with their start and end apart: 32, of which 12 were waited for; matrix products, arithmetic and copies ran while one was open for 0% of the time, Pallas kernels for 12%

profile of v4, /device:TPU:6, one launch (start us, length us, event | category | flops | bytes accessed | tf_op | source)
XLA Modules:
  0.0 139.9 jit_solution(2228731617356532123)
XLA Ops:
  0.0 1.5 %collective-permute-done = bf16[144,256]{1,0:T(8,128)(2,1)S(1)} collective-permute-done((bf16[144,256]{1,0:T(8,128)(2,1)}, bf16[144,256]{1,0:T(8,128)(2,1)S(1)}, u32[]{:S(2)}, u32[]{:S(2)}) %collective-permute-start) | collective-permute-done | bytes 73760 | tf_op jit(solution)/shard_map/ppermute | solution.py:108
  1.5 0.9 pad_maximum_fusion.1.refs_0_
  2.4 2.0 %collective-permute-start.1 = (bf16[288,256]{1,0:T(8,128)(2,1)S(1)}, bf16[288,256]{1,0:T(8,128)(2,1)S(1)}, u32[]{:S(2)}, u32[]{:S(2)}) collective-permute-start(bf16[288,256]{1,0:T(8,128)(2,1)S(1)} %pad_maximum_fusion.1.refs_0_), channel_id=1, source_target_pairs={{0,8},{4,60},{8,16},{12,4},{16,24},{20,12},{24,32},{28,20},{32,40}... | collective-permute-start | bytes 442376 | tf_op jit(solution)/shard_map/ppermute | solution.py:110
  4.4 3.3 %collective-permute-start.4 = (bf16[288,256]{1,0:T(8,128)(2,1)S(1)}, bf16[288,256]{1,0:T(8,128)(2,1)S(1)}, u32[]{:S(2)}, u32[]{:S(2)}) collective-permute-start(bf16[288,256]{1,0:T(8,128)(2,1)S(1)} %pad_maximum_fusion.1.refs_0_), channel_id=1, source_target_pairs={{0,16},{4,52},{8,24},{12,60},{16,32},{20,4},{24,40},{28,12},{32,48... | collective-permute-start | bytes 442376 | tf_op jit(solution)/shard_map/ppermute | solution.py:111
  7.6 3.8 %collective-permute-done.1.refs_1_ = bf16[288,256]{1,0:T(8,128)(2,1)S(1)} collective-permute-done((bf16[288,256]{1,0:T(8,128)(2,1)S(1)}, bf16[288,256]{1,0:T(8,128)(2,1)S(1)}, u32[]{:S(2)}, u32[]{:S(2)}) %collective-permute-start.1) | collective-permute-done | bytes 147488 | tf_op jit(solution)/shard_map/ppermute | solution.py:110
  11.4 0.0 collective-permute-start.2
  11.4 1.5 %collective-permute-start.6 = (bf16[288,256]{1,0:T(8,128)(2,1)S(1)}, bf16[288,256]{1,0:T(8,128)(2,1)S(1)}, u32[]{:S(2)}, u32[]{:S(2)}) collective-permute-start(bf16[288,256]{1,0:T(8,128)(2,1)S(1)} %collective-permute-done.1.refs_1_), channel_id=1, source_target_pairs={{0,4},{4,0},{8,12},{12,8},{16,20},{20,16},{24,28},{28,24},{32,36},... | collective-permute-start | bytes 442376 | tf_op jit(solution)/shard_map/ppermute | solution.py:114
  12.9 2.1 %collective-permute-done.4.refs_3_ = bf16[288,256]{1,0:T(8,128)(2,1)S(1)} collective-permute-done((bf16[288,256]{1,0:T(8,128)(2,1)S(1)}, bf16[288,256]{1,0:T(8,128)(2,1)S(1)}, u32[]{:S(2)}, u32[]{:S(2)}) %collective-permute-start.4) | collective-permute-done | bytes 147488 | tf_op jit(solution)/shard_map/ppermute | solution.py:111
  15.0 0.0 collective-permute-start.7
  15.0 2.1 %collective-permute-start.5 = (bf16[288,256]{1,0:T(8,128)(2,1)S(1)}, bf16[288,256]{1,0:T(8,128)(2,1)S(1)}, u32[]{:S(2)}, u32[]{:S(2)}) collective-permute-start(bf16[288,256]{1,0:T(8,128)(2,1)S(1)} %collective-permute-done.4.refs_3_), channel_id=1, source_target_pairs={{0,16},{4,52},{8,24},{12,60},{16,32},{20,4},{24,40},{28,12},{32,48... | collective-permute-start | bytes 442376 | tf_op jit(solution)/shard_map/ppermute | solution.py:113
  17.1 2.2 %collective-permute-done.2.refs_0_ = bf16[288,256]{1,0:T(8,128)(2,1)S(1)} collective-permute-done((bf16[288,256]{1,0:T(8,128)(2,1)S(1)}, bf16[288,256]{1,0:T(8,128)(2,1)S(1)}, u32[]{:S(2)}, u32[]{:S(2)}) %collective-permute-start.2) | collective-permute-done | bytes 147488 | tf_op jit(solution)/shard_map/ppermute | solution.py:112
  19.2 0.1 stack.30.where_ref
  19.3 2.5 %shard_map.61 = (bf16[576,1024]{1,0:T(8,128)(2,1)S(1)}, bf16[576,1024]{1,0:T(8,128)(2,1)S(1)}) custom-call(s32[7]{0:T(128)S(1)} %stack.30.where_ref, bf16[4,576,1024]{2,1,0:T(8,128)(2,1)} %bitcast.47), custom_call_target="tpu_custom_call" | custom-call | tf_op jit(solution)/shard_map/pallas_call | solution.py:38
  21.8 2.5 %collective-permute-start.18 = (bf16[576,1024]{1,0:T(8,128)(2,1)S(1)}, bf16[576,1024]{1,0:T(8,128)(2,1)S(1)}, u32[]{:S(2)}, u32[]{:S(2)}) collective-permute-start(bf16[576,1024]{1,0:T(8,128)(2,1)S(1)} %get-tuple-element.25), channel_id=1, source_target_pairs={{128,64},{192,0},{129,65},{193,1},{130,66},{194,2},{131,67},{195,3... | collective-permute-start | bytes 3538952 | tf_op jit(solution)/shard_map/ppermute | solution.py:224
  24.2 0.0 collective-permute-done.6.refs_2_
  24.3 2.9 %collective-permute-start.19 = (bf16[576,1024]{1,0:T(8,128)(2,1)S(1)}, bf16[576,1024]{1,0:T(8,128)(2,1)S(1)}, u32[]{:S(2)}, u32[]{:S(2)}) collective-permute-start(bf16[576,1024]{1,0:T(8,128)(2,1)S(1)} %get-tuple-element.26), channel_id=1, source_target_pairs={{192,128},{193,129},{194,130},{195,131},{196,132},{197,133},{198,1... | collective-permute-start | bytes 3538952 | tf_op jit(solution)/shard_map/ppermute | solution.py:225
  27.1 0.0 collective-permute-done.7.refs_4_
  27.2 0.0 copy-start.1
  27.2 1.6 %shard_map.55.refs_3_ = f32[256,1024]{1,0:T(8,128)S(1)} custom-call(s32[7]{0:T(128)S(1)} %stack.30.where_ref, bf16[2304,1024]{1,0:T(8,128)(2,1)S(1)} %bitcast.45, bf16[288,256]{1,0:T(8,128)(2,1)S(1)} %pad_maximum_fusion.1.refs_0_, bf16[288,256]{1,0:T(8,128)(2,1)S(1)} %collective-permute-done.1.refs_1_, bf16[288,256]{1,0:T(8,128)(2,1)S(1)} %collective-permute-done.6.refs_2_, ...), custom_call_target="tpu_custom_call" | custom-call | tf_op jit(solution)/shard_map/pallas_call | solution.py:38
  28.7 0.0 collective-permute-done.5.refs_2_
  28.8 1.3 shard_map.56.refs_0_
  30.1 1.7 %collective-permute-start.13 = (bf16[256,1024]{1,0:T(8,128)(2,1)S(1)}, bf16[256,1024]{1,0:T(8,128)(2,1)S(1)}, u32[]{:S(2)}, u32[]{:S(2)}) collective-permute-start(bf16[256,1024]{1,0:T(8,128)(2,1)S(1)} %shard_map.56.refs_0_), channel_id=1, source_target_pairs={{0,1},{1,2},{2,3},{3,0},{4,5},{5,6},{6,7},{7,4},{8,9},{9,10},{10,1... | collective-permute-start | bytes 1572872 | tf_op jit(solution)/shard_map/ppermute | solution.py:131
  31.7 0.7 collective-permute-start.23
  32.5 1.7 %collective-permute-start.14 = (bf16[256,1024]{1,0:T(8,128)(2,1)S(1)}, bf16[256,1024]{1,0:T(8,128)(2,1)S(1)}, u32[]{:S(2)}, u32[]{:S(2)}) collective-permute-start(bf16[256,1024]{1,0:T(8,128)(2,1)S(1)} %shard_map.56.refs_0_), channel_id=1, source_target_pairs={{0,3},{1,0},{2,1},{3,2},{4,7},{5,4},{6,5},{7,6},{8,11},{9,8},{10,9... | collective-permute-start | bytes 1572872 | tf_op jit(solution)/shard_map/ppermute | solution.py:132
  34.2 11.0 %collective-permute-done.13.refs_1_ = bf16[256,1024]{1,0:T(8,128)(2,1)S(1)} collective-permute-done((bf16[256,1024]{1,0:T(8,128)(2,1)S(1)}, bf16[256,1024]{1,0:T(8,128)(2,1)S(1)}, u32[]{:S(2)}, u32[]{:S(2)}) %collective-permute-start.13) | collective-permute-done | bytes 524320 | tf_op jit(solution)/shard_map/ppermute | solution.py:131
  45.2 1.3 collective-permute-start.8
  46.5 0.0 collective-permute-done.14.refs_2_
  46.5 1.1 collective-permute-start.15
  47.6 21.9 %collective-permute-done.8.refs_0_ = bf16[256,1024]{1,0:T(8,128)(2,1)S(1)} collective-permute-done((bf16[256,1024]{1,0:T(8,128)(2,1)S(1)}, bf16[256,1024]{1,0:T(8,128)(2,1)S(1)}, u32[]{:S(2)}, u32[]{:S(2)}) %collective-permute-start.8) | collective-permute-done | bytes 524320 | tf_op jit(solution)/shard_map/ppermute | solution.py:230
  69.6 1.7 %collective-permute-start.16 = (bf16[128,1024]{1,0:T(8,128)(2,1)S(1)}, bf16[128,1024]{1,0:T(8,128)(2,1)S(1)}, u32[]{:S(2)}, u32[]{:S(2)}) collective-permute-start(bf16[128,1024]{1,0:T(8,128)(2,1)S(1)} %slice.59), channel_id=1, source_target_pairs={{0,3},{1,0},{2,1},{3,2},{4,7},{5,4},{6,5},{7,6},{8,11},{9,8},{10,9... | collective-permute-start | bytes 786440 | tf_op jit(solution)/shard_map/ppermute | solution.py:135
  71.3 0.3 collective-permute-start.9
  71.6 0.0 collective-permute-done.19.refs_6_
  71.6 3.0 %collective-permute-start.11 = (bf16[256,1024]{1,0:T(8,128)(2,1)S(1)}, bf16[256,1024]{1,0:T(8,128)(2,1)S(1)}, u32[]{:S(2)}, u32[]{:S(2)}) collective-permute-start(bf16[256,1024]{1,0:T(8,128)(2,1)S(1)} %collective-permute-done.8.refs_0_), channel_id=1, source_target_pairs={{0,3},{1,0},{2,1},{3,2},{4,7},{5,4},{6,5},{7,6},{8,11},{9,8},{10,9... | collective-permute-start | bytes 1572872 | tf_op jit(solution)/shard_map/ppermute | solution.py:132
  74.6 4.2 %collective-permute-done.16.refs_4_ = bf16[128,1024]{1,0:T(8,128)(2,1)S(1)} collective-permute-done((bf16[128,1024]{1,0:T(8,128)(2,1)S(1)}, bf16[128,1024]{1,0:T(8,128)(2,1)S(1)}, u32[]{:S(2)}, u32[]{:S(2)}) %collective-permute-start.16) | collective-permute-done | bytes 262176 | tf_op jit(solution)/shard_map/ppermute | solution.py:135
  78.8 2.6 %shard_map.62 = (f32[8,64,576]{2,1,0:T(8,128)S(1)}, bf16[8,64,576]{2,1,0:T(8,128)(2,1)S(1)}) custom-call(s32[7]{0:T(128)S(1)} %stack.30.where_ref, bf16[256,1024]{1,0:T(8,128)(2,1)S(1)} %shard_map.56.refs_0_, bf16[256,1024]{1,0:T(8,128)(2,1)S(1)} %collective-permute-done.13.refs_1_, bf16[256,1024]{1,0:T(8,128)(2,1)S(1)} %collective-permute-done.14.refs_2_, ...), custom_call_target="tpu_custom_call" | custom-call | tf_op jit(solution)/shard_map/pallas_call | solution.py:38
  81.4 0.1 collective-permute-start.20
  81.5 0.6 shard_map.63
  82.0 0.7 collective-permute-start.24
  82.8 2.8 %collective-permute-done.9.refs_1_ = bf16[256,1024]{1,0:T(8,128)(2,1)S(1)} collective-permute-done((bf16[256,1024]{1,0:T(8,128)(2,1)S(1)}, bf16[256,1024]{1,0:T(8,128)(2,1)S(1)}, u32[]{:S(2)}, u32[]{:S(2)}) %collective-permute-start.9) | collective-permute-done | bytes 524320 | tf_op jit(solution)/shard_map/ppermute | solution.py:131
  85.6 0.1 collective-permute-start.10
  85.6 2.8 %collective-permute-done.11.refs_2_ = bf16[256,1024]{1,0:T(8,128)(2,1)S(1)} collective-permute-done((bf16[256,1024]{1,0:T(8,128)(2,1)S(1)}, bf16[256,1024]{1,0:T(8,128)(2,1)S(1)}, u32[]{:S(2)}, u32[]{:S(2)}) %collective-permute-start.11) | collective-permute-done | bytes 524320 | tf_op jit(solution)/shard_map/ppermute | solution.py:132
  88.4 3.1 %collective-permute-start.12 = (bf16[128,1024]{1,0:T(8,128)(2,1)S(1)}, bf16[128,1024]{1,0:T(8,128)(2,1)S(1)}, u32[]{:S(2)}, u32[]{:S(2)}) collective-permute-start(bf16[128,1024]{1,0:T(8,128)(2,1)S(1)} %slice.57), channel_id=1, source_target_pairs={{0,3},{1,0},{2,1},{3,2},{4,7},{5,4},{6,5},{7,6},{8,11},{9,8},{10,9... | collective-permute-start | bytes 786440 | tf_op jit(solution)/shard_map/ppermute | solution.py:135
  91.5 2.2 %shard_map.57 = (bf16[576,1024]{1,0:T(8,128)(2,1)S(1)}, bf16[576,1024]{1,0:T(8,128)(2,1)S(1)}) custom-call(s32[7]{0:T(128)S(1)} %stack.30.where_ref, bf16[4,576,1024]{2,1,0:T(8,128)(2,1)} %bitcast.48), custom_call_target="tpu_custom_call" | custom-call | tf_op jit(solution)/shard_map/pallas_call | solution.py:38
  93.7 2.5 %shard_map.58.refs_4_.start_ref = f32[4,256,576]{2,1,0:T(8,128)S(1)} custom-call(s32[7]{0:T(128)S(1)} %stack.30.where_ref, bf16[256,1024]{1,0:T(8,128)(2,1)S(1)} %shard_map.56.refs_0_, bf16[256,1024]{1,0:T(8,128)(2,1)S(1)} %collective-permute-done.13.refs_1_, bf16[256,1024]{1,0:T(8,128)(2,1)S(1)} %collective-permute-done.14.refs_2_, ...), custom_call_target="tpu_custom_call" | custom-call | tf_op jit(solution)/shard_map/pallas_call | solution.py:38
  96.2 2.1 %shard_map.59 = (f32[8,64,576]{2,1,0:T(8,128)S(1)}, bf16[8,64,576]{2,1,0:T(8,128)(2,1)S(1)}, bf16[1024,576]{1,0:T(8,128)(2,1)S(1)}) custom-call(s32[7]{0:T(128)S(1)} %stack.30.where_ref, bf16[256,1024]{1,0:T(8,128)(2,1)S(1)} %collective-permute-done.8.refs_0_, bf16[256,1024]{1,0:T(8,128)(2,1)S(1)} %collective-permute-done.9.refs_1_, ...), custom_call_target="tpu_custom_call" | custom-call | tf_op jit(solution)/shard_map/pallas_call | solution.py:38
  98.3 1.1 shard_map.60
  99.4 0.1 collective-permute-start.17
  99.5 0.1 add_convert_fusion.1
  99.7 1.3 collective-permute-start.21
  101.0 1.3 collective-permute-start.22
  102.3 0.1 add_convert_fusion
  102.5 0.7 collective-permute-start.25
  103.2 16.8 %collective-permute-done.21 = bf16[8,64,576]{2,1,0:T(8,128)(2,1)S(1)} collective-permute-done((bf16[8,64,576]{2,1,0:T(8,128)(2,1)S(1)}, bf16[8,64,576]{2,1,0:T(8,128)(2,1)S(1)}, u32[]{:S(2)}, u32[]{:S(2)}) %collective-permute-start.21) | collective-permute-done | bytes 589856 | tf_op jit(solution)/shard_map/ppermute | solution.py:236
  119.9 0.1 collective-permute-done.22
  120.0 0.5 fusion.13
  120.5 0.0 copy-start.2
  120.5 2.1 %collective-permute-start.30 = (bf16[64,576]{1,0:T(8,128)(2,1)S(1)}, bf16[64,576]{1,0:T(8,128)(2,1)S(1)}, u32[]{:S(2)}, u32[]{:S(2)}) collective-permute-start(bf16[64,576]{1,0:T(8,128)(2,1)S(1)} %get-tuple-element.36), channel_id=1, source_target_pairs={{0,56},{4,60},{8,0},{12,4},{16,8},{20,12},{24,16},{28,20},{32,24},... | collective-permute-start | bytes 221192 | tf_op jit(solution)/shard_map/ppermute | solution.py:251
  122.7 0.3 collective-permute-start.27
  123.0 4.7 %collective-permute-start.26 = (bf16[64,576]{1,0:T(8,128)(2,1)S(1)}, bf16[64,576]{1,0:T(8,128)(2,1)S(1)}, u32[]{:S(2)}, u32[]{:S(2)}) collective-permute-start(bf16[64,576]{1,0:T(8,128)(2,1)S(1)} %get-tuple-element.35), channel_id=1, source_target_pairs={{0,40},{4,44},{8,48},{12,52},{16,56},{20,60},{24,0},{28,4},{32,8},... | collective-permute-start | bytes 221192 | tf_op jit(solution)/shard_map/ppermute | solution.py:252
  127.7 2.0 %collective-permute-start.31 = (bf16[64,576]{1,0:T(8,128)(2,1)S(1)}, bf16[64,576]{1,0:T(8,128)(2,1)S(1)}, u32[]{:S(2)}, u32[]{:S(2)}) collective-permute-start(bf16[64,576]{1,0:T(8,128)(2,1)S(1)} %fusion.1), channel_id=1, source_target_pairs={{0,56},{4,60},{8,0},{12,4},{16,8},{20,12},{24,16},{28,20},{32,24},... | collective-permute-start | bytes 221192 | tf_op jit(solution)/shard_map/ppermute | solution.py:255
  129.8 1.4 %collective-permute-start.28 = (bf16[64,576]{1,0:T(8,128)(2,1)S(1)}, bf16[64,576]{1,0:T(8,128)(2,1)S(1)}, u32[]{:S(2)}, u32[]{:S(2)}) collective-permute-start(bf16[64,576]{1,0:T(8,128)(2,1)S(1)} %get-tuple-element.33), channel_id=1, source_target_pairs={{0,24},{4,28},{8,32},{12,36},{16,40},{20,44},{24,48},{28,52},{32,5... | collective-permute-start | bytes 221192 | tf_op jit(solution)/shard_map/ppermute | solution.py:255
  131.2 3.5 %collective-permute-start.29 = (bf16[64,576]{1,0:T(8,128)(2,1)S(1)}, bf16[64,576]{1,0:T(8,128)(2,1)S(1)}, u32[]{:S(2)}, u32[]{:S(2)}) collective-permute-start(bf16[64,576]{1,0:T(8,128)(2,1)S(1)} %get-tuple-element.34), channel_id=1, source_target_pairs={{0,8},{4,12},{8,16},{12,20},{16,24},{20,28},{24,32},{28,36},{32,40... | collective-permute-start | bytes 221192 | tf_op jit(solution)/shard_map/ppermute | solution.py:255
  134.7 4.5 %collective-permute-done.28 = bf16[64,576]{1,0:T(8,128)(2,1)S(1)} collective-permute-done((bf16[64,576]{1,0:T(8,128)(2,1)S(1)}, bf16[64,576]{1,0:T(8,128)(2,1)S(1)}, u32[]{:S(2)}, u32[]{:S(2)}) %collective-permute-start.28) | collective-permute-done | bytes 73760 | tf_op jit(solution)/shard_map/ppermute | solution.py:255
  139.2 0.7 fusion.10
  (30 shorter events, 0.3 us)
Async XLA Ops:
  0.0 1.5 %collective-permute-start = (bf16[144,256]{1,0:T(8,128)(2,1)}, bf16[144,256]{1,0:T(8,128)(2,1)S(1)}, u32[]{:S(2)}, u32[]{:S(2)}) collective-permute-start(bf16[144,256]{1,0:T(8,128)(2,1)} %bitcast.49), channel_id=1, source_target_pairs={{0,4},{4,0},{8,12},{12,8},{16,20},{20,16},{24,28},{28,24},{32,36},... | collective-permute-start | bytes 221192 | tf_op jit(solution)/shard_map/ppermute | solution.py:108
  2.4 9.1 %collective-permute-start.1 = (bf16[288,256]{1,0:T(8,128)(2,1)S(1)}, bf16[288,256]{1,0:T(8,128)(2,1)S(1)}, u32[]{:S(2)}, u32[]{:S(2)}) collective-permute-start(bf16[288,256]{1,0:T(8,128)(2,1)S(1)} %pad_maximum_fusion.1.refs_0_), channel_id=1, source_target_pairs={{0,8},{4,60},{8,16},{12,4},{16,24},{20,12},{24,32},{28,20},{32,40}... | collective-permute-start | bytes 442376 | tf_op jit(solution)/shard_map/ppermute | solution.py:110
  4.4 10.6 %collective-permute-start.4 = (bf16[288,256]{1,0:T(8,128)(2,1)S(1)}, bf16[288,256]{1,0:T(8,128)(2,1)S(1)}, u32[]{:S(2)}, u32[]{:S(2)}) collective-permute-start(bf16[288,256]{1,0:T(8,128)(2,1)S(1)} %pad_maximum_fusion.1.refs_0_), channel_id=1, source_target_pairs={{0,16},{4,52},{8,24},{12,60},{16,32},{20,4},{24,40},{28,12},{32,48... | collective-permute-start | bytes 442376 | tf_op jit(solution)/shard_map/ppermute | solution.py:111
  11.4 7.8 %collective-permute-start.2 = (bf16[288,256]{1,0:T(8,128)(2,1)S(1)}, bf16[288,256]{1,0:T(8,128)(2,1)S(1)}, u32[]{:S(2)}, u32[]{:S(2)}) collective-permute-start(bf16[288,256]{1,0:T(8,128)(2,1)S(1)} %collective-permute-done.1.refs_1_), channel_id=1, source_target_pairs={{0,16},{4,52},{8,24},{12,60},{16,32},{20,4},{24,40},{28,12},{32,48... | collective-permute-start | bytes 442376 | tf_op jit(solution)/shard_map/ppermute | solution.py:112
  11.4 12.8 %collective-permute-start.6 = (bf16[288,256]{1,0:T(8,128)(2,1)S(1)}, bf16[288,256]{1,0:T(8,128)(2,1)S(1)}, u32[]{:S(2)}, u32[]{:S(2)}) collective-permute-start(bf16[288,256]{1,0:T(8,128)(2,1)S(1)} %collective-permute-done.1.refs_1_), channel_id=1, source_target_pairs={{0,4},{4,0},{8,12},{12,8},{16,20},{20,16},{24,28},{28,24},{32,36},... | collective-permute-start | bytes 442376 | tf_op jit(solution)/shard_map/ppermute | solution.py:114
  15.0 12.1 %collective-permute-start.7 = (bf16[288,256]{1,0:T(8,128)(2,1)S(1)}, bf16[288,256]{1,0:T(8,128)(2,1)S(1)}, u32[]{:S(2)}, u32[]{:S(2)}) collective-permute-start(bf16[288,256]{1,0:T(8,128)(2,1)S(1)} %collective-permute-done.4.refs_3_), channel_id=1, source_target_pairs={{0,4},{4,0},{8,12},{12,8},{16,20},{20,16},{24,28},{28,24},{32,36},... | collective-permute-start | bytes 442376 | tf_op jit(solution)/shard_map/ppermute | solution.py:115
  15.0 13.7 %collective-permute-start.5 = (bf16[288,256]{1,0:T(8,128)(2,1)S(1)}, bf16[288,256]{1,0:T(8,128)(2,1)S(1)}, u32[]{:S(2)}, u32[]{:S(2)}) collective-permute-start(bf16[288,256]{1,0:T(8,128)(2,1)S(1)} %collective-permute-done.4.refs_3_), channel_id=1, source_target_pairs={{0,16},{4,52},{8,24},{12,60},{16,32},{20,4},{24,40},{28,12},{32,48... | collective-permute-start | bytes 442376 | tf_op jit(solution)/shard_map/ppermute | solution.py:113
  19.2 9.5 %collective-permute-start.3 = (bf16[288,256]{1,0:T(8,128)(2,1)S(1)}, bf16[288,256]{1,0:T(8,128)(2,1)S(1)}, u32[]{:S(2)}, u32[]{:S(2)}) collective-permute-start(bf16[288,256]{1,0:T(8,128)(2,1)S(1)} %collective-permute-done.2.refs_0_), channel_id=1, source_target_pairs={{0,4},{4,0},{8,12},{12,8},{16,20},{20,16},{24,28},{28,24},{32,36},... | collective-permute-start | bytes 442376 | tf_op jit(solution)/shard_map/ppermute | solution.py:116
  19.3 7.8 %copy-start = (bf16[1,2304,1024]{2,1,0:T(8,128)(2,1)S(1)}, bf16[1,2304,1024]{2,1,0:T(8,128)(2,1)}, u32[]{:S(2)}) copy-start(bf16[1,2304,1024]{2,1,0:T(8,128)(2,1)} %param.6) | copy-start | bytes 14155780
  21.8 49.5 %collective-permute-start.18 = (bf16[576,1024]{1,0:T(8,128)(2,1)S(1)}, bf16[576,1024]{1,0:T(8,128)(2,1)S(1)}, u32[]{:S(2)}, u32[]{:S(2)}) collective-permute-start(bf16[576,1024]{1,0:T(8,128)(2,1)S(1)} %get-tuple-element.25), channel_id=1, source_target_pairs={{128,64},{192,0},{129,65},{193,1},{130,66},{194,2},{131,67},{195,3... | collective-permute-start | bytes 3538952 | tf_op jit(solution)/shard_map/ppermute | solution.py:224
  24.3 47.3 %collective-permute-start.19 = (bf16[576,1024]{1,0:T(8,128)(2,1)S(1)}, bf16[576,1024]{1,0:T(8,128)(2,1)S(1)}, u32[]{:S(2)}, u32[]{:S(2)}) collective-permute-start(bf16[576,1024]{1,0:T(8,128)(2,1)S(1)} %get-tuple-element.26), channel_id=1, source_target_pairs={{192,128},{193,129},{194,130},{195,131},{196,132},{197,133},{198,1... | collective-permute-start | bytes 3538952 | tf_op jit(solution)/shard_map/ppermute | solution.py:225
  27.2 1.6 %copy-start.1 = (f32[1,1024]{1,0:T(1,128)S(1)}, f32[1,1024]{1,0:T(1,128)}, u32[]{:S(2)}) copy-start(f32[1,1024]{1,0:T(1,128)} %refs_4_.1) | copy-start | bytes 12292
  30.1 15.1 %collective-permute-start.13 = (bf16[256,1024]{1,0:T(8,128)(2,1)S(1)}, bf16[256,1024]{1,0:T(8,128)(2,1)S(1)}, u32[]{:S(2)}, u32[]{:S(2)}) collective-permute-start(bf16[256,1024]{1,0:T(8,128)(2,1)S(1)} %shard_map.56.refs_0_), channel_id=1, source_target_pairs={{0,1},{1,2},{2,3},{3,0},{4,5},{5,6},{6,7},{7,4},{8,9},{9,10},{10,1... | collective-permute-start | bytes 1572872 | tf_op jit(solution)/shard_map/ppermute | solution.py:131
  31.7 49.7 %collective-permute-start.23 = (bf16[576,1024]{1,0:T(8,128)(2,1)S(1)}, bf16[576,1024]{1,0:T(8,128)(2,1)S(1)}, u32[]{:S(2)}, u32[]{:S(2)}) collective-permute-start(bf16[576,1024]{1,0:T(8,128)(2,1)S(1)} %get-tuple-element.25), channel_id=1, source_target_pairs={{64,0},{65,1},{66,2},{67,3},{68,4},{69,5},{70,6},{71,7},{72,8},{73... | collective-permute-start | bytes 3538952 | tf_op jit(solution)/shard_map/ppermute | solution.py:223
  32.5 14.1 %collective-permute-start.14 = (bf16[256,1024]{1,0:T(8,128)(2,1)S(1)}, bf16[256,1024]{1,0:T(8,128)(2,1)S(1)}, u32[]{:S(2)}, u32[]{:S(2)}) collective-permute-start(bf16[256,1024]{1,0:T(8,128)(2,1)S(1)} %shard_map.56.refs_0_), channel_id=1, source_target_pairs={{0,3},{1,0},{2,1},{3,2},{4,7},{5,4},{6,5},{7,6},{8,11},{9,8},{10,9... | collective-permute-start | bytes 1572872 | tf_op jit(solution)/shard_map/ppermute | solution.py:132
  45.2 24.4 %collective-permute-start.8 = (bf16[256,1024]{1,0:T(8,128)(2,1)S(1)}, bf16[256,1024]{1,0:T(8,128)(2,1)S(1)}, u32[]{:S(2)}, u32[]{:S(2)}) collective-permute-start(bf16[256,1024]{1,0:T(8,128)(2,1)S(1)} %shard_map.56.refs_0_), channel_id=1, source_target_pairs={{0,128},{64,192},{1,129},{65,193},{2,130},{66,194},{3,131},{67,195... | collective-permute-start | bytes 1572872 | tf_op jit(solution)/shard_map/ppermute | solution.py:230
  46.5 28.0 %collective-permute-start.15 = (bf16[128,1024]{1,0:T(8,128)(2,1)S(1)}, bf16[128,1024]{1,0:T(8,128)(2,1)S(1)}, u32[]{:S(2)}, u32[]{:S(2)}) collective-permute-start(bf16[128,1024]{1,0:T(8,128)(2,1)S(1)} %slice.58), channel_id=1, source_target_pairs={{0,1},{1,2},{2,3},{3,0},{4,5},{5,6},{6,7},{7,4},{8,9},{9,10},{10,1... | collective-permute-start | bytes 786440 | tf_op jit(solution)/shard_map/ppermute | solution.py:134
  69.6 9.2 %collective-permute-start.16 = (bf16[128,1024]{1,0:T(8,128)(2,1)S(1)}, bf16[128,1024]{1,0:T(8,128)(2,1)S(1)}, u32[]{:S(2)}, u32[]{:S(2)}) collective-permute-start(bf16[128,1024]{1,0:T(8,128)(2,1)S(1)} %slice.59), channel_id=1, source_target_pairs={{0,3},{1,0},{2,1},{3,2},{4,7},{5,4},{6,5},{7,6},{8,11},{9,8},{10,9... | collective-permute-start | bytes 786440 | tf_op jit(solution)/shard_map/ppermute | solution.py:135
  71.3 14.2 %collective-permute-start.9 = (bf16[256,1024]{1,0:T(8,128)(2,1)S(1)}, bf16[256,1024]{1,0:T(8,128)(2,1)S(1)}, u32[]{:S(2)}, u32[]{:S(2)}) collective-permute-start(bf16[256,1024]{1,0:T(8,128)(2,1)S(1)} %collective-permute-done.8.refs_0_), channel_id=1, source_target_pairs={{0,1},{1,2},{2,3},{3,0},{4,5},{5,6},{6,7},{7,4},{8,9},{9,10},{10,1... | collective-permute-start | bytes 1572872 | tf_op jit(solution)/shard_map/ppermute | solution.py:131
  71.6 16.8 %collective-permute-start.11 = (bf16[256,1024]{1,0:T(8,128)(2,1)S(1)}, bf16[256,1024]{1,0:T(8,128)(2,1)S(1)}, u32[]{:S(2)}, u32[]{:S(2)}) collective-permute-start(bf16[256,1024]{1,0:T(8,128)(2,1)S(1)} %collective-permute-done.8.refs_0_), channel_id=1, source_target_pairs={{0,3},{1,0},{2,1},{3,2},{4,7},{5,4},{6,5},{7,6},{8,11},{9,8},{10,9... | collective-permute-start | bytes 1572872 | tf_op jit(solution)/shard_map/ppermute | solution.py:132
  81.4 18.2 %collective-permute-start.20 = (bf16[8,64,576]{2,1,0:T(8,128)(2,1)S(1)}, bf16[8,64,576]{2,1,0:T(8,128)(2,1)S(1)}, u32[]{:S(2)}, u32[]{:S(2)}) collective-permute-start(bf16[8,64,576]{2,1,0:T(8,128)(2,1)S(1)} %get-tuple-element.28), channel_id=1, source_target_pairs={{0,4},{4,0},{8,12},{12,8},{16,20},{20,16},{24,28},{28,24},{32,36},... | collective-permute-start | bytes 1769480 | tf_op jit(solution)/shard_map/ppermute | solution.py:234
  82.0 20.2 %collective-permute-start.24 = (bf16[8,64,576]{2,1,0:T(8,128)(2,1)S(1)}, bf16[8,64,576]{2,1,0:T(8,128)(2,1)S(1)}, u32[]{:S(2)}, u32[]{:S(2)}) collective-permute-start(bf16[8,64,576]{2,1,0:T(8,128)(2,1)S(1)} %get-tuple-element.30), channel_id=1, source_target_pairs={{0,4},{4,0},{8,12},{12,8},{16,20},{20,16},{24,28},{28,24},{32,36},... | collective-permute-start | bytes 1769480 | tf_op jit(solution)/shard_map/ppermute | solution.py:239
  85.6 12.7 %collective-permute-start.10 = (bf16[128,1024]{1,0:T(8,128)(2,1)S(1)}, bf16[128,1024]{1,0:T(8,128)(2,1)S(1)}, u32[]{:S(2)}, u32[]{:S(2)}) collective-permute-start(bf16[128,1024]{1,0:T(8,128)(2,1)S(1)} %slice.56), channel_id=1, source_target_pairs={{0,1},{1,2},{2,3},{3,0},{4,5},{5,6},{6,7},{7,4},{8,9},{9,10},{10,1... | collective-permute-start | bytes 786440 | tf_op jit(solution)/shard_map/ppermute | solution.py:134
  88.4 9.9 %collective-permute-start.12 = (bf16[128,1024]{1,0:T(8,128)(2,1)S(1)}, bf16[128,1024]{1,0:T(8,128)(2,1)S(1)}, u32[]{:S(2)}, u32[]{:S(2)}) collective-permute-start(bf16[128,1024]{1,0:T(8,128)(2,1)S(1)} %slice.57), channel_id=1, source_target_pairs={{0,3},{1,0},{2,1},{3,2},{4,7},{5,4},{6,5},{7,6},{8,11},{9,8},{10,9... | collective-permute-start | bytes 786440 | tf_op jit(solution)/shard_map/ppermute | solution.py:135
  99.4 3.7 %collective-permute-start.17 = (bf16[8,64,576]{2,1,0:T(8,128)(2,1)S(1)}, bf16[8,64,576]{2,1,0:T(8,128)(2,1)S(1)}, u32[]{:S(2)}, u32[]{:S(2)}) collective-permute-start(bf16[8,64,576]{2,1,0:T(8,128)(2,1)S(1)} %get-tuple-element.24), channel_id=1, source_target_pairs={{0,4},{4,0},{8,12},{12,8},{16,20},{20,16},{24,28},{28,24},{32,36},... | collective-permute-start | bytes 1769480 | tf_op jit(solution)/shard_map/ppermute | solution.py:246
  99.7 20.2 %collective-permute-start.21 = (bf16[8,64,576]{2,1,0:T(8,128)(2,1)S(1)}, bf16[8,64,576]{2,1,0:T(8,128)(2,1)S(1)}, u32[]{:S(2)}, u32[]{:S(2)}) collective-permute-start(bf16[8,64,576]{2,1,0:T(8,128)(2,1)S(1)} %add_convert_fusion.1), channel_id=1, source_target_pairs={{0,192},{64,128},{1,193},{65,129},{2,194},{66,130},{3,195},{67,131... | collective-permute-start | bytes 1769480 | tf_op jit(solution)/shard_map/ppermute | solution.py:236
  101.0 19.0 %collective-permute-start.22 = (bf16[8,64,576]{2,1,0:T(8,128)(2,1)S(1)}, bf16[8,64,576]{2,1,0:T(8,128)(2,1)S(1)}, u32[]{:S(2)}, u32[]{:S(2)}) collective-permute-start(bf16[8,64,576]{2,1,0:T(8,128)(2,1)S(1)} %add_convert_fusion.1), channel_id=1, source_target_pairs={{128,192},{129,193},{130,194},{131,195},{132,196},{133,197},{134,1... | collective-permute-start | bytes 1769480 | tf_op jit(solution)/shard_map/ppermute | solution.py:237
  102.5 17.6 %collective-permute-start.25 = (bf16[8,64,576]{2,1,0:T(8,128)(2,1)S(1)}, bf16[8,64,576]{2,1,0:T(8,128)(2,1)S(1)}, u32[]{:S(2)}, u32[]{:S(2)}) collective-permute-start(bf16[8,64,576]{2,1,0:T(8,128)(2,1)S(1)} %add_convert_fusion), channel_id=1, source_target_pairs={{0,64},{1,65},{2,66},{3,67},{4,68},{5,69},{6,70},{7,71},{8,72},{9,... | collective-permute-start | bytes 1769480 | tf_op jit(solution)/shard_map/ppermute | solution.py:240
  120.5 14.2 %copy-start.2 = (f32[1,576]{1,0:T(1,128)S(1)}, f32[1,576]{1,0:T(1,128)}, u32[]{:S(2)}) copy-start(f32[1,576]{1,0:T(1,128)} %param.9) | copy-start | bytes 6916
  120.5 7.2 %collective-permute-start.30 = (bf16[64,576]{1,0:T(8,128)(2,1)S(1)}, bf16[64,576]{1,0:T(8,128)(2,1)S(1)}, u32[]{:S(2)}, u32[]{:S(2)}) collective-permute-start(bf16[64,576]{1,0:T(8,128)(2,1)S(1)} %get-tuple-element.36), channel_id=1, source_target_pairs={{0,56},{4,60},{8,0},{12,4},{16,8},{20,12},{24,16},{28,20},{32,24},... | collective-permute-start | bytes 221192 | tf_op jit(solution)/shard_map/ppermute | solution.py:251
  122.7 7.0 %collective-permute-start.27 = (bf16[2,64,576]{2,1,0:T(8,128)(2,1)S(1)}, bf16[2,64,576]{2,1,0:T(8,128)(2,1)S(1)}, u32[]{:S(2)}, u32[]{:S(2)}) collective-permute-start(bf16[2,64,576]{2,1,0:T(8,128)(2,1)S(1)} %pad_maximum_fusion), channel_id=1, source_target_pairs={{0,8},{4,12},{8,16},{12,20},{16,24},{20,28},{24,32},{28,36},{32,40... | collective-permute-start | bytes 442376 | tf_op jit(solution)/shard_map/ppermute | solution.py:250
  123.0 11.8 %collective-permute-start.26 = (bf16[64,576]{1,0:T(8,128)(2,1)S(1)}, bf16[64,576]{1,0:T(8,128)(2,1)S(1)}, u32[]{:S(2)}, u32[]{:S(2)}) collective-permute-start(bf16[64,576]{1,0:T(8,128)(2,1)S(1)} %get-tuple-element.35), channel_id=1, source_target_pairs={{0,40},{4,44},{8,48},{12,52},{16,56},{20,60},{24,0},{28,4},{32,8},... | collective-permute-start | bytes 221192 | tf_op jit(solution)/shard_map/ppermute | solution.py:252
  127.7 7.0 %collective-permute-start.31 = (bf16[64,576]{1,0:T(8,128)(2,1)S(1)}, bf16[64,576]{1,0:T(8,128)(2,1)S(1)}, u32[]{:S(2)}, u32[]{:S(2)}) collective-permute-start(bf16[64,576]{1,0:T(8,128)(2,1)S(1)} %fusion.1), channel_id=1, source_target_pairs={{0,56},{4,60},{8,0},{12,4},{16,8},{20,12},{24,16},{28,20},{32,24},... | collective-permute-start | bytes 221192 | tf_op jit(solution)/shard_map/ppermute | solution.py:255
  129.8 9.4 %collective-permute-start.28 = (bf16[64,576]{1,0:T(8,128)(2,1)S(1)}, bf16[64,576]{1,0:T(8,128)(2,1)S(1)}, u32[]{:S(2)}, u32[]{:S(2)}) collective-permute-start(bf16[64,576]{1,0:T(8,128)(2,1)S(1)} %get-tuple-element.33), channel_id=1, source_target_pairs={{0,24},{4,28},{8,32},{12,36},{16,40},{20,44},{24,48},{28,52},{32,5... | collective-permute-start | bytes 221192 | tf_op jit(solution)/shard_map/ppermute | solution.py:255
  131.2 8.0 %collective-permute-start.29 = (bf16[64,576]{1,0:T(8,128)(2,1)S(1)}, bf16[64,576]{1,0:T(8,128)(2,1)S(1)}, u32[]{:S(2)}, u32[]{:S(2)}) collective-permute-start(bf16[64,576]{1,0:T(8,128)(2,1)S(1)} %get-tuple-element.34), channel_id=1, source_target_pairs={{0,8},{4,12},{8,16},{12,20},{16,24},{20,28},{24,32},{28,36},{32,40... | collective-permute-start | bytes 221192 | tf_op jit(solution)/shard_map/ppermute | solution.py:255

commit v5 on v4

--- a/solution.py
+++ b/solution.py
@@ -46,7 +46,7 @@
     )(where, *in_vmem(vmem), *rest)
 
 
-def copy_weights(where, decoders, picks):
+def copy_weights(where, decoders, picks, least=(0, 0)):
     _, width, count = decoders.shape
     n = len(picks)
 
@@ -61,10 +61,13 @@
             for i, pick in enumerate(picks)
             for part in range(3)
         ]
-        for copy in copies:
-            copy.start()
-        for copy in copies:
-            copy.wait()
+        for step in ("start", "wait"):
+            for i, first in enumerate(least):
+
+                @pl.when(where_ref[4] >= first)
+                def _(i=i, step=step):
+                    for copy in copies[3 * i : 3 * i + 3]:
+                        getattr(copy, step)()
 
     out = [((width, count), decoders.dtype)] * n
     decoders = pltpu.with_memory_space_constraint(decoders, pltpu.HBM)
@@ -219,7 +222,7 @@
     where = jnp.stack([core, chip, row, jnp.where(sec == 2, 1, 0), sec, jnp.where(sec == 3, 1, 0), 2])
     where = where.astype(jnp.int32)
 
-    lent_a, lent_b = copy_weights(where, decoders, (3, 6))
+    lent_a, lent_b = copy_weights(where, decoders, (3, 6), (1, 3))
     lent_c = lax.ppermute(lent_a, "sec", [(1, 0)])
     lent_a = lax.ppermute(lent_a, "sec", [(2, 1), (3, 0)])
     lent_b = lax.ppermute(lent_b, "sec", [(3, 2)])

time: 142 us -> 141 us (level)
  no operation moved by 1% of the time
where the time goes in v5:
time: 141 us; the launch traced here: 139 us
  waiting for transfers between devices  73 us (52%)
  starting transfers between devices  46.6 us (33%)
  Pallas kernels  16.4 us (12%)
  other arithmetic  2.42 us (2%)
    ppermute x1, waiting for transfers between devices, per_device(): brought = lax.ppermute(features, 'sec', [(0, 2), (1, 3)])  21.1 us
    ppermute x1, waiting for transfers between devices, per_device(): back_a = lax.ppermute(pair, 'sec', [(0, 3), (1, 2)])  16.8 us
    pallas_call x9, Pallas kernels, call(): pl.pallas_call(kernel, in_specs=[SMEM] + [VMEM] * len(vmem) + [ANY] * len...  16.4 us
    ppermute x2, waiting for transfers between devices, gather_rows(): before = lax.ppermute(own, 'row', ring(1))  14.1 us
    ppermute x3, starting transfers between devices, per_device(): got.append(lax.ppermute(merged, 'feat', hop(shift)))  6.93 us
    ppermute x2, starting transfers between devices, gather_rows(): second = lax.ppermute(after_half, 'row', ring(-1))  4.85 us
    ppermute x1, starting transfers between devices, per_device(): got = [lax.ppermute(send[5], 'feat', hop(-3))]  4.71 us
    ppermute x2, starting transfers between devices, gather_rows(): after = lax.ppermute(own, 'row', ring(-1))  4.68 us
  transfers between devices with their start and end apart: 32, of which 12 were waited for; matrix products, arithmetic and copies ran while one was open for 0% of the time, Pallas kernels for 12%

profile of v5, /device:TPU:6, one launch (start us, length us, event | category | flops | bytes accessed | tf_op | source)
XLA Modules:
  0.0 139.0 jit_solution(1272133289894005664)
XLA Ops:
  0.0 1.5 %collective-permute-done = bf16[144,256]{1,0:T(8,128)(2,1)S(1)} collective-permute-done((bf16[144,256]{1,0:T(8,128)(2,1)}, bf16[144,256]{1,0:T(8,128)(2,1)S(1)}, u32[]{:S(2)}, u32[]{:S(2)}) %collective-permute-start) | collective-permute-done | bytes 73760 | tf_op jit(solution)/shard_map/ppermute | solution.py:111
  1.5 0.9 pad_maximum_fusion.1.refs_0_
  2.4 2.0 %collective-permute-start.1 = (bf16[288,256]{1,0:T(8,128)(2,1)S(1)}, bf16[288,256]{1,0:T(8,128)(2,1)S(1)}, u32[]{:S(2)}, u32[]{:S(2)}) collective-permute-start(bf16[288,256]{1,0:T(8,128)(2,1)S(1)} %pad_maximum_fusion.1.refs_0_), channel_id=1, source_target_pairs={{0,8},{4,60},{8,16},{12,4},{16,24},{20,12},{24,32},{28,20},{32,40}... | collective-permute-start | bytes 442376 | tf_op jit(solution)/shard_map/ppermute | solution.py:113
  4.4 3.3 %collective-permute-start.4 = (bf16[288,256]{1,0:T(8,128)(2,1)S(1)}, bf16[288,256]{1,0:T(8,128)(2,1)S(1)}, u32[]{:S(2)}, u32[]{:S(2)}) collective-permute-start(bf16[288,256]{1,0:T(8,128)(2,1)S(1)} %pad_maximum_fusion.1.refs_0_), channel_id=1, source_target_pairs={{0,16},{4,52},{8,24},{12,60},{16,32},{20,4},{24,40},{28,12},{32,48... | collective-permute-start | bytes 442376 | tf_op jit(solution)/shard_map/ppermute | solution.py:114
  7.6 3.8 %collective-permute-done.1.refs_1_ = bf16[288,256]{1,0:T(8,128)(2,1)S(1)} collective-permute-done((bf16[288,256]{1,0:T(8,128)(2,1)S(1)}, bf16[288,256]{1,0:T(8,128)(2,1)S(1)}, u32[]{:S(2)}, u32[]{:S(2)}) %collective-permute-start.1) | collective-permute-done | bytes 147488 | tf_op jit(solution)/shard_map/ppermute | solution.py:113
  11.4 0.0 collective-permute-start.2
  11.4 1.5 %collective-permute-start.6 = (bf16[288,256]{1,0:T(8,128)(2,1)S(1)}, bf16[288,256]{1,0:T(8,128)(2,1)S(1)}, u32[]{:S(2)}, u32[]{:S(2)}) collective-permute-start(bf16[288,256]{1,0:T(8,128)(2,1)S(1)} %collective-permute-done.1.refs_1_), channel_id=1, source_target_pairs={{0,4},{4,0},{8,12},{12,8},{16,20},{20,16},{24,28},{28,24},{32,36},... | collective-permute-start | bytes 442376 | tf_op jit(solution)/shard_map/ppermute | solution.py:117
  12.9 2.1 %collective-permute-done.4.refs_3_ = bf16[288,256]{1,0:T(8,128)(2,1)S(1)} collective-permute-done((bf16[288,256]{1,0:T(8,128)(2,1)S(1)}, bf16[288,256]{1,0:T(8,128)(2,1)S(1)}, u32[]{:S(2)}, u32[]{:S(2)}) %collective-permute-start.4) | collective-permute-done | bytes 147488 | tf_op jit(solution)/shard_map/ppermute | solution.py:114
  15.0 0.0 collective-permute-start.7
  15.0 2.1 %collective-permute-start.5 = (bf16[288,256]{1,0:T(8,128)(2,1)S(1)}, bf16[288,256]{1,0:T(8,128)(2,1)S(1)}, u32[]{:S(2)}, u32[]{:S(2)}) collective-permute-start(bf16[288,256]{1,0:T(8,128)(2,1)S(1)} %collective-permute-done.4.refs_3_), channel_id=1, source_target_pairs={{0,16},{4,52},{8,24},{12,60},{16,32},{20,4},{24,40},{28,12},{32,48... | collective-permute-start | bytes 442376 | tf_op jit(solution)/shard_map/ppermute | solution.py:116
  17.1 2.2 %collective-permute-done.2.refs_0_ = bf16[288,256]{1,0:T(8,128)(2,1)S(1)} collective-permute-done((bf16[288,256]{1,0:T(8,128)(2,1)S(1)}, bf16[288,256]{1,0:T(8,128)(2,1)S(1)}, u32[]{:S(2)}, u32[]{:S(2)}) %collective-permute-start.2) | collective-permute-done | bytes 147488 | tf_op jit(solution)/shard_map/ppermute | solution.py:115
  19.2 0.1 stack.30.where_ref
  19.3 2.5 %shard_map.61 = (bf16[576,1024]{1,0:T(8,128)(2,1)S(1)}, bf16[576,1024]{1,0:T(8,128)(2,1)S(1)}) custom-call(s32[7]{0:T(128)S(1)} %stack.30.where_ref, bf16[4,576,1024]{2,1,0:T(8,128)(2,1)} %bitcast.47), custom_call_target="tpu_custom_call" | custom-call | tf_op jit(solution)/shard_map/pallas_call | solution.py:38
  21.8 1.4 collective-permute-start.18
  23.2 0.0 collective-permute-done.6.refs_2_
  23.2 3.6 %collective-permute-start.19 = (bf16[576,1024]{1,0:T(8,128)(2,1)S(1)}, bf16[576,1024]{1,0:T(8,128)(2,1)S(1)}, u32[]{:S(2)}, u32[]{:S(2)}) collective-permute-start(bf16[576,1024]{1,0:T(8,128)(2,1)S(1)} %get-tuple-element.26), channel_id=1, source_target_pairs={{192,128},{193,129},{194,130},{195,131},{196,132},{197,133},{198,1... | collective-permute-start | bytes 3538952 | tf_op jit(solution)/shard_map/ppermute | solution.py:228
  26.8 0.0 copy-start.1
  26.8 1.6 %shard_map.55.refs_3_ = f32[256,1024]{1,0:T(8,128)S(1)} custom-call(s32[7]{0:T(128)S(1)} %stack.30.where_ref, bf16[2304,1024]{1,0:T(8,128)(2,1)S(1)} %bitcast.45, bf16[288,256]{1,0:T(8,128)(2,1)S(1)} %pad_maximum_fusion.1.refs_0_, bf16[288,256]{1,0:T(8,128)(2,1)S(1)} %collective-permute-done.1.refs_1_, bf16[288,256]{1,0:T(8,128)(2,1)S(1)} %collective-permute-done.6.refs_2_, ...), custom_call_target="tpu_custom_call" | custom-call | tf_op jit(solution)/shard_map/pallas_call | solution.py:38
  28.4 0.0 collective-permute-done.5.refs_2_
  28.4 1.3 shard_map.56.refs_0_
  29.7 1.7 %collective-permute-start.13 = (bf16[256,1024]{1,0:T(8,128)(2,1)S(1)}, bf16[256,1024]{1,0:T(8,128)(2,1)S(1)}, u32[]{:S(2)}, u32[]{:S(2)}) collective-permute-start(bf16[256,1024]{1,0:T(8,128)(2,1)S(1)} %shard_map.56.refs_0_), channel_id=1, source_target_pairs={{0,1},{1,2},{2,3},{3,0},{4,5},{5,6},{6,7},{7,4},{8,9},{9,10},{10,1... | collective-permute-start | bytes 1572872 | tf_op jit(solution)/shard_map/ppermute | solution.py:134
  31.4 0.7 collective-permute-start.23
  32.1 1.7 %collective-permute-start.14 = (bf16[256,1024]{1,0:T(8,128)(2,1)S(1)}, bf16[256,1024]{1,0:T(8,128)(2,1)S(1)}, u32[]{:S(2)}, u32[]{:S(2)}) collective-permute-start(bf16[256,1024]{1,0:T(8,128)(2,1)S(1)} %shard_map.56.refs_0_), channel_id=1, source_target_pairs={{0,3},{1,0},{2,1},{3,2},{4,7},{5,4},{6,5},{7,6},{8,11},{9,8},{10,9... | collective-permute-start | bytes 1572872 | tf_op jit(solution)/shard_map/ppermute | solution.py:135
  33.8 11.0 %collective-permute-done.13.refs_1_ = bf16[256,1024]{1,0:T(8,128)(2,1)S(1)} collective-permute-done((bf16[256,1024]{1,0:T(8,128)(2,1)S(1)}, bf16[256,1024]{1,0:T(8,128)(2,1)S(1)}, u32[]{:S(2)}, u32[]{:S(2)}) %collective-permute-start.13) | collective-permute-done | bytes 524320 | tf_op jit(solution)/shard_map/ppermute | solution.py:134
  44.9 1.3 collective-permute-start.8
  46.2 1.1 collective-permute-start.15
  47.3 21.1 %collective-permute-done.8.refs_0_ = bf16[256,1024]{1,0:T(8,128)(2,1)S(1)} collective-permute-done((bf16[256,1024]{1,0:T(8,128)(2,1)S(1)}, bf16[256,1024]{1,0:T(8,128)(2,1)S(1)}, u32[]{:S(2)}, u32[]{:S(2)}) %collective-permute-start.8) | collective-permute-done | bytes 524320 | tf_op jit(solution)/shard_map/ppermute | solution.py:233
  68.4 1.7 %collective-permute-start.16 = (bf16[128,1024]{1,0:T(8,128)(2,1)S(1)}, bf16[128,1024]{1,0:T(8,128)(2,1)S(1)}, u32[]{:S(2)}, u32[]{:S(2)}) collective-permute-start(bf16[128,1024]{1,0:T(8,128)(2,1)S(1)} %slice.59), channel_id=1, source_target_pairs={{0,3},{1,0},{2,1},{3,2},{4,7},{5,4},{6,5},{7,6},{8,11},{9,8},{10,9... | collective-permute-start | bytes 786440 | tf_op jit(solution)/shard_map/ppermute | solution.py:138
  70.1 0.0 collective-permute-done.18.refs_5_
  70.1 0.3 collective-permute-start.9
  70.4 3.0 %collective-permute-start.11 = (bf16[256,1024]{1,0:T(8,128)(2,1)S(1)}, bf16[256,1024]{1,0:T(8,128)(2,1)S(1)}, u32[]{:S(2)}, u32[]{:S(2)}) collective-permute-start(bf16[256,1024]{1,0:T(8,128)(2,1)S(1)} %collective-permute-done.8.refs_0_), channel_id=1, source_target_pairs={{0,3},{1,0},{2,1},{3,2},{4,7},{5,4},{6,5},{7,6},{8,11},{9,8},{10,9... | collective-permute-start | bytes 1572872 | tf_op jit(solution)/shard_map/ppermute | solution.py:135
  73.3 0.0 collective-permute-done.15.refs_3_
  73.3 4.2 %collective-permute-done.16.refs_4_ = bf16[128,1024]{1,0:T(8,128)(2,1)S(1)} collective-permute-done((bf16[128,1024]{1,0:T(8,128)(2,1)S(1)}, bf16[128,1024]{1,0:T(8,128)(2,1)S(1)}, u32[]{:S(2)}, u32[]{:S(2)}) %collective-permute-start.16) | collective-permute-done | bytes 262176 | tf_op jit(solution)/shard_map/ppermute | solution.py:138
  77.5 2.6 %shard_map.62 = (f32[8,64,576]{2,1,0:T(8,128)S(1)}, bf16[8,64,576]{2,1,0:T(8,128)(2,1)S(1)}) custom-call(s32[7]{0:T(128)S(1)} %stack.30.where_ref, bf16[256,1024]{1,0:T(8,128)(2,1)S(1)} %shard_map.56.refs_0_, bf16[256,1024]{1,0:T(8,128)(2,1)S(1)} %collective-permute-done.13.refs_1_, bf16[256,1024]{1,0:T(8,128)(2,1)S(1)} %collective-permute-done.14.refs_2_, ...), custom_call_target="tpu_custom_call" | custom-call | tf_op jit(solution)/shard_map/pallas_call | solution.py:38
  80.2 0.1 collective-permute-start.20
  80.3 0.6 shard_map.63
  80.8 0.7 collective-permute-start.24
  81.5 3.0 %collective-permute-done.9.refs_1_ = bf16[256,1024]{1,0:T(8,128)(2,1)S(1)} collective-permute-done((bf16[256,1024]{1,0:T(8,128)(2,1)S(1)}, bf16[256,1024]{1,0:T(8,128)(2,1)S(1)}, u32[]{:S(2)}, u32[]{:S(2)}) %collective-permute-start.9) | collective-permute-done | bytes 524320 | tf_op jit(solution)/shard_map/ppermute | solution.py:134
  84.6 0.1 collective-permute-start.10
  84.7 2.7 %collective-permute-done.11.refs_2_ = bf16[256,1024]{1,0:T(8,128)(2,1)S(1)} collective-permute-done((bf16[256,1024]{1,0:T(8,128)(2,1)S(1)}, bf16[256,1024]{1,0:T(8,128)(2,1)S(1)}, u32[]{:S(2)}, u32[]{:S(2)}) %collective-permute-start.11) | collective-permute-done | bytes 524320 | tf_op jit(solution)/shard_map/ppermute | solution.py:135
  87.5 3.1 %collective-permute-start.12 = (bf16[128,1024]{1,0:T(8,128)(2,1)S(1)}, bf16[128,1024]{1,0:T(8,128)(2,1)S(1)}, u32[]{:S(2)}, u32[]{:S(2)}) collective-permute-start(bf16[128,1024]{1,0:T(8,128)(2,1)S(1)} %slice.57), channel_id=1, source_target_pairs={{0,3},{1,0},{2,1},{3,2},{4,7},{5,4},{6,5},{7,6},{8,11},{9,8},{10,9... | collective-permute-start | bytes 786440 | tf_op jit(solution)/shard_map/ppermute | solution.py:138
  90.6 2.2 %shard_map.57 = (bf16[576,1024]{1,0:T(8,128)(2,1)S(1)}, bf16[576,1024]{1,0:T(8,128)(2,1)S(1)}) custom-call(s32[7]{0:T(128)S(1)} %stack.30.where_ref, bf16[4,576,1024]{2,1,0:T(8,128)(2,1)} %bitcast.48), custom_call_target="tpu_custom_call" | custom-call | tf_op jit(solution)/shard_map/pallas_call | solution.py:38
  92.8 2.5 %shard_map.58.refs_4_.start_ref = f32[4,256,576]{2,1,0:T(8,128)S(1)} custom-call(s32[7]{0:T(128)S(1)} %stack.30.where_ref, bf16[256,1024]{1,0:T(8,128)(2,1)S(1)} %shard_map.56.refs_0_, bf16[256,1024]{1,0:T(8,128)(2,1)S(1)} %collective-permute-done.13.refs_1_, bf16[256,1024]{1,0:T(8,128)(2,1)S(1)} %collective-permute-done.14.refs_2_, ...), custom_call_target="tpu_custom_call" | custom-call | tf_op jit(solution)/shard_map/pallas_call | solution.py:38
  95.3 2.1 %shard_map.59 = (f32[8,64,576]{2,1,0:T(8,128)S(1)}, bf16[8,64,576]{2,1,0:T(8,128)(2,1)S(1)}, bf16[1024,576]{1,0:T(8,128)(2,1)S(1)}) custom-call(s32[7]{0:T(128)S(1)} %stack.30.where_ref, bf16[256,1024]{1,0:T(8,128)(2,1)S(1)} %collective-permute-done.8.refs_0_, bf16[256,1024]{1,0:T(8,128)(2,1)S(1)} %collective-permute-done.9.refs_1_, ...), custom_call_target="tpu_custom_call" | custom-call | tf_op jit(solution)/shard_map/pallas_call | solution.py:38
  97.3 0.0 collective-permute-done.10.first
  97.4 1.1 shard_map.60
  98.5 0.1 collective-permute-start.17
  98.6 0.1 add_convert_fusion.1
  98.8 1.3 collective-permute-start.21
  100.1 1.3 collective-permute-start.22
  101.4 0.1 add_convert_fusion
  101.5 0.7 collective-permute-start.25
  102.2 16.8 %collective-permute-done.21 = bf16[8,64,576]{2,1,0:T(8,128)(2,1)S(1)} collective-permute-done((bf16[8,64,576]{2,1,0:T(8,128)(2,1)S(1)}, bf16[8,64,576]{2,1,0:T(8,128)(2,1)S(1)}, u32[]{:S(2)}, u32[]{:S(2)}) %collective-permute-start.21) | collective-permute-done | bytes 589856 | tf_op jit(solution)/shard_map/ppermute | solution.py:239
  119.0 0.1 collective-permute-done.22
  119.1 0.5 fusion.13
  119.5 0.0 copy-start.2
  119.6 2.1 %collective-permute-start.30 = (bf16[64,576]{1,0:T(8,128)(2,1)S(1)}, bf16[64,576]{1,0:T(8,128)(2,1)S(1)}, u32[]{:S(2)}, u32[]{:S(2)}) collective-permute-start(bf16[64,576]{1,0:T(8,128)(2,1)S(1)} %get-tuple-element.36), channel_id=1, source_target_pairs={{0,56},{4,60},{8,0},{12,4},{16,8},{20,12},{24,16},{28,20},{32,24},... | collective-permute-start | bytes 221192 | tf_op jit(solution)/shard_map/ppermute | solution.py:254
  121.8 0.3 collective-permute-start.27
  122.0 4.7 %collective-permute-start.26 = (bf16[64,576]{1,0:T(8,128)(2,1)S(1)}, bf16[64,576]{1,0:T(8,128)(2,1)S(1)}, u32[]{:S(2)}, u32[]{:S(2)}) collective-permute-start(bf16[64,576]{1,0:T(8,128)(2,1)S(1)} %get-tuple-element.35), channel_id=1, source_target_pairs={{0,40},{4,44},{8,48},{12,52},{16,56},{20,60},{24,0},{28,4},{32,8},... | collective-permute-start | bytes 221192 | tf_op jit(solution)/shard_map/ppermute | solution.py:255
  126.8 2.0 %collective-permute-start.31 = (bf16[64,576]{1,0:T(8,128)(2,1)S(1)}, bf16[64,576]{1,0:T(8,128)(2,1)S(1)}, u32[]{:S(2)}, u32[]{:S(2)}) collective-permute-start(bf16[64,576]{1,0:T(8,128)(2,1)S(1)} %fusion.1), channel_id=1, source_target_pairs={{0,56},{4,60},{8,0},{12,4},{16,8},{20,12},{24,16},{28,20},{32,24},... | collective-permute-start | bytes 221192 | tf_op jit(solution)/shard_map/ppermute | solution.py:258
  128.8 1.4 %collective-permute-start.28 = (bf16[64,576]{1,0:T(8,128)(2,1)S(1)}, bf16[64,576]{1,0:T(8,128)(2,1)S(1)}, u32[]{:S(2)}, u32[]{:S(2)}) collective-permute-start(bf16[64,576]{1,0:T(8,128)(2,1)S(1)} %get-tuple-element.33), channel_id=1, source_target_pairs={{0,24},{4,28},{8,32},{12,36},{16,40},{20,44},{24,48},{28,52},{32,5... | collective-permute-start | bytes 221192 | tf_op jit(solution)/shard_map/ppermute | solution.py:258
  130.3 3.5 %collective-permute-start.29 = (bf16[64,576]{1,0:T(8,128)(2,1)S(1)}, bf16[64,576]{1,0:T(8,128)(2,1)S(1)}, u32[]{:S(2)}, u32[]{:S(2)}) collective-permute-start(bf16[64,576]{1,0:T(8,128)(2,1)S(1)} %get-tuple-element.34), channel_id=1, source_target_pairs={{0,8},{4,12},{8,16},{12,20},{16,24},{20,28},{24,32},{28,36},{32,40... | collective-permute-start | bytes 221192 | tf_op jit(solution)/shard_map/ppermute | solution.py:258
  133.8 4.5 %collective-permute-done.28 = bf16[64,576]{1,0:T(8,128)(2,1)S(1)} collective-permute-done((bf16[64,576]{1,0:T(8,128)(2,1)S(1)}, bf16[64,576]{1,0:T(8,128)(2,1)S(1)}, u32[]{:S(2)}, u32[]{:S(2)}) %collective-permute-start.28) | collective-permute-done | bytes 73760 | tf_op jit(solution)/shard_map/ppermute | solution.py:258
  138.3 0.7 fusion.10
  (30 shorter events, 0.3 us)
Async XLA Ops:
  0.0 1.5 %collective-permute-start = (bf16[144,256]{1,0:T(8,128)(2,1)}, bf16[144,256]{1,0:T(8,128)(2,1)S(1)}, u32[]{:S(2)}, u32[]{:S(2)}) collective-permute-start(bf16[144,256]{1,0:T(8,128)(2,1)} %bitcast.49), channel_id=1, source_target_pairs={{0,4},{4,0},{8,12},{12,8},{16,20},{20,16},{24,28},{28,24},{32,36},... | collective-permute-start | bytes 221192 | tf_op jit(solution)/shard_map/ppermute | solution.py:111
  2.4 9.1 %collective-permute-start.1 = (bf16[288,256]{1,0:T(8,128)(2,1)S(1)}, bf16[288,256]{1,0:T(8,128)(2,1)S(1)}, u32[]{:S(2)}, u32[]{:S(2)}) collective-permute-start(bf16[288,256]{1,0:T(8,128)(2,1)S(1)} %pad_maximum_fusion.1.refs_0_), channel_id=1, source_target_pairs={{0,8},{4,60},{8,16},{12,4},{16,24},{20,12},{24,32},{28,20},{32,40}... | collective-permute-start | bytes 442376 | tf_op jit(solution)/shard_map/ppermute | solution.py:113
  4.4 10.6 %collective-permute-start.4 = (bf16[288,256]{1,0:T(8,128)(2,1)S(1)}, bf16[288,256]{1,0:T(8,128)(2,1)S(1)}, u32[]{:S(2)}, u32[]{:S(2)}) collective-permute-start(bf16[288,256]{1,0:T(8,128)(2,1)S(1)} %pad_maximum_fusion.1.refs_0_), channel_id=1, source_target_pairs={{0,16},{4,52},{8,24},{12,60},{16,32},{20,4},{24,40},{28,12},{32,48... | collective-permute-start | bytes 442376 | tf_op jit(solution)/shard_map/ppermute | solution.py:114
  11.4 7.8 %collective-permute-start.2 = (bf16[288,256]{1,0:T(8,128)(2,1)S(1)}, bf16[288,256]{1,0:T(8,128)(2,1)S(1)}, u32[]{:S(2)}, u32[]{:S(2)}) collective-permute-start(bf16[288,256]{1,0:T(8,128)(2,1)S(1)} %collective-permute-done.1.refs_1_), channel_id=1, source_target_pairs={{0,16},{4,52},{8,24},{12,60},{16,32},{20,4},{24,40},{28,12},{32,48... | collective-permute-start | bytes 442376 | tf_op jit(solution)/shard_map/ppermute | solution.py:115
  11.4 11.7 %collective-permute-start.6 = (bf16[288,256]{1,0:T(8,128)(2,1)S(1)}, bf16[288,256]{1,0:T(8,128)(2,1)S(1)}, u32[]{:S(2)}, u32[]{:S(2)}) collective-permute-start(bf16[288,256]{1,0:T(8,128)(2,1)S(1)} %collective-permute-done.1.refs_1_), channel_id=1, source_target_pairs={{0,4},{4,0},{8,12},{12,8},{16,20},{20,16},{24,28},{28,24},{32,36},... | collective-permute-start | bytes 442376 | tf_op jit(solution)/shard_map/ppermute | solution.py:117
  15.0 11.8 %collective-permute-start.7 = (bf16[288,256]{1,0:T(8,128)(2,1)S(1)}, bf16[288,256]{1,0:T(8,128)(2,1)S(1)}, u32[]{:S(2)}, u32[]{:S(2)}) collective-permute-start(bf16[288,256]{1,0:T(8,128)(2,1)S(1)} %collective-permute-done.4.refs_3_), channel_id=1, source_target_pairs={{0,4},{4,0},{8,12},{12,8},{16,20},{20,16},{24,28},{28,24},{32,36},... | collective-permute-start | bytes 442376 | tf_op jit(solution)/shard_map/ppermute | solution.py:118
  15.0 13.4 %collective-permute-start.5 = (bf16[288,256]{1,0:T(8,128)(2,1)S(1)}, bf16[288,256]{1,0:T(8,128)(2,1)S(1)}, u32[]{:S(2)}, u32[]{:S(2)}) collective-permute-start(bf16[288,256]{1,0:T(8,128)(2,1)S(1)} %collective-permute-done.4.refs_3_), channel_id=1, source_target_pairs={{0,16},{4,52},{8,24},{12,60},{16,32},{20,4},{24,40},{28,12},{32,48... | collective-permute-start | bytes 442376 | tf_op jit(solution)/shard_map/ppermute | solution.py:116
  19.2 9.2 %collective-permute-start.3 = (bf16[288,256]{1,0:T(8,128)(2,1)S(1)}, bf16[288,256]{1,0:T(8,128)(2,1)S(1)}, u32[]{:S(2)}, u32[]{:S(2)}) collective-permute-start(bf16[288,256]{1,0:T(8,128)(2,1)S(1)} %collective-permute-done.2.refs_0_), channel_id=1, source_target_pairs={{0,4},{4,0},{8,12},{12,8},{16,20},{20,16},{24,28},{28,24},{32,36},... | collective-permute-start | bytes 442376 | tf_op jit(solution)/shard_map/ppermute | solution.py:119
  19.3 7.5 %copy-start = (bf16[1,2304,1024]{2,1,0:T(8,128)(2,1)S(1)}, bf16[1,2304,1024]{2,1,0:T(8,128)(2,1)}, u32[]{:S(2)}) copy-start(bf16[1,2304,1024]{2,1,0:T(8,128)(2,1)} %param.6) | copy-start | bytes 14155780
  21.8 48.3 %collective-permute-start.18 = (bf16[576,1024]{1,0:T(8,128)(2,1)S(1)}, bf16[576,1024]{1,0:T(8,128)(2,1)S(1)}, u32[]{:S(2)}, u32[]{:S(2)}) collective-permute-start(bf16[576,1024]{1,0:T(8,128)(2,1)S(1)} %get-tuple-element.25), channel_id=1, source_target_pairs={{128,64},{192,0},{129,65},{193,1},{130,66},{194,2},{131,67},{195,3... | collective-permute-start | bytes 3538952 | tf_op jit(solution)/shard_map/ppermute | solution.py:227
  23.2 47.2 %collective-permute-start.19 = (bf16[576,1024]{1,0:T(8,128)(2,1)S(1)}, bf16[576,1024]{1,0:T(8,128)(2,1)S(1)}, u32[]{:S(2)}, u32[]{:S(2)}) collective-permute-start(bf16[576,1024]{1,0:T(8,128)(2,1)S(1)} %get-tuple-element.26), channel_id=1, source_target_pairs={{192,128},{193,129},{194,130},{195,131},{196,132},{197,133},{198,1... | collective-permute-start | bytes 3538952 | tf_op jit(solution)/shard_map/ppermute | solution.py:228
  26.8 1.6 %copy-start.1 = (f32[1,1024]{1,0:T(1,128)S(1)}, f32[1,1024]{1,0:T(1,128)}, u32[]{:S(2)}) copy-start(f32[1,1024]{1,0:T(1,128)} %refs_4_.1) | copy-start | bytes 12292
  29.7 15.1 %collective-permute-start.13 = (bf16[256,1024]{1,0:T(8,128)(2,1)S(1)}, bf16[256,1024]{1,0:T(8,128)(2,1)S(1)}, u32[]{:S(2)}, u32[]{:S(2)}) collective-permute-start(bf16[256,1024]{1,0:T(8,128)(2,1)S(1)} %shard_map.56.refs_0_), channel_id=1, source_target_pairs={{0,1},{1,2},{2,3},{3,0},{4,5},{5,6},{6,7},{7,4},{8,9},{9,10},{10,1... | collective-permute-start | bytes 1572872 | tf_op jit(solution)/shard_map/ppermute | solution.py:134
  31.4 48.9 %collective-permute-start.23 = (bf16[576,1024]{1,0:T(8,128)(2,1)S(1)}, bf16[576,1024]{1,0:T(8,128)(2,1)S(1)}, u32[]{:S(2)}, u32[]{:S(2)}) collective-permute-start(bf16[576,1024]{1,0:T(8,128)(2,1)S(1)} %get-tuple-element.25), channel_id=1, source_target_pairs={{64,0},{65,1},{66,2},{67,3},{68,4},{69,5},{70,6},{71,7},{72,8},{73... | collective-permute-start | bytes 3538952 | tf_op jit(solution)/shard_map/ppermute | solution.py:226
  32.1 14.1 %collective-permute-start.14 = (bf16[256,1024]{1,0:T(8,128)(2,1)S(1)}, bf16[256,1024]{1,0:T(8,128)(2,1)S(1)}, u32[]{:S(2)}, u32[]{:S(2)}) collective-permute-start(bf16[256,1024]{1,0:T(8,128)(2,1)S(1)} %shard_map.56.refs_0_), channel_id=1, source_target_pairs={{0,3},{1,0},{2,1},{3,2},{4,7},{5,4},{6,5},{7,6},{8,11},{9,8},{10,9... | collective-permute-start | bytes 1572872 | tf_op jit(solution)/shard_map/ppermute | solution.py:135
  44.9 23.5 %collective-permute-start.8 = (bf16[256,1024]{1,0:T(8,128)(2,1)S(1)}, bf16[256,1024]{1,0:T(8,128)(2,1)S(1)}, u32[]{:S(2)}, u32[]{:S(2)}) collective-permute-start(bf16[256,1024]{1,0:T(8,128)(2,1)S(1)} %shard_map.56.refs_0_), channel_id=1, source_target_pairs={{0,128},{64,192},{1,129},{65,193},{2,130},{66,194},{3,131},{67,195... | collective-permute-start | bytes 1572872 | tf_op jit(solution)/shard_map/ppermute | solution.py:233
  46.2 27.2 %collective-permute-start.15 = (bf16[128,1024]{1,0:T(8,128)(2,1)S(1)}, bf16[128,1024]{1,0:T(8,128)(2,1)S(1)}, u32[]{:S(2)}, u32[]{:S(2)}) collective-permute-start(bf16[128,1024]{1,0:T(8,128)(2,1)S(1)} %slice.58), channel_id=1, source_target_pairs={{0,1},{1,2},{2,3},{3,0},{4,5},{5,6},{6,7},{7,4},{8,9},{9,10},{10,1... | collective-permute-start | bytes 786440 | tf_op jit(solution)/shard_map/ppermute | solution.py:137
  68.4 9.2 %collective-permute-start.16 = (bf16[128,1024]{1,0:T(8,128)(2,1)S(1)}, bf16[128,1024]{1,0:T(8,128)(2,1)S(1)}, u32[]{:S(2)}, u32[]{:S(2)}) collective-permute-start(bf16[128,1024]{1,0:T(8,128)(2,1)S(1)} %slice.59), channel_id=1, source_target_pairs={{0,3},{1,0},{2,1},{3,2},{4,7},{5,4},{6,5},{7,6},{8,11},{9,8},{10,9... | collective-permute-start | bytes 786440 | tf_op jit(solution)/shard_map/ppermute | solution.py:138
  70.1 14.5 %collective-permute-start.9 = (bf16[256,1024]{1,0:T(8,128)(2,1)S(1)}, bf16[256,1024]{1,0:T(8,128)(2,1)S(1)}, u32[]{:S(2)}, u32[]{:S(2)}) collective-permute-start(bf16[256,1024]{1,0:T(8,128)(2,1)S(1)} %collective-permute-done.8.refs_0_), channel_id=1, source_target_pairs={{0,1},{1,2},{2,3},{3,0},{4,5},{5,6},{6,7},{7,4},{8,9},{9,10},{10,1... | collective-permute-start | bytes 1572872 | tf_op jit(solution)/shard_map/ppermute | solution.py:134
  70.4 17.1 %collective-permute-start.11 = (bf16[256,1024]{1,0:T(8,128)(2,1)S(1)}, bf16[256,1024]{1,0:T(8,128)(2,1)S(1)}, u32[]{:S(2)}, u32[]{:S(2)}) collective-permute-start(bf16[256,1024]{1,0:T(8,128)(2,1)S(1)} %collective-permute-done.8.refs_0_), channel_id=1, source_target_pairs={{0,3},{1,0},{2,1},{3,2},{4,7},{5,4},{6,5},{7,6},{8,11},{9,8},{10,9... | collective-permute-start | bytes 1572872 | tf_op jit(solution)/shard_map/ppermute | solution.py:135
  80.2 18.4 %collective-permute-start.20 = (bf16[8,64,576]{2,1,0:T(8,128)(2,1)S(1)}, bf16[8,64,576]{2,1,0:T(8,128)(2,1)S(1)}, u32[]{:S(2)}, u32[]{:S(2)}) collective-permute-start(bf16[8,64,576]{2,1,0:T(8,128)(2,1)S(1)} %get-tuple-element.28), channel_id=1, source_target_pairs={{0,4},{4,0},{8,12},{12,8},{16,20},{20,16},{24,28},{28,24},{32,36},... | collective-permute-start | bytes 1769480 | tf_op jit(solution)/shard_map/ppermute | solution.py:237
  80.8 20.5 %collective-permute-start.24 = (bf16[8,64,576]{2,1,0:T(8,128)(2,1)S(1)}, bf16[8,64,576]{2,1,0:T(8,128)(2,1)S(1)}, u32[]{:S(2)}, u32[]{:S(2)}) collective-permute-start(bf16[8,64,576]{2,1,0:T(8,128)(2,1)S(1)} %get-tuple-element.30), channel_id=1, source_target_pairs={{0,4},{4,0},{8,12},{12,8},{16,20},{20,16},{24,28},{28,24},{32,36},... | collective-permute-start | bytes 1769480 | tf_op jit(solution)/shard_map/ppermute | solution.py:242
  84.6 12.7 %collective-permute-start.10 = (bf16[128,1024]{1,0:T(8,128)(2,1)S(1)}, bf16[128,1024]{1,0:T(8,128)(2,1)S(1)}, u32[]{:S(2)}, u32[]{:S(2)}) collective-permute-start(bf16[128,1024]{1,0:T(8,128)(2,1)S(1)} %slice.56), channel_id=1, source_target_pairs={{0,1},{1,2},{2,3},{3,0},{4,5},{5,6},{6,7},{7,4},{8,9},{9,10},{10,1... | collective-permute-start | bytes 786440 | tf_op jit(solution)/shard_map/ppermute | solution.py:137
  87.5 9.9 %collective-permute-start.12 = (bf16[128,1024]{1,0:T(8,128)(2,1)S(1)}, bf16[128,1024]{1,0:T(8,128)(2,1)S(1)}, u32[]{:S(2)}, u32[]{:S(2)}) collective-permute-start(bf16[128,1024]{1,0:T(8,128)(2,1)S(1)} %slice.57), channel_id=1, source_target_pairs={{0,3},{1,0},{2,1},{3,2},{4,7},{5,4},{6,5},{7,6},{8,11},{9,8},{10,9... | collective-permute-start | bytes 786440 | tf_op jit(solution)/shard_map/ppermute | solution.py:138
  98.5 3.7 %collective-permute-start.17 = (bf16[8,64,576]{2,1,0:T(8,128)(2,1)S(1)}, bf16[8,64,576]{2,1,0:T(8,128)(2,1)S(1)}, u32[]{:S(2)}, u32[]{:S(2)}) collective-permute-start(bf16[8,64,576]{2,1,0:T(8,128)(2,1)S(1)} %get-tuple-element.24), channel_id=1, source_target_pairs={{0,4},{4,0},{8,12},{12,8},{16,20},{20,16},{24,28},{28,24},{32,36},... | collective-permute-start | bytes 1769480 | tf_op jit(solution)/shard_map/ppermute | solution.py:249
  98.8 20.2 %collective-permute-start.21 = (bf16[8,64,576]{2,1,0:T(8,128)(2,1)S(1)}, bf16[8,64,576]{2,1,0:T(8,128)(2,1)S(1)}, u32[]{:S(2)}, u32[]{:S(2)}) collective-permute-start(bf16[8,64,576]{2,1,0:T(8,128)(2,1)S(1)} %add_convert_fusion.1), channel_id=1, source_target_pairs={{0,192},{64,128},{1,193},{65,129},{2,194},{66,130},{3,195},{67,131... | collective-permute-start | bytes 1769480 | tf_op jit(solution)/shard_map/ppermute | solution.py:239
  100.1 19.0 %collective-permute-start.22 = (bf16[8,64,576]{2,1,0:T(8,128)(2,1)S(1)}, bf16[8,64,576]{2,1,0:T(8,128)(2,1)S(1)}, u32[]{:S(2)}, u32[]{:S(2)}) collective-permute-start(bf16[8,64,576]{2,1,0:T(8,128)(2,1)S(1)} %add_convert_fusion.1), channel_id=1, source_target_pairs={{128,192},{129,193},{130,194},{131,195},{132,196},{133,197},{134,1... | collective-permute-start | bytes 1769480 | tf_op jit(solution)/shard_map/ppermute | solution.py:240
  101.5 17.6 %collective-permute-start.25 = (bf16[8,64,576]{2,1,0:T(8,128)(2,1)S(1)}, bf16[8,64,576]{2,1,0:T(8,128)(2,1)S(1)}, u32[]{:S(2)}, u32[]{:S(2)}) collective-permute-start(bf16[8,64,576]{2,1,0:T(8,128)(2,1)S(1)} %add_convert_fusion), channel_id=1, source_target_pairs={{0,64},{1,65},{2,66},{3,67},{4,68},{5,69},{6,70},{7,71},{8,72},{9,... | collective-permute-start | bytes 1769480 | tf_op jit(solution)/shard_map/ppermute | solution.py:243
  119.5 14.2 %copy-start.2 = (f32[1,576]{1,0:T(1,128)S(1)}, f32[1,576]{1,0:T(1,128)}, u32[]{:S(2)}) copy-start(f32[1,576]{1,0:T(1,128)} %param.9) | copy-start | bytes 6916
  119.6 7.1 %collective-permute-start.30 = (bf16[64,576]{1,0:T(8,128)(2,1)S(1)}, bf16[64,576]{1,0:T(8,128)(2,1)S(1)}, u32[]{:S(2)}, u32[]{:S(2)}) collective-permute-start(bf16[64,576]{1,0:T(8,128)(2,1)S(1)} %get-tuple-element.36), channel_id=1, source_target_pairs={{0,56},{4,60},{8,0},{12,4},{16,8},{20,12},{24,16},{28,20},{32,24},... | collective-permute-start | bytes 221192 | tf_op jit(solution)/shard_map/ppermute | solution.py:254
  121.8 7.0 %collective-permute-start.27 = (bf16[2,64,576]{2,1,0:T(8,128)(2,1)S(1)}, bf16[2,64,576]{2,1,0:T(8,128)(2,1)S(1)}, u32[]{:S(2)}, u32[]{:S(2)}) collective-permute-start(bf16[2,64,576]{2,1,0:T(8,128)(2,1)S(1)} %pad_maximum_fusion), channel_id=1, source_target_pairs={{0,8},{4,12},{8,16},{12,20},{16,24},{20,28},{24,32},{28,36},{32,40... | collective-permute-start | bytes 442376 | tf_op jit(solution)/shard_map/ppermute | solution.py:253
  122.0 11.7 %collective-permute-start.26 = (bf16[64,576]{1,0:T(8,128)(2,1)S(1)}, bf16[64,576]{1,0:T(8,128)(2,1)S(1)}, u32[]{:S(2)}, u32[]{:S(2)}) collective-permute-start(bf16[64,576]{1,0:T(8,128)(2,1)S(1)} %get-tuple-element.35), channel_id=1, source_target_pairs={{0,40},{4,44},{8,48},{12,52},{16,56},{20,60},{24,0},{28,4},{32,8},... | collective-permute-start | bytes 221192 | tf_op jit(solution)/shard_map/ppermute | solution.py:255
  126.8 7.0 %collective-permute-start.31 = (bf16[64,576]{1,0:T(8,128)(2,1)S(1)}, bf16[64,576]{1,0:T(8,128)(2,1)S(1)}, u32[]{:S(2)}, u32[]{:S(2)}) collective-permute-start(bf16[64,576]{1,0:T(8,128)(2,1)S(1)} %fusion.1), channel_id=1, source_target_pairs={{0,56},{4,60},{8,0},{12,4},{16,8},{20,12},{24,16},{28,20},{32,24},... | collective-permute-start | bytes 221192 | tf_op jit(solution)/shard_map/ppermute | solution.py:258
  128.8 9.4 %collective-permute-start.28 = (bf16[64,576]{1,0:T(8,128)(2,1)S(1)}, bf16[64,576]{1,0:T(8,128)(2,1)S(1)}, u32[]{:S(2)}, u32[]{:S(2)}) collective-permute-start(bf16[64,576]{1,0:T(8,128)(2,1)S(1)} %get-tuple-element.33), channel_id=1, source_target_pairs={{0,24},{4,28},{8,32},{12,36},{16,40},{20,44},{24,48},{28,52},{32,5... | collective-permute-start | bytes 221192 | tf_op jit(solution)/shard_map/ppermute | solution.py:258
  130.3 8.0 %collective-permute-start.29 = (bf16[64,576]{1,0:T(8,128)(2,1)S(1)}, bf16[64,576]{1,0:T(8,128)(2,1)S(1)}, u32[]{:S(2)}, u32[]{:S(2)}) collective-permute-start(bf16[64,576]{1,0:T(8,128)(2,1)S(1)} %get-tuple-element.34), channel_id=1, source_target_pairs={{0,8},{4,12},{8,16},{12,20},{16,24},{20,28},{24,32},{28,36},{32,40... | collective-permute-start | bytes 221192 | tf_op jit(solution)/shard_map/ppermute | solution.py:258
